TPU v7x, 32 devices: a whole 2x2x4 slice. The times are simulated.
32 devices in a mesh: fsdp: 8 (over z, y), ctx: 2 (over x), tp: 2 (over core).
Axes of the slice: x: 2, y: 2, z: 4, core: 2. Of those that a mesh axis runs over, the one named last changes fastest.
Arguments:
- hidden_in: bfloat16 [8, 1024, 2048], P('fsdp', 'ctx'), may hold values from -6 to 6
- segments: int32 [8, 1024], P('fsdp'), may hold values from 0 to 7, never falling along the last dimension, each value on 1 to 512 neighbouring positions
- gain_attn: float32 [2048], P(('fsdp', 'ctx')), may hold values from 0.5 to 1.5
- query_weight: bfloat16 [2048, 2048], P(('fsdp', 'ctx'), 'tp'), may hold values from -0.5 to 0.5
- key_weight: bfloat16 [2048, 512], P(('fsdp', 'ctx'), 'tp'), may hold values from -0.5 to 0.5
- value_weight: bfloat16 [2048, 512], P(('fsdp', 'ctx'), 'tp'), may hold values from -0.125 to 0.125
- out_weight: bfloat16 [2048, 2048], P(('fsdp', 'ctx'), 'tp'), may hold values from -2 to 2
- gain_ffn: float32 [2048], P(('fsdp', 'ctx')), may hold values from 0.5 to 1.5
- gate_weight: bfloat16 [2048, 8192], P(('fsdp', 'ctx'), 'tp'), may hold values from -0.125 to 0.125
- up_weight: bfloat16 [2048, 8192], P(('fsdp', 'ctx'), 'tp'), may hold values from -0.125 to 0.125
- down_weight: bfloat16 [2048, 8192], P(('fsdp', 'ctx'), 'tp'), may hold values from -0.375 to 0.375
- cotangent: bfloat16 [8, 1024, 2048], P('fsdp', 'ctx'), may hold values from -6 to 6
Outputs:
- layer_out: bfloat16 [8, 1024, 2048], P('fsdp', 'ctx')
- input_grad: float32 [8, 1024, 2048], P('fsdp', 'ctx')
- grad_gain_attn: float32 [2048], P(('fsdp', 'ctx'))
- grad_query: float32 [2048, 2048], P(('fsdp', 'ctx'), 'tp')
- grad_key: float32 [2048, 512], P(('fsdp', 'ctx'), 'tp')
- grad_value: float32 [2048, 512], P(('fsdp', 'ctx'), 'tp')
- grad_out: float32 [2048, 2048], P(('fsdp', 'ctx'), 'tp')
- grad_gain_ffn: float32 [2048], P(('fsdp', 'ctx'))
- grad_gate: float32 [2048, 8192], P(('fsdp', 'ctx'), 'tp')
- grad_up: float32 [2048, 8192], P(('fsdp', 'ctx'), 'tp')
- grad_down: float32 [2048, 8192], P(('fsdp', 'ctx'), 'tp')
Inputs may be any that keep to these rules, and one draw needn't show every extreme that they name: `segments`: in each sequence the ids start at 0 and never fall; each of the 8 ids covers 1 to 512 consecutive tokens, and one document of each sequence has exactly 512.
All inputs are finite; a program needn't handle non-finite values.
Results may differ from a plain program's by a relative error of at most 0.038.
Values may be sent and summed in bfloat16 or wider, within the bound.
No kernel may reach another device: no remote copies, remote signals or barrier semaphores. Data moves between devices by JAX's collectives and lax.ppermute only.
A program may use at most 320 MiB of HBM per device.

v0:
```python
import jax
import jax.numpy as jnp
from jax import lax
from jax.sharding import PartitionSpec as P

HQ = 32
KVH = 8
HD = 64


EPSILON = 1e-05
SCALE = 0.015625
RESIDUAL = 0.22
THETA = 10000000.0


def rotate_pairs(values, cosine, sine):
    half = values.shape[-1] // 2
    swapped = jnp.concatenate([-values[..., half:], values[..., :half]], axis=-1)
    return values * cosine + swapped * sine


def matmul_low(left, right):
    return jnp.dot(left, right, preferred_element_type=jnp.float32)


def matmul_trans(left, right):
    return lax.dot_general(
        left, right, (((1,), (1,)), ((), ())), preferred_element_type=jnp.float32
    )


def matmul_outer(left, right):
    return lax.dot_general(
        left, right, (((0,), (0,)), ((), ())), preferred_element_type=jnp.float32
    )


def norm_back(grad_normed, gain, unit_rows, inv_rms):
    scaled = grad_normed * gain
    return inv_rms * (scaled - unit_rows * jnp.mean(scaled * unit_rows, axis=-1, keepdims=True))


def shards(
    hidden_in,
    segments,
    gain_attn,
    query_weight,
    key_weight,
    value_weight,
    out_weight,
    gain_ffn,
    gate_weight,
    up_weight,
    down_weight,
    cotangent,
):
    seqs_here, rows_here, width = hidden_in.shape
    length = segments.shape[1]
    tokens = seqs_here * rows_here
    kv_local = key_weight.shape[1] // HD
    group_size = HQ // KVH
    head_cols = kv_local * group_size * HD
    bfloat = jnp.bfloat16
    first_row = lax.axis_index("ctx") * rows_here
    own_seg = lax.dynamic_slice_in_dim(segments, first_row, rows_here, 1)
    before = jnp.sum((segments[:, None, :] < own_seg[:, :, None]).astype(jnp.int32), axis=2)
    own_place = first_row + jnp.arange(rows_here, dtype=jnp.int32)
    places = (own_place[None, :] - before).astype(jnp.float32)
    freqs = THETA ** (-jnp.arange(0, HD, 2, dtype=jnp.float32) / HD)
    phase = places[:, :, None] * freqs
    phase = jnp.concatenate([phase, phase], axis=-1)
    cosine = jnp.cos(phase)
    sine = jnp.sin(phase)
    key_place = jnp.arange(length, dtype=jnp.int32)
    allowed = (own_seg[:, :, None] == segments[:, None, :]) & (
        key_place[None, None, :] <= own_place[None, :, None]
    )
    allowed = allowed[:, None, None, :, :]
    attn_full = (
        lax.all_gather(gain_attn.astype(jnp.bfloat16), ("fsdp", "ctx"), axis=0, tiled=True).astype(
            gain_attn.dtype
        ),
        lax.all_gather(query_weight, ("fsdp", "ctx"), axis=0, tiled=True),
        lax.all_gather(key_weight, ("fsdp", "ctx"), axis=0, tiled=True),
        lax.all_gather(value_weight, ("fsdp", "ctx"), axis=0, tiled=True),
        lax.all_gather(out_weight, ("fsdp", "ctx"), axis=0, tiled=True),
    )
    gain_a, query_full, key_full, value_full, out_full = attn_full
    inputs_f = hidden_in.reshape(tokens, width).astype(jnp.float32)
    inv_a = lax.rsqrt(jnp.mean(inputs_f * inputs_f, axis=-1, keepdims=True) + EPSILON)
    unit_a = inputs_f * inv_a
    normed_a = (unit_a * gain_a).astype(bfloat)
    query_raw = matmul_low(normed_a, query_full).reshape(
        seqs_here, rows_here, kv_local, group_size, HD
    )
    key_raw = matmul_low(normed_a, key_full).reshape(seqs_here, rows_here, kv_local, HD)
    value_low = (
        matmul_low(normed_a, value_full).astype(bfloat).reshape(seqs_here, rows_here, kv_local * HD)
    )
    query_rot = rotate_pairs(
        query_raw, cosine[:, :, None, None, :], sine[:, :, None, None, :]
    ).astype(bfloat)
    key_rot = rotate_pairs(key_raw, cosine[:, :, None, :], sine[:, :, None, :]).astype(bfloat)
    key_rot = key_rot.reshape(seqs_here, rows_here, kv_local * HD)
    key_all, value_all = (
        lax.all_gather(key_rot, "ctx", axis=1, tiled=True),
        lax.all_gather(value_low, "ctx", axis=1, tiled=True),
    )
    key_all = key_all.reshape(seqs_here, length, kv_local, HD)
    value_all = value_all.reshape(seqs_here, length, kv_local, HD)

    def masked_scores():
        scores = (
            jnp.einsum("srngd,slnd->sngrl", query_rot, key_all, preferred_element_type=jnp.float32)
            * SCALE
        )
        return jnp.where(allowed, scores, -1e30)

    scores = masked_scores()
    highest = jnp.max(scores, axis=-1, keepdims=True)
    raised = jnp.exp(scores - highest)
    totals = jnp.sum(raised, axis=-1, keepdims=True)
    log_total = highest + jnp.log(totals)
    probs_low = (raised / totals).astype(bfloat)
    mixed = jnp.einsum(
        "sngrl,slnd->srngd", probs_low, value_all, preferred_element_type=jnp.float32
    )
    mixed = mixed.astype(bfloat).reshape(tokens, head_cols)
    branch_a = lax.psum(matmul_trans(mixed, out_full).astype(jnp.bfloat16), "tp").astype(
        jnp.float32
    )
    middle = inputs_f + RESIDUAL * branch_a
    ffn_full = (
        lax.all_gather(gain_ffn.astype(jnp.bfloat16), ("fsdp", "ctx"), axis=0, tiled=True).astype(
            gain_ffn.dtype
        ),
        lax.all_gather(gate_weight, ("fsdp", "ctx"), axis=0, tiled=True),
        lax.all_gather(up_weight, ("fsdp", "ctx"), axis=0, tiled=True),
        lax.all_gather(down_weight, ("fsdp", "ctx"), axis=0, tiled=True),
    )
    gain_f, gate_full, up_full, down_full = ffn_full
    inv_f = lax.rsqrt(jnp.mean(middle * middle, axis=-1, keepdims=True) + EPSILON)
    unit_f = middle * inv_f
    normed_f = (unit_f * gain_f).astype(bfloat)
    gate_pre = matmul_low(normed_f, gate_full)
    upward = matmul_low(normed_f, up_full)
    sigma = jax.nn.sigmoid(gate_pre)
    active = gate_pre * sigma
    hidden = (active * upward).astype(bfloat)
    branch_f = lax.psum(matmul_trans(hidden, down_full).astype(jnp.bfloat16), "tp").astype(
        jnp.float32
    )
    layer_out = (middle + RESIDUAL * branch_f).astype(bfloat).reshape(seqs_here, rows_here, width)
    gain_fb, gate_back, up_back, down_back = (
        lax.all_gather(gain_ffn.astype(jnp.bfloat16), ("fsdp", "ctx"), axis=0, tiled=True).astype(
            gain_ffn.dtype
        ),
        lax.all_gather(gate_weight, ("fsdp", "ctx"), axis=0, tiled=True),
        lax.all_gather(up_weight, ("fsdp", "ctx"), axis=0, tiled=True),
        lax.all_gather(down_weight, ("fsdp", "ctx"), axis=0, tiled=True),
    )
    grad_y = cotangent.reshape(tokens, width).astype(jnp.float32)
    d_branch_f = (RESIDUAL * grad_y).astype(bfloat)
    grad_down = matmul_outer(d_branch_f, hidden)
    d_hidden = matmul_low(d_branch_f, down_back)
    d_gate = (d_hidden * upward * sigma * (1.0 + gate_pre * (1.0 - sigma))).astype(bfloat)
    d_up = (d_hidden * active).astype(bfloat)
    grad_gate = matmul_outer(normed_f, d_gate)
    grad_up = matmul_outer(normed_f, d_up)
    d_normed_f = lax.psum(
        (matmul_trans(d_gate, gate_back) + matmul_trans(d_up, up_back)).astype(jnp.bfloat16), "tp"
    ).astype(jnp.float32)
    grad_gain_ffn = jnp.sum(d_normed_f * unit_f, axis=0)
    d_middle = grad_y + norm_back(d_normed_f, gain_fb, unit_f, inv_f)
    ffn_grads = (
        lax.psum_scatter(grad_gain_ffn, ("fsdp", "ctx"), scatter_dimension=0, tiled=True),
        lax.psum_scatter(grad_gate, ("fsdp", "ctx"), scatter_dimension=0, tiled=True),
        lax.psum_scatter(grad_up, ("fsdp", "ctx"), scatter_dimension=0, tiled=True),
        lax.psum_scatter(grad_down, ("fsdp", "ctx"), scatter_dimension=0, tiled=True),
    )
    gain_ab, query_back, key_back, value_back, out_back = (
        lax.all_gather(gain_attn.astype(jnp.bfloat16), ("fsdp", "ctx"), axis=0, tiled=True).astype(
            gain_attn.dtype
        ),
        lax.all_gather(query_weight, ("fsdp", "ctx"), axis=0, tiled=True),
        lax.all_gather(key_weight, ("fsdp", "ctx"), axis=0, tiled=True),
        lax.all_gather(value_weight, ("fsdp", "ctx"), axis=0, tiled=True),
        lax.all_gather(out_weight, ("fsdp", "ctx"), axis=0, tiled=True),
    )
    d_branch_a = (RESIDUAL * d_middle).astype(bfloat)
    grad_out = matmul_outer(d_branch_a, mixed)
    d_mixed = (
        matmul_low(d_branch_a, out_back)
        .astype(bfloat)
        .reshape(seqs_here, rows_here, kv_local, group_size, HD)
    )
    probs_again = jnp.exp(masked_scores() - log_total)
    probs_again_low = probs_again.astype(bfloat)
    d_probs = jnp.einsum(
        "srngd,slnd->sngrl", d_mixed, value_all, preferred_element_type=jnp.float32
    )
    inner = jnp.sum(probs_again * d_probs, axis=-1, keepdims=True)
    d_scores = (probs_again * (d_probs - inner)).astype(bfloat)
    d_query_rot = (
        jnp.einsum("sngrl,slnd->srngd", d_scores, key_all, preferred_element_type=jnp.float32)
        * SCALE
    )
    d_key_all = (
        jnp.einsum("sngrl,srngd->slnd", d_scores, query_rot, preferred_element_type=jnp.float32)
        * SCALE
    )
    d_value_all = jnp.einsum(
        "sngrl,srngd->slnd", probs_again_low, d_mixed, preferred_element_type=jnp.float32
    )
    d_key_own, d_value_own = (
        lax.psum_scatter(
            d_key_all.reshape(seqs_here, length, kv_local * HD).astype(jnp.bfloat16),
            "ctx",
            scatter_dimension=1,
            tiled=True,
        ).astype(jnp.float32),
        lax.psum_scatter(
            d_value_all.reshape(seqs_here, length, kv_local * HD).astype(jnp.bfloat16),
            "ctx",
            scatter_dimension=1,
            tiled=True,
        ).astype(jnp.float32),
    )
    d_query = (
        rotate_pairs(d_query_rot, cosine[:, :, None, None, :], -sine[:, :, None, None, :])
        .astype(bfloat)
        .reshape(tokens, head_cols)
    )
    d_key = rotate_pairs(
        d_key_own.reshape(seqs_here, rows_here, kv_local, HD),
        cosine[:, :, None, :],
        -sine[:, :, None, :],
    )
    d_key = d_key.astype(bfloat).reshape(tokens, kv_local * HD)
    d_value = d_value_own.reshape(tokens, kv_local * HD).astype(bfloat)
    grad_query = matmul_outer(normed_a, d_query)
    grad_key = matmul_outer(normed_a, d_key)
    grad_value = matmul_outer(normed_a, d_value)
    d_normed_part = (
        matmul_trans(d_query, query_back)
        + matmul_trans(d_key, key_back)
        + matmul_trans(d_value, value_back)
    )
    d_normed_a = lax.psum(d_normed_part.astype(jnp.bfloat16), "tp").astype(jnp.float32)
    grad_gain_attn = jnp.sum(d_normed_a * unit_a, axis=0)
    input_grad = (d_middle + norm_back(d_normed_a, gain_ab, unit_a, inv_a)).reshape(
        seqs_here, rows_here, width
    )
    attn_grads = (
        lax.psum_scatter(grad_gain_attn, ("fsdp", "ctx"), scatter_dimension=0, tiled=True),
        lax.psum_scatter(grad_query, ("fsdp", "ctx"), scatter_dimension=0, tiled=True),
        lax.psum_scatter(grad_key, ("fsdp", "ctx"), scatter_dimension=0, tiled=True),
        lax.psum_scatter(grad_value, ("fsdp", "ctx"), scatter_dimension=0, tiled=True),
        lax.psum_scatter(grad_out, ("fsdp", "ctx"), scatter_dimension=0, tiled=True),
    )
    return (
        layer_out,
        input_grad,
        attn_grads[0],
        attn_grads[1],
        attn_grads[2],
        attn_grads[3],
        attn_grads[4],
        ffn_grads[0],
        ffn_grads[1],
        ffn_grads[2],
        ffn_grads[3],
    )


def solution(mesh):
    in_specs = (
        P("fsdp", "ctx", None),
        P("fsdp", None),
        P(("fsdp", "ctx")),
        P(("fsdp", "ctx"), "tp"),
        P(("fsdp", "ctx"), "tp"),
        P(("fsdp", "ctx"), "tp"),
        P(("fsdp", "ctx"), "tp"),
        P(("fsdp", "ctx")),
        P(("fsdp", "ctx"), "tp"),
        P(("fsdp", "ctx"), "tp"),
        P(("fsdp", "ctx"), "tp"),
        P("fsdp", "ctx", None),
    )
    out_specs = (
        P("fsdp", "ctx", None),
        P("fsdp", "ctx", None),
        P(("fsdp", "ctx")),
        P(("fsdp", "ctx"), "tp"),
        P(("fsdp", "ctx"), "tp"),
        P(("fsdp", "ctx"), "tp"),
        P(("fsdp", "ctx"), "tp"),
        P(("fsdp", "ctx")),
        P(("fsdp", "ctx"), "tp"),
        P(("fsdp", "ctx"), "tp"),
        P(("fsdp", "ctx"), "tp"),
    )
    return jax.shard_map(shards, mesh=mesh, in_specs=in_specs, out_specs=out_specs, check_vma=False)
```

profile of v0, /device:TPU:0, one launch (start us, length us, event | category | flops | bytes accessed | tf_op | source)
XLA Modules:
  0.0 3722.1 jit_solution(10371249642786095840)
XLA Ops:
  14.5 42.2 %all-gather.2 = bf16[16,1,128]{2,1,0:T(2,128)(2,1)S(1)} all-gather(bf16[1,1,128]{2,1,0:T(2,128)(2,1)S(1)} %convert_bitcast_fusion.2), channel_id=1, replica_groups=mesh['fsdp'=8,'ctx'=2,'tp'=2] {'fsdp','ctx'}, dimensions={0}, use_global_device_ids=true | all-gather | bytes 4352 | tf_op jit(solution)/shard_map/all_gather | solution.py:81
  59.1 9.7 all-gather.12.cloned.1.call-done
  71.5 7.4 all-gather
  79.9 45.8 %all-gather.14.cloned.1.call-done = bf16[2048,256]{1,0:T(8,128)(2,1)} async-done(((bf16[128,256]{1,0:T(8,128)(2,1)}), bf16[2048,256]{1,0:T(8,128)(2,1)}) %all-gather.14.cloned.1.call-update) | async-done | bytes 1048592 | tf_op jit(solution)/shard_map/all_gather | solution.py:85
  128.1 7.4 all-gather.1
  135.5 67.9 %all-gather.16.cloned.1.call-done = bf16[2048,1024]{1,0:T(8,128)(2,1)} async-done(((bf16[128,1024]{1,0:T(8,128)(2,1)}), bf16[2048,1024]{1,0:T(8,128)(2,1)}) %all-gather.16.cloned.1.call-update) | async-done | bytes 4194320 | tf_op jit(solution)/shard_map/all_gather | solution.py:84
  203.4 4.6 fusion.82
  209.0 14.0 fusion.87
  223.1 13.3 fusion.3
  236.4 13.8 fusion.47
  250.2 30.6 all-gather.18.cloned.1.call-done
  280.7 5.9 convolution_convert_fusion
  288.8 38.2 %all-gather.3 = bf16[16,1,128]{2,1,0:T(2,128)(2,1)S(1)} all-gather(bf16[1,1,128]{2,1,0:T(2,128)(2,1)S(1)} %convert_bitcast_fusion.1), channel_id=1, replica_groups=mesh['fsdp'=8,'ctx'=2,'tp'=2] {'fsdp','ctx'}, dimensions={0}, use_global_device_ids=true | all-gather | bytes 4352 | tf_op jit(solution)/shard_map/all_gather | solution.py:135
  332.7 169.7 %all-gather.22.cloned.1.call-done = bf16[2048,4096]{1,0:T(8,128)(2,1)} async-done(((bf16[128,4096]{1,0:T(8,128)(2,1)}), bf16[2048,4096]{1,0:T(8,128)(2,1)}) %all-gather.22.cloned.1.call-update) | async-done | bytes 16777232 | tf_op jit(solution)/shard_map/all_gather | solution.py:139
  502.5 15.2 fusion.89
  517.6 177.8 %all-gather.20.cloned.1.call-done = bf16[2048,4096]{1,0:T(8,128)(2,1)} async-done(((bf16[128,4096]{1,0:T(8,128)(2,1)}), bf16[2048,4096]{1,0:T(8,128)(2,1)}) %all-gather.20.cloned.1.call-update) | async-done | bytes 16777232 | tf_op jit(solution)/shard_map/all_gather | solution.py:138
  695.4 15.0 fusion.88
  710.4 178.0 %all-gather.24.cloned.1.call-done = bf16[2048,4096]{1,0:T(8,128)(2,1)} async-done(((bf16[128,4096]{1,0:T(8,128)(2,1)}), bf16[2048,4096]{1,0:T(8,128)(2,1)}) %all-gather.24.cloned.1.call-update) | async-done | bytes 16777232 | tf_op jit(solution)/shard_map/all_gather | solution.py:140
  888.4 22.2 multiply_convert_fusion
  910.6 15.5 fusion.90
  926.1 14.0 add_convert_fusion.1
  940.2 15.7 convolution_convert_fusion.1
  955.9 3.8 all-reduce.10.cloned.1.call-done
  959.7 4.6 fusion.28
  964.4 6.7 convolution_convert_fusion.2
  972.6 14.1 fusion.55
  986.8 22.1 fusion
  1008.9 28.0 fusion.8
  1036.9 11.7 fusion.54
  1048.6 10.3 bitcast_multiply_fusion.1
  1063.9 4.3 fusion.91
  1071.4 2.8 fusion.92
  1074.2 7.2 reduce-scatter.12.cloned.1.call-done
  1081.4 6.0 add_convert_fusion
  1093.6 11.4 fusion.59
  1106.2 6.2 fusion.80
  1112.5 18.4 fusion.43
  1131.3 18.0 fusion.94
  1149.4 17.9 fusion.93
  1169.3 2.9 fusion.31
  1172.2 76.8 %all-reduce.2 = (f32[2048]{0:T(1024)S(1)}, f32[2048]{0:T(1024)S(1)}) all-reduce(f32[2048]{0:T(1024)S(1)} %get-tuple-element.13, f32[2048]{0:T(1024)S(1)} %copy-done.23), channel_id=6, replica_groups=mesh['fsdp'=8,'ctx'=2,'tp'=2] {'fsdp','ctx'}, use_global_device_ids=true, to_apply=%region_15.16.clone | all-reduce | flops 4096 | bytes 32768
  1250.2 8.3 fusion.25
  1258.5 23.1 reduce-scatter.16.cloned.1.call-done
  1281.6 177.8 %reduce-scatter.20.cloned.1.call-done = f32[128,1024]{1,0:T(8,128)} async-done(((f32[2048,1024]{1,0:T(8,128)}), f32[128,1024]{1,0:T(8,128)}) %reduce-scatter.20.cloned.1.call-update) | async-done | bytes 524304 | tf_op jit(solution)/shard_map/reduce_scatter | solution.py:260
  1459.3 183.1 %reduce-scatter.14.cloned.1.call-done = f32[128,1024]{1,0:T(8,128)} async-done(((f32[2048,1024]{1,0:T(8,128)}), f32[128,1024]{1,0:T(8,128)}) %reduce-scatter.14.cloned.1.call-update) | async-done | bytes 524304 | tf_op jit(solution)/shard_map/reduce_scatter | solution.py:257
  1642.4 688.8 %reduce-scatter.26.cloned.1.call-done = f32[128,4096]{1,0:T(8,128)} async-done(((f32[2048,4096]{1,0:T(8,128)}), f32[128,4096]{1,0:T(8,128)}) %reduce-scatter.26.cloned.1.call-update) | async-done | bytes 2097168 | tf_op jit(solution)/shard_map/reduce_scatter | solution.py:180
  2331.2 692.0 %reduce-scatter.24.cloned.1.call-done = f32[128,4096]{1,0:T(8,128)} async-done(((f32[2048,4096]{1,0:T(8,128)}), f32[128,4096]{1,0:T(8,128)}) %reduce-scatter.24.cloned.1.call-update) | async-done | bytes 2097168 | tf_op jit(solution)/shard_map/reduce_scatter | solution.py:179
  3023.3 692.1 %reduce-scatter.22.cloned.1.call-done = f32[128,4096]{1,0:T(8,128)} async-done(((f32[2048,4096]{1,0:T(8,128)}), f32[128,4096]{1,0:T(8,128)}) %reduce-scatter.22.cloned.1.call-update) | async-done | bytes 2097168 | tf_op jit(solution)/shard_map/reduce_scatter | solution.py:178
  (152 shorter events, 44.5 us)
Async XLA Ops:
  7.2 61.7 %all-gather.12.cloned.1.call-start = ((), (), s32[]{:S(2)}) async-start(), calls=%async_computation.9 | async-start | bytes 1114112 | tf_op jit(solution)/shard_map/all_gather | solution.py:86
  7.9 117.8 %all-gather.14.cloned.1.call-start = ((), (), s32[]{:S(2)}) async-start(), calls=%async_computation.10 | async-start | bytes 1114112 | tf_op jit(solution)/shard_map/all_gather | solution.py:85
  8.7 194.7 %all-gather.16.cloned.1.call-start = ((), (), s32[]{:S(2)}) async-start(), calls=%async_computation.11 | async-start | bytes 4456448 | tf_op jit(solution)/shard_map/all_gather | solution.py:84
  9.4 271.3 %all-gather.18.cloned.1.call-start = ((), (), s32[]{:S(2)}) async-start(), calls=%async_computation.12 | async-start | bytes 4456448 | tf_op jit(solution)/shard_map/all_gather | solution.py:87
  10.0 317.6 %all-reduce.8.cloned.1.call-start = ((), (), s32[]{:S(2)}) async-start(), calls=%async_computation.13 | async-start | bytes 4194304 | tf_op jit(solution)/shard_map/psum | solution.py:130
  14.5 188.9 %copy-start.24 = (f32[512]{0:T(512)}, f32[512]{0:T(512)S(1)}, u32[]{:S(2)}) copy-start(f32[512]{0:T(512)S(1)} %add_rsqrt_fusion.1) | copy-start | bytes 6148
  56.7 146.7 %copy-start.19 = (f32[16,1,128]{2,1,0:T(1,128)}, f32[16,1,128]{2,1,0:T(1,128)S(1)}, u32[]{:S(2)}) copy-start(f32[16,1,128]{2,1,0:T(1,128)S(1)} %convert_element_type.267) | copy-start | bytes 24580
  57.8 150.6 %copy-start.8 = (f32[512,64]{0,1:T(8,128)}, f32[512,64]{0,1:T(8,128)S(1)}, u32[]{:S(2)}) copy-start(f32[512,64]{0,1:T(8,128)S(1)} %get-tuple-element.33) | copy-start | bytes 393220
  57.8 67.9 %copy-start = (bf16[1,512,2048]{2,1,0:T(8,128)(2,1)S(1)}, bf16[1,512,2048]{2,1,0:T(8,128)(2,1)}, u32[]{:S(2)}) copy-start(bf16[1,512,2048]{2,1,0:T(8,128)(2,1)} %param.12) | copy-start | bytes 6291460
  135.5 73.5 %copy-start.6 = (bf16[1024,256]{0,1:T(8,128)(2,1)}, bf16[1024,256]{0,1:T(8,128)(2,1)S(1)}, u32[]{:S(2)}) copy-start(bf16[1024,256]{0,1:T(8,128)(2,1)S(1)} %all-gather.1) | copy-start | bytes 1572868
  209.0 14.1 copy-start.3
  223.1 13.3 copy-start.10
  250.1 30.6 copy-start.31
  286.6 2.2 copy-start.30
  286.7 215.8 %all-gather.22.cloned.1.call-start = ((), (), s32[]{:S(2)}) async-start(), calls=%async_computation.15 | async-start | bytes 17825792 | tf_op jit(solution)/shard_map/all_gather | solution.py:139
  287.2 408.2 %all-gather.20.cloned.1.call-start = ((), (), s32[]{:S(2)}) async-start(), calls=%async_computation.14 | async-start | bytes 17825792 | tf_op jit(solution)/shard_map/all_gather | solution.py:138
  288.0 600.4 %all-gather.24.cloned.1.call-start = ((), (), s32[]{:S(2)}) async-start(), calls=%async_computation.16 | async-start | bytes 17825792 | tf_op jit(solution)/shard_map/all_gather | solution.py:140
  288.7 671.0 %all-reduce.10.cloned.1.call-start = ((), (), s32[]{:S(2)}) async-start(), calls=%async_computation.17 | async-start | bytes 4194304 | tf_op jit(solution)/shard_map/psum | solution.py:171
  327.6 2.6 copy-start.1
  330.3 634.1 %copy-start.21 = (f32[512]{0:T(512)}, f32[512]{0:T(512)S(1)}, u32[]{:S(2)}) copy-start(f32[512]{0:T(512)S(1)} %add_rsqrt_fusion) | copy-start | bytes 6148
  910.6 15.5 copy-start.33
  940.1 128.1 %reduce-scatter.10.cloned.1.call-start = ((), (), s32[]{:S(2)}) async-start(), calls=%async_computation.18 | async-start | bytes 786432 | tf_op jit(solution)/shard_map/reduce_scatter | solution.py:217
  959.7 4.7 copy-start.2
  959.7 4.7 copy-start.5
  959.7 4.7 copy-start.11
  964.4 6.8 copy-start.27
  964.4 8.3 copy-start.16
  1008.9 28.0 copy-start.4
  1048.6 32.8 reduce-scatter.12.cloned.1.call-start
  1058.9 1.3 copy-start.12
  1058.9 1.3 copy-start.17
  1060.1 109.1 %all-reduce.12.cloned.1.call-start = ((), (), s32[]{:S(2)}) async-start(), calls=%async_computation.27 | async-start | bytes 8388608 | tf_op jit(solution)/shard_map/psum | solution.py:151
  1060.2 3.7 copy-start.29
  1063.9 6.5 copy-start.9
  1068.2 3.2 copy-start.15
  1087.4 3.6 copy-start.7
  1087.4 171.1 %reduce-scatter.18.cloned.1.call-start = ((), (), s32[]{:S(2)}) async-start(), calls=%async_computation.22 | async-start | bytes 2228224 | tf_op jit(solution)/shard_map/reduce_scatter | solution.py:259
  1090.7 190.9 %reduce-scatter.16.cloned.1.call-start = ((), (), s32[]{:S(2)}) async-start(), calls=%async_computation.21 | async-start | bytes 2228224 | tf_op jit(solution)/shard_map/reduce_scatter | solution.py:258
  1091.1 2.5 copy-start.22
  1091.1 2.5 copy-start.28
  1093.5 365.8 %reduce-scatter.20.cloned.1.call-start = ((), (), s32[]{:S(2)}) async-start(), calls=%async_computation.23 | async-start | bytes 8912896 | tf_op jit(solution)/shard_map/reduce_scatter | solution.py:260
  1105.0 1.3 copy-start.14
  1105.0 1.3 copy-start.26
  1105.0 537.4 %reduce-scatter.14.cloned.1.call-start = ((), (), s32[]{:S(2)}) async-start(), calls=%async_computation.20 | async-start | bytes 8912896 | tf_op jit(solution)/shard_map/reduce_scatter | solution.py:257
  1112.4 1218.8 %reduce-scatter.26.cloned.1.call-start = ((), (), s32[]{:S(2)}) async-start(), calls=%async_computation.26 | async-start | bytes 35651584 | tf_op jit(solution)/shard_map/reduce_scatter | solution.py:180
  1130.9 1892.4 %reduce-scatter.24.cloned.1.call-start = ((), (), s32[]{:S(2)}) async-start(), calls=%async_computation.25 | async-start | bytes 35651584 | tf_op jit(solution)/shard_map/reduce_scatter | solution.py:179
  1149.4 2566.0 %reduce-scatter.22.cloned.1.call-start = ((), (), s32[]{:S(2)}) async-start(), calls=%async_computation.24 | async-start | bytes 35651584 | tf_op jit(solution)/shard_map/reduce_scatter | solution.py:178
  1167.4 4.8 copy-start.23
  (5 other events, 4.5 us)
Sparse Core Ops, SparseCore 0:
  10.8 58.0 all-gather.11
  71.6 54.0 all-gather.13
  128.5 74.8 all-gather.15
  206.0 74.6 all-gather.17
  286.8 19.7 all-reduce.7
  309.6 192.7 all-gather.21
  505.6 189.7 all-gather.19
  698.6 189.7 all-gather.23
  940.3 19.3 all-reduce.9
  1048.7 15.7 reduce-scatter.9
  1066.8 14.5 reduce-scatter.11
  1087.5 28.5 all-reduce.11
  1119.0 81.5 reduce-scatter.17
  1203.4 78.0 reduce-scatter.15
  1284.4 174.8 reduce-scatter.19
  1462.2 180.2 reduce-scatter.13
  1645.3 685.8 reduce-scatter.25
  2334.1 689.0 reduce-scatter.23
  3026.3 689.0 reduce-scatter.21
where the time goes:
time: 3730 us; the launch traced here: 3720 us
  waiting for transfers between devices  3150 us (84%)
  matrix products  295 us (8%)
  blocking collectives  172 us (5%)
  other arithmetic  76.2 us (2%)
    reduce_scatter x1, waiting for transfers between devices, shards(): lax.psum_scatter(grad_gate, ('fsdp', 'ctx'), scatter_dimension=0, tiled=T...  692 us
    reduce_scatter x1, waiting for transfers between devices, shards(): lax.psum_scatter(grad_up, ('fsdp', 'ctx'), scatter_dimension=0, tiled=True)  692 us
    reduce_scatter x1, waiting for transfers between devices, shards(): lax.psum_scatter(grad_down, ('fsdp', 'ctx'), scatter_dimension=0, tiled=T...  689 us
    reduce_scatter x1, waiting for transfers between devices, shards(): lax.psum_scatter(grad_query, ('fsdp', 'ctx'), scatter_dimension=0, tiled=...  183 us
    all_gather x1, waiting for transfers between devices, shards(): lax.all_gather(down_weight, ('fsdp', 'ctx'), axis=0, tiled=True)  178 us
    all_gather x1, waiting for transfers between devices, shards(): lax.all_gather(gate_weight, ('fsdp', 'ctx'), axis=0, tiled=True)  178 us
    reduce_scatter x1, waiting for transfers between devices, shards(): lax.psum_scatter(grad_out, ('fsdp', 'ctx'), scatter_dimension=0, tiled=True)  178 us
    all_gather x1, waiting for transfers between devices, shards(): lax.all_gather(up_weight, ('fsdp', 'ctx'), axis=0, tiled=True)  170 us
  transfers between devices with their start and end apart: 19, of which 15 were waited for; matrix products, arithmetic and copies ran while one was open for 6% of the time, Pallas kernels for 0%

commit v1 on v0

--- a/solution.py
+++ b/solution.py
@@ -1,6 +1,11 @@
+import functools
+
 import jax
 import jax.numpy as jnp
 from jax import lax
+from jax.experimental import pallas as pl
+from jax.experimental.pallas import tpu as pltpu
+from jax.sharding import Mesh
 from jax.sharding import PartitionSpec as P
 
 HQ = 32
@@ -41,7 +46,14 @@
     return inv_rms * (scaled - unit_rows * jnp.mean(scaled * unit_rows, axis=-1, keepdims=True))
 
 
-def shards(
+def reduce_low(grad):
+    low = lax.psum_scatter(
+        grad.astype(jnp.bfloat16), ("fsdp", "ctx"), scatter_dimension=0, tiled=True
+    )
+    return low.astype(jnp.float32)
+
+
+def generic_shards(
     hidden_in,
     segments,
     gain_attn,
@@ -175,9 +187,9 @@
     d_middle = grad_y + norm_back(d_normed_f, gain_fb, unit_f, inv_f)
     ffn_grads = (
         lax.psum_scatter(grad_gain_ffn, ("fsdp", "ctx"), scatter_dimension=0, tiled=True),
-        lax.psum_scatter(grad_gate, ("fsdp", "ctx"), scatter_dimension=0, tiled=True),
-        lax.psum_scatter(grad_up, ("fsdp", "ctx"), scatter_dimension=0, tiled=True),
-        lax.psum_scatter(grad_down, ("fsdp", "ctx"), scatter_dimension=0, tiled=True),
+        reduce_low(grad_gate),
+        reduce_low(grad_up),
+        reduce_low(grad_down),
     )
     gain_ab, query_back, key_back, value_back, out_back = (
         lax.all_gather(gain_attn.astype(jnp.bfloat16), ("fsdp", "ctx"), axis=0, tiled=True).astype(
@@ -254,10 +266,10 @@
     )
     attn_grads = (
         lax.psum_scatter(grad_gain_attn, ("fsdp", "ctx"), scatter_dimension=0, tiled=True),
-        lax.psum_scatter(grad_query, ("fsdp", "ctx"), scatter_dimension=0, tiled=True),
-        lax.psum_scatter(grad_key, ("fsdp", "ctx"), scatter_dimension=0, tiled=True),
-        lax.psum_scatter(grad_value, ("fsdp", "ctx"), scatter_dimension=0, tiled=True),
-        lax.psum_scatter(grad_out, ("fsdp", "ctx"), scatter_dimension=0, tiled=True),
+        reduce_low(grad_query),
+        reduce_low(grad_key),
+        reduce_low(grad_value),
+        reduce_low(grad_out),
     )
     return (
         layer_out,
@@ -274,32 +286,484 @@
     )
 
 
+MAX_DOC = 512
+LANES = 128
+NEG = -1e30
+
+
+def half_lanes(rows):
+    lane = lax.broadcasted_iota(jnp.int32, (rows, LANES), 1)
+    return lane % HD < HD // 2, lane < HD
+
+
+def turn(slab, cosine, sine_signed):
+    first, _ = half_lanes(slab.shape[0])
+    swapped = jnp.where(
+        first,
+        pltpu.roll(slab, LANES - HD // 2, 1),
+        pltpu.roll(slab, HD // 2, 1),
+    )
+    return slab * cosine + swapped * sine_signed
+
+
+def dot_nt(left, right):
+    return lax.dot_general(left, right, (((1,), (1,)), ((), ())), preferred_element_type=jnp.float32)
+
+
+def dot_tn(left, right):
+    return lax.dot_general(left, right, (((0,), (0,)), ((), ())), preferred_element_type=jnp.float32)
+
+
+def window_mask(start, first_query, first_key, rows, keys):
+    query = first_query + lax.broadcasted_iota(jnp.int32, (rows, keys), 0)
+    key = first_key + lax.broadcasted_iota(jnp.int32, (rows, keys), 1)
+    return (key <= query) & (key >= start)
+
+
+def attend_kernel(
+    rows, window, heads, place_ref, qkv_ref, inv_ref, cos_ref, sin_ref, start_ref,
+    query_ref, kv_ref, mixed_ref, lse_ref, keys, values,
+):
+    step = pl.program_id(1)
+    _, low_half = half_lanes(rows)
+    inv = inv_ref[...]
+    cosine, sine = cos_ref[...], sin_ref[...]
+
+    @pl.when(step == 0)
+    def _():
+        keys[...] = jnp.zeros_like(keys)
+        values[...] = jnp.zeros_like(values)
+
+    width = heads * HD
+    raw = qkv_ref[:, width:] * inv
+    kv = jnp.where(low_half, turn(raw, cosine, sine), raw)
+    kv_ref[...] = kv.astype(jnp.bfloat16)
+    moved = pltpu.roll(kv, HD, 1)
+    own = pl.ds(pl.multiple_of(step * rows, rows), rows)
+    keys[own, :] = jnp.where(low_half, kv, moved).astype(jnp.bfloat16)
+    values[own, :] = jnp.where(low_half, moved, kv).astype(jnp.bfloat16)
+
+    first_key = pl.multiple_of(jnp.maximum((step + 1) * rows - window, 0), rows)
+    keys_w = keys[pl.ds(first_key, window), :]
+    values_w = values[pl.ds(first_key, window), :]
+    allowed = window_mask(start_ref[...], step * rows, first_key, rows, window)
+    for slab in range(width // LANES):
+        at = slice(slab * LANES, (slab + 1) * LANES)
+        rot = turn(qkv_ref[:, at] * inv, cosine, sine).astype(jnp.bfloat16)
+        query_ref[:, at] = rot
+        both = []
+        for part in range(2):
+            mine = low_half if part == 0 else jnp.logical_not(low_half)
+            one = jnp.where(mine, rot, jnp.zeros_like(rot))
+            scores = jnp.where(allowed, dot_nt(one, keys_w) * SCALE, NEG)
+            highest = jnp.max(scores, axis=1, keepdims=True)
+            raised = jnp.exp(scores - highest)
+            total = jnp.sum(raised, axis=1, keepdims=True)
+            mixed = jnp.dot(
+                raised.astype(jnp.bfloat16), values_w, preferred_element_type=jnp.float32
+            )
+            both.append(mixed / total)
+            head = slab * 2 + part
+            lse_ref[:, head : head + 1] = highest + jnp.log(total)
+        mixed_ref[:, at] = jnp.where(low_half, both[0], both[1]).astype(jnp.bfloat16)
+
+
+def attend_back_kernel(
+    rows, window, heads, blocks, place_ref, query_ref, kv_ref, lse_ref, grad_ref, inv_ref, cos_ref, sin_ref, start_ref,
+    out_ref, keys, values, d_keys, d_values,
+):
+    seq = pl.program_id(0)
+    step = blocks - 1 - pl.program_id(1)
+    _, low_half = half_lanes(rows)
+    inv = inv_ref[...]
+    cosine, sine = cos_ref[...], sin_ref[...]
+
+    @pl.when(step == blocks - 1)
+    def _():
+        for block in range(blocks):
+            source = pl.multiple_of(place_ref[seq * blocks + block] * rows, rows)
+            kv = kv_ref[pl.ds(source, rows), :].astype(jnp.float32)
+            moved = pltpu.roll(kv, HD, 1)
+            at = slice(block * rows, (block + 1) * rows)
+            keys[at, :] = jnp.where(low_half, kv, moved).astype(jnp.bfloat16)
+            values[at, :] = jnp.where(low_half, moved, kv).astype(jnp.bfloat16)
+        d_keys[...] = jnp.zeros_like(d_keys)
+        d_values[...] = jnp.zeros_like(d_values)
+
+    first_key = pl.multiple_of(jnp.maximum((step + 1) * rows - window, 0), rows)
+    span = pl.ds(first_key, window)
+    keys_w = keys[span, :]
+    values_w = values[span, :]
+    allowed = window_mask(start_ref[...], step * rows, first_key, rows, window)
+    d_keys_w = jnp.zeros((window, LANES), jnp.float32)
+    d_values_w = jnp.zeros((window, LANES), jnp.float32)
+    width = heads * HD
+    for slab in range(width // LANES):
+        at = slice(slab * LANES, (slab + 1) * LANES)
+        query, grad = query_ref[:, at], grad_ref[:, at]
+        both = []
+        for part in range(2):
+            mine = low_half if part == 0 else jnp.logical_not(low_half)
+            head = slab * 2 + part
+            one = jnp.where(mine, query, jnp.zeros_like(query))
+            one_grad = jnp.where(mine, grad, jnp.zeros_like(grad))
+            scores = dot_nt(one, keys_w) * SCALE - lse_ref[:, head : head + 1]
+            probs = jnp.exp(jnp.where(allowed, scores, NEG))
+            d_probs = dot_nt(one_grad, values_w)
+            inner = jnp.sum(probs * d_probs, axis=1, keepdims=True)
+            d_scores = (probs * (d_probs - inner)).astype(jnp.bfloat16)
+            both.append(jnp.dot(d_scores, keys_w, preferred_element_type=jnp.float32))
+            d_keys_w = d_keys_w + dot_tn(d_scores, one)
+            d_values_w = d_values_w + dot_tn(probs.astype(jnp.bfloat16), one_grad)
+        d_query = jnp.where(low_half, both[0], both[1]) * SCALE
+        out_ref[:, at] = (turn(d_query, cosine, -sine) * inv).astype(jnp.bfloat16)
+    d_keys[span, :] += d_keys_w
+    d_values[span, :] += d_values_w
+    own = pl.ds(pl.multiple_of(step * rows, rows), rows)
+    d_key = d_keys[own, :] * SCALE
+    d_key = turn(d_key + pltpu.roll(d_key, HD, 1), cosine, -sine)
+    d_value = d_values[own, :]
+    d_value = d_value + pltpu.roll(d_value, HD, 1)
+    out_ref[:, width:] = (jnp.where(low_half, d_key, d_value) * inv).astype(jnp.bfloat16)
+
+
+def attend(place, qkv, inv, cosine, sine, start, seqs, blocks, rows, heads):
+    tokens = qkv.shape[0]
+    width = heads * HD
+    window = min(blocks * rows, rows + -(-MAX_DOC // rows) * rows)
+
+    def placed(cols):
+        return pl.BlockSpec((rows, cols), lambda s, i, place: (place[s * blocks + i], 0))
+
+    def natural(cols):
+        return pl.BlockSpec((rows, cols), lambda s, i, place: (s * blocks + i, 0))
+
+    return pl.pallas_call(
+        functools.partial(attend_kernel, rows, window, heads),
+        out_shape=(
+            jax.ShapeDtypeStruct((tokens, width), jnp.bfloat16),
+            jax.ShapeDtypeStruct((tokens, LANES), jnp.bfloat16),
+            jax.ShapeDtypeStruct((tokens, width), jnp.bfloat16),
+            jax.ShapeDtypeStruct((tokens, heads), jnp.float32),
+        ),
+        grid_spec=pltpu.PrefetchScalarGridSpec(
+            num_scalar_prefetch=1,
+            grid=(seqs, blocks),
+            in_specs=[placed(width + LANES), placed(1), natural(LANES), natural(LANES), natural(1)],
+            out_specs=[placed(width), placed(LANES), placed(width), placed(heads)],
+            scratch_shapes=[pltpu.VMEM((blocks * rows, LANES), jnp.bfloat16)] * 2,
+        ),
+        compiler_params=pltpu.CompilerParams(vmem_limit_bytes=48 << 20),
+        name="attend",
+    )(place, qkv, inv, cosine, sine, start)
+
+
+def attend_back(place, query, kv, lse, grad, inv, cosine, sine, start, seqs, blocks, rows, heads):
+    tokens = query.shape[0]
+    width = heads * HD
+    window = min(blocks * rows, rows + -(-MAX_DOC // rows) * rows)
+
+    def placed(cols):
+        return pl.BlockSpec(
+            (rows, cols), lambda s, i, place: (place[s * blocks + blocks - 1 - i], 0)
+        )
+
+    def natural(cols):
+        return pl.BlockSpec((rows, cols), lambda s, i, place: (s * blocks + blocks - 1 - i, 0))
+
+    return pl.pallas_call(
+        functools.partial(attend_back_kernel, rows, window, heads, blocks),
+        out_shape=jax.ShapeDtypeStruct((tokens, width + LANES), jnp.bfloat16),
+        grid_spec=pltpu.PrefetchScalarGridSpec(
+            num_scalar_prefetch=1,
+            grid=(seqs, blocks),
+            in_specs=[
+                placed(width),
+                pl.BlockSpec((tokens, LANES), lambda s, i, place: (0, 0)),
+                placed(heads),
+                placed(width),
+                placed(1),
+                natural(LANES),
+                natural(LANES),
+                natural(1),
+            ],
+            out_specs=placed(width + LANES),
+            scratch_shapes=[pltpu.VMEM((blocks * rows, LANES), jnp.bfloat16)] * 2
+            + [pltpu.VMEM((blocks * rows, LANES), jnp.float32)] * 2,
+        ),
+        compiler_params=pltpu.CompilerParams(vmem_limit_bytes=48 << 20),
+        name="attend_back",
+    )(place, query, kv, lse, grad, inv, cosine, sine, start)
+
+
+def tied(value, *others):
+    return lax.optimization_barrier((value, *others))[0]
+
+
+def group_shards(
+    group, cores,
+    hidden_in, segments, gain_attn, query_weight, key_weight, value_weight, out_weight,
+    gain_ffn, gate_weight, up_weight, down_weight, cotangent,
+):
+    bfloat = jnp.bfloat16
+    seqs_here, rows_here, width = hidden_in.shape
+    length = segments.shape[1]
+    rows = rows_here // cores
+    near = group // (length // rows_here)
+    blocks = length // rows
+    heads = HQ // KVH
+    me = lax.axis_index(("near", "ctx"))
+    me_core = lax.axis_index("tp")
+
+    def swap(value, m):
+        return lax.ppermute(value, ("near", "ctx"), [(i, i ^ m) for i in range(group)])
+
+    def swap_core(value):
+        return lax.ppermute(value, "tp", [(0, 1), (1, 0)])
+
+    def gather(own):
+        same = [own] + [swap(own, m) for m in range(1, group)]
+        return same, jnp.concatenate(same + [swap_core(v) for v in same], axis=0)
+
+    def scatter(product, left):
+        half = group * rows
+        other = swap_core(product(left[half:]).astype(bfloat))
+        mine = product(left[:half]) + other.astype(jnp.float32)
+        low = mine.astype(bfloat)
+        total = mine[:rows]
+        for m in range(1, group):
+            total = total + swap(low[m * rows : (m + 1) * rows], m).astype(jnp.float32)
+        return total
+
+    def own_half(value):
+        return lax.dynamic_slice_in_dim(value, me_core * rows, rows, 0)
+
+    def both_halves(own):
+        other = swap_core(own)
+        whole = jnp.zeros((rows_here, own.shape[1]), own.dtype)
+        whole = lax.dynamic_update_slice_in_dim(whole, own, me_core * rows, 0)
+        return lax.dynamic_update_slice_in_dim(whole, other, (1 - me_core) * rows, 0)
+
+    def to_columns(weight):
+        deep, cols = weight.shape[0], weight.shape[1] // group
+        whole = jnp.zeros((group * deep, cols), weight.dtype)
+        for m in range(group):
+            piece = lax.dynamic_slice_in_dim(weight, (me ^ m) * cols, cols, 1)
+            piece = swap(piece, m) if m else piece
+            whole = lax.dynamic_update_slice_in_dim(whole, piece, (me ^ m) * deep, 0)
+        return whole
+
+    def to_rows(grad):
+        deep, cols = grad.shape[0] // group, grad.shape[1]
+        whole = jnp.zeros((deep, group * cols), grad.dtype)
+        for m in range(group):
+            piece = lax.dynamic_slice_in_dim(grad, (me ^ m) * deep, deep, 0)
+            piece = swap(piece, m) if m else piece
+            whole = lax.dynamic_update_slice_in_dim(whole, piece, (me ^ m) * cols, 1)
+        return whole
+
+    def far_gather(weight):
+        return lax.all_gather(weight, "far", axis=0, tiled=True)
+
+    def far_scatter(grad):
+        low = lax.psum_scatter(grad.astype(bfloat), "far", scatter_dimension=0, tiled=True)
+        return to_rows(low).astype(jnp.float32)
+
+    deep = query_weight.shape[0]
+    col_gain_a, col_gain_f = gain_attn[:, None], gain_ffn[:, None]
+
+    def scaled(weight, gain):
+        return (weight.astype(jnp.float32) * gain).astype(bfloat)
+
+    def chunks(weight):
+        return weight.reshape(deep, group, weight.shape[1] // group)
+
+    attn_local = jnp.concatenate(
+        [
+            chunks(scaled(query_weight, col_gain_a)),
+            chunks(scaled(key_weight, col_gain_a)),
+            chunks(scaled(value_weight, col_gain_a)),
+            chunks(out_weight),
+        ],
+        axis=2,
+    ).reshape(deep, -1)
+    attn_cols = to_columns(attn_local)
+    attn_w = far_gather(attn_cols)
+    head_cols = heads * HD
+    in_w, out_w = attn_w[:, : head_cols + 2 * HD], attn_w[:, head_cols + 2 * HD :]
+
+    own_in = tied(own_half(hidden_in.reshape(rows_here, width)), attn_cols)
+    pieces, inputs = gather(own_in)
+    last = pieces[-1]
+    gate_cols = to_columns(tied(scaled(gate_weight, col_gain_f), last))
+    up_cols = to_columns(tied(scaled(up_weight, col_gain_f), gate_cols))
+    down_cols = to_columns(tied(down_weight, up_cols))
+    gate_w = far_gather(gate_cols)
+    up_w = far_gather(up_cols)
+    down_w = far_gather(down_cols)
+    own_cot = own_half(cotangent.reshape(rows_here, width))
+    _, cots = gather(tied(own_cot, down_cols))
+
+    seg_all = jnp.concatenate(
+        [segments]
+        + [swap(segments, n * (group // near)) for n in range(1, near)],
+        axis=0,
+    )
+    start = jnp.sum((seg_all[:, None, :] < seg_all[:, :, None]).astype(jnp.int32), axis=2)
+    places = (jnp.arange(length, dtype=jnp.int32)[None, :] - start).astype(jnp.float32)
+    freqs = THETA ** (-jnp.arange(0, HD, 2, dtype=jnp.float32) / HD)
+    phase = places.reshape(-1)[:, None] * freqs
+    cosine, sine = jnp.cos(phase), jnp.sin(phase)
+    cosine = jnp.concatenate([cosine, cosine, cosine, cosine], axis=1)
+    sine = jnp.concatenate([-sine, sine, -sine, sine], axis=1)
+    start = start.reshape(-1)[:, None]
+    at = jnp.arange(near * blocks, dtype=jnp.int32)
+    in_seq = at % blocks
+    here_ctx = lax.axis_index("ctx")
+    place = (
+        ((in_seq % cores) ^ me_core) * group
+        + (at // blocks) * (group // near)
+        + ((in_seq // cores) ^ here_ctx)
+    ).astype(jnp.int32)
+
+    def inverse_rms(values):
+        values = values.astype(jnp.float32)
+        return lax.rsqrt(jnp.mean(values * values, axis=-1, keepdims=True) + EPSILON)
+
+    inv_a = inverse_rms(inputs)
+    qkv = matmul_low(inputs, in_w)
+    query, kv, mixed, lse = attend(
+        place, qkv, inv_a, cosine, sine, start, near, blocks, rows, heads
+    )
+    branch_a = scatter(lambda left: matmul_trans(left, out_w), mixed)
+    own_f = own_in.astype(jnp.float32)
+    middle = own_f + RESIDUAL * branch_a
+
+    _, mids = gather(middle.astype(bfloat))
+    inv_f = inverse_rms(mids)
+    gate_pre = matmul_low(mids, gate_w) * inv_f
+    upward = matmul_low(mids, up_w) * inv_f
+    sigma = jax.nn.sigmoid(gate_pre)
+    active = gate_pre * sigma
+    hidden = (active * upward).astype(bfloat)
+    branch_f = scatter(lambda left: matmul_trans(left, down_w), hidden)
+    layer_out = both_halves((middle + RESIDUAL * branch_f).astype(bfloat))
+    grad_down = far_scatter(matmul_outer(cots, hidden)) * RESIDUAL
+    d_hidden = matmul_low(cots, down_w) * RESIDUAL
+    d_gate = (inv_f * (d_hidden * upward * sigma * (1.0 + gate_pre * (1.0 - sigma)))).astype(bfloat)
+    d_up = (inv_f * (d_hidden * active)).astype(bfloat)
+    grad_gate = far_scatter(matmul_outer(mids, d_gate))
+    grad_up = far_scatter(matmul_outer(mids, d_up))
+    both = jnp.concatenate([d_gate, d_up], axis=1)
+    back_f = scatter(
+        lambda left: matmul_trans(left[:, : d_gate.shape[1]], gate_w)
+        + matmul_trans(left[:, d_gate.shape[1] :], up_w),
+        both,
+    )
+
+    def through_norm(grad, unit):
+        return grad - unit * jnp.mean(grad * unit, axis=-1, keepdims=True)
+
+    d_middle = own_cot.astype(jnp.float32) + through_norm(back_f, middle * inverse_rms(middle))
+
+    _, d_mids = gather(d_middle.astype(bfloat))
+    d_mixed = (matmul_low(d_mids, out_w) * RESIDUAL).astype(bfloat)
+    grad_out_part = matmul_outer(d_mids, mixed) * RESIDUAL
+    d_qkv = attend_back(
+        place, query, kv, lse, d_mixed, inv_a, cosine, sine, start, near, blocks, rows, heads
+    )
+    grad_attn = jnp.concatenate(
+        [matmul_outer(inputs, d_qkv).astype(bfloat), grad_out_part.astype(bfloat)], axis=1
+    )
+    grad_attn = far_scatter(grad_attn).reshape(deep, group, -1)
+    back_a = scatter(lambda left: matmul_trans(left, in_w), d_qkv)
+    input_grad = d_middle + through_norm(back_a, own_f * inverse_rms(own_f))
+    input_grad = both_halves(input_grad)
+
+    def cut(first, size):
+        return grad_attn[:, :, first : first + size].reshape(deep, group * size)
+
+    grad_query, grad_key, grad_value, grad_out = (
+        cut(0, head_cols),
+        cut(head_cols, HD),
+        cut(head_cols + HD, HD),
+        cut(head_cols + 2 * HD, head_cols),
+    )
+
+    def row_sum(*pairs):
+        return sum(jnp.sum(weight.astype(jnp.float32) * grad, axis=1) for weight, grad in pairs)
+
+    gain_grads = jnp.stack(
+        [
+            row_sum(
+                (query_weight, grad_query), (key_weight, grad_key), (value_weight, grad_value)
+            ),
+            row_sum((gate_weight, grad_gate), (up_weight, grad_up)),
+        ]
+    )
+    gain_grads = gain_grads + swap_core(gain_grads)
+    return (
+        layer_out.reshape(hidden_in.shape),
+        input_grad.reshape(hidden_in.shape),
+        gain_grads[0],
+        grad_query * col_gain_a,
+        grad_key * col_gain_a,
+        grad_value * col_gain_a,
+        grad_out,
+        gain_grads[1],
+        grad_gate * col_gain_f,
+        grad_up * col_gain_f,
+        grad_down,
+    )
+
+
 def solution(mesh):
+    sizes = dict(mesh.shape)
+    fsdp, ctx, tp = sizes["fsdp"], sizes["ctx"], sizes["tp"]
+    near = KVH // (ctx * tp)
+    group = near * ctx
+    fits = (
+        tuple(mesh.axis_names) == ("fsdp", "ctx", "tp")
+        and tp == 2
+        and near > 0
+        and group * tp == KVH
+        and fsdp % near == 0
+        and group & (group - 1) == 0
+    )
+    if fits:
+        mesh = Mesh(
+            mesh.devices.reshape(fsdp // near, near, ctx, tp), ("far", "near", "ctx", "tp")
+        )
+        body, data = functools.partial(group_shards, group, tp), ("far", "near")
+    else:
+        body, data = generic_shards, ("fsdp",)
+    owner = (*data, "ctx")
+    weight, gain, tokens = P(owner, "tp"), P(owner), P(data, "ctx", None)
     in_specs = (
-        P("fsdp", "ctx", None),
-        P("fsdp", None),
-        P(("fsdp", "ctx")),
-        P(("fsdp", "ctx"), "tp"),
-        P(("fsdp", "ctx"), "tp"),
-        P(("fsdp", "ctx"), "tp"),
-        P(("fsdp", "ctx"), "tp"),
-        P(("fsdp", "ctx")),
-        P(("fsdp", "ctx"), "tp"),
-        P(("fsdp", "ctx"), "tp"),
-        P(("fsdp", "ctx"), "tp"),
-        P("fsdp", "ctx", None),
+        tokens,
+        P(data, None),
+        gain,
+        weight,
+        weight,
+        weight,
+        weight,
+        gain,
+        weight,
+        weight,
+        weight,
+        tokens,
     )
     out_specs = (
-        P("fsdp", "ctx", None),
-        P("fsdp", "ctx", None),
-        P(("fsdp", "ctx")),
-        P(("fsdp", "ctx"), "tp"),
-        P(("fsdp", "ctx"), "tp"),
-        P(("fsdp", "ctx"), "tp"),
-        P(("fsdp", "ctx"), "tp"),
-        P(("fsdp", "ctx")),
-        P(("fsdp", "ctx"), "tp"),
-        P(("fsdp", "ctx"), "tp"),
-        P(("fsdp", "ctx"), "tp"),
-    )
-    return jax.shard_map(shards, mesh=mesh, in_specs=in_specs, out_specs=out_specs, check_vma=False)
+        tokens,
+        tokens,
+        gain,
+        weight,
+        weight,
+        weight,
+        weight,
+        gain,
+        weight,
+        weight,
+        weight,
+    )
+    return jax.shard_map(body, mesh=mesh, in_specs=in_specs, out_specs=out_specs, check_vma=False)

time: 3730 us -> 788 us (0.21)
  waiting for transfers between devices: 3150 us -> 304 us
  blocking collectives: 172 us -> 0 us
  matrix products: 295 us -> 197 us
  local copies, waits for them, and re-layouts: 9.68 us -> 84.2 us
  starting transfers between devices: 1.38 us -> 62.8 us
  Pallas kernels: 0 us -> 53.3 us
    reduce_scatter x9 -> x4, waiting for transfers between devices: 2460 us -> 0.01 us  [far_scatter(): lax.psum_scatter(grad.astype(bfloat), 'far', scatter_dimension=0, tiled=T...]
    all_gather x7 -> x4, waiting for transfers between devices: 679 us -> 0.03 us  [far_gather(): return lax.all_gather(weight, 'far', axis=0, tiled=True)]
    ppermute x0 -> x72, waiting for transfers between devices: none -> 304 us  [the longest x49 299 us: swap(): lax.ppermute(value, ('near', 'ctx'), [(i, i ^ m) for i in range(group)])]
    all_gather x4 -> x0, blocking collectives: 95.2 us -> none  [the longest x1 42.2 us: shards(): lax.all_gather(gain_attn.astype(jnp.bfloat16), ('fsdp', 'ctx'), axis=0, t...]
    dot_general x6 -> x0, matrix products: 86 us -> none  [the longest x1 22.1 us: shards(): jnp.einsum('srngd,slnd->sngrl', d_mixed, value_all, preferred_element_typ...]
    unnamed x1 -> x0, blocking collectives: 76.8 us -> none
    ppermute x0 -> x72, starting transfers between devices: none -> 61.8 us  [the longest x49 59 us: swap(): lax.ppermute(value, ('near', 'ctx'), [(i, i ^ m) for i in range(group)])]
    pallas_call x0 -> x2, Pallas kernels: none -> 53.3 us  [the longest x1 32.6 us: attend_back(): pl.pallas_call(functools.partial(attend_back_kernel, rows, window, heads,...]
  transfers between devices with their start and end apart: 19 -> 80, of which waited for: 15 -> 32; matrix products, arithmetic and copies ran while one was open for 6% -> 37% of each run, Pallas kernels for 0% -> 7%
where the time goes in v1:
time: 788 us; the launch traced here: 779 us
  waiting for transfers between devices  304 us (39%)
  matrix products  197 us (25%)
  local copies, waits for them, and re-layouts  84.2 us (11%)
  starting transfers between devices  62.8 us (8%)
  other arithmetic  62 us (8%)
  Pallas kernels  53.3 us (7%)
  between operations  15.7 us (2%)
    ppermute x49, waiting for transfers between devices, swap(): lax.ppermute(value, ('near', 'ctx'), [(i, i ^ m) for i in range(group)])  299 us
    dot_general x10, matrix products, matmul_trans(): lax.dot_general(left, right, (((1,), (1,)), ((), ())), preferred_element_...  81.1 us
    dot_general x5, matrix products, matmul_low(): return jnp.dot(left, right, preferred_element_type=jnp.float32)  67.1 us
    ppermute x49, starting transfers between devices, swap(): lax.ppermute(value, ('near', 'ctx'), [(i, i ^ m) for i in range(group)])  59 us
    dot_general x5, matrix products, matmul_outer(): lax.dot_general(left, right, (((0,), (0,)), ((), ())), preferred_element_...  48.9 us
    unnamed x143, local copies, waits for them, and re-layouts  39.8 us
    pallas_call x1, Pallas kernels, attend_back(): pl.pallas_call(functools.partial(attend_back_kernel, rows, window, heads,...  32.6 us
    pallas_call x1, Pallas kernels, attend(): pl.pallas_call(functools.partial(attend_kernel, rows, window, heads), out...  20.7 us
  transfers between devices with their start and end apart: 80, of which 32 were waited for; matrix products, arithmetic and copies ran while one was open for 37% of the time, Pallas kernels for 7%

profile of v1, /device:TPU:0, one launch (start us, length us, event | category | flops | bytes accessed | tf_op | source)
XLA Modules:
  0.0 779.5 jit_solution(17949569197343938704)
XLA Ops:
  22.4 4.1 collective-permute-done.1
  31.3 21.3 %collective-permute-done.5 = bf16[256,2048]{1,0:T(8,128)(2,1)} collective-permute-done((bf16[256,2048]{1,0:T(8,128)(2,1)S(1)}, bf16[256,2048]{1,0:T(8,128)(2,1)}, u32[]{:S(2)}, u32[]{:S(2)}) %collective-permute-start.5) | collective-permute-done | bytes 1048608 | tf_op jit(solution)/shard_map/ppermute | solution.py:519
  56.4 5.4 collective-permute-done.22
  61.8 4.1 collective-permute-done.23
  75.3 3.7 fusion.47
  83.2 11.1 %collective-permute-done.3 = bf16[256,2048]{1,0:T(8,128)(2,1)} collective-permute-done((bf16[256,2048]{1,0:T(8,128)(2,1)S(1)}, bf16[256,2048]{1,0:T(8,128)(2,1)}, u32[]{:S(2)}, u32[]{:S(2)}) %collective-permute-start.3) | collective-permute-done | bytes 1048608 | tf_op jit(solution)/shard_map/ppermute | solution.py:519
  110.7 8.2 %collective-permute-done.26 = bf16[128,1024]{1,0:T(8,128)(2,1)S(1)} collective-permute-done((bf16[128,1024]{1,0:T(8,128)(2,1)S(1)}, bf16[128,1024]{1,0:T(8,128)(2,1)S(1)}, u32[]{:S(2)}, u32[]{:S(2)}) %collective-permute-start.26) | collective-permute-done | bytes 262176 | tf_op jit(solution)/shard_map/ppermute | solution.py:519
  127.7 5.1 multiply_reduce_fusion.1
  133.2 10.0 %fusion.36.qkv_ref = f32[2048,384]{1,0:T(8,128)} fusion(bf16[2048,2048]{1,0:T(8,128)(2,1)} %constant_dynamic-update-slice_fusion, bf16[2048,640]{1,0:T(8,128)(2,1)} %all-gather.5.cloned.1.call-done), kind=kOutput, calls=%fused_computation.79 | convolution fusion | flops 3221225472 | bytes 13107200 | tf_op jit(solution)/shard_map/dot_general | solution.py:29
  143.2 20.7 %attend.1 = (bf16[2048,256]{1,0:T(8,128)(2,1)S(1)}, bf16[2048,128]{1,0:T(8,128)(2,1)S(1)}, bf16[2048,256]{1,0:T(8,128)(2,1)S(1)}, f32[2048,4]{1,0:T(8,128)S(1)}) custom-call(s32[8]{0:T(128)S(1)} %fusion.55.place_ref, f32[2048,384]{1,0:T(8,128)} %fusion.36.qkv_ref, f32[2048,1]{1,0:T(8,128)S(1)} %copy.60.inv_ref, f32[2048,128]{1,0:T(8,128)S(1)} %get-tuple-element.156.cos_ref, ...), custom_call_target="tpu_custom_call" | custom-call | tf_op jit(solution)/shard_map/attend/pallas_call | solution.py:441
  163.9 5.5 convolution_convert_fusion.1
  176.1 4.5 collective-permute-done.28
  181.3 4.8 collective-permute-done.29
  191.0 7.2 fusion.67
  202.1 11.8 %collective-permute-done.36 = bf16[256,2048]{1,0:T(8,128)(2,1)} collective-permute-done((bf16[256,2048]{1,0:T(8,128)(2,1)}, bf16[256,2048]{1,0:T(8,128)(2,1)}, u32[]{:S(2)}, u32[]{:S(2)}) %collective-permute-start.36) | collective-permute-done | bytes 1048608 | tf_op jit(solution)/shard_map/ppermute | solution.py:519
  218.6 18.0 %collective-permute-done.37 = bf16[256,2048]{1,0:T(8,128)(2,1)} collective-permute-done((bf16[256,2048]{1,0:T(8,128)(2,1)}, bf16[256,2048]{1,0:T(8,128)(2,1)}, u32[]{:S(2)}, u32[]{:S(2)}) %collective-permute-start.37) | collective-permute-done | bytes 1048608 | tf_op jit(solution)/shard_map/ppermute | solution.py:519
  237.7 21.2 %collective-permute-done.12 = bf16[256,2048]{1,0:T(8,128)(2,1)} collective-permute-done((bf16[256,2048]{1,0:T(8,128)(2,1)}, bf16[256,2048]{1,0:T(8,128)(2,1)}, u32[]{:S(2)}, u32[]{:S(2)}) %collective-permute-start.12) | collective-permute-done | bytes 1048608 | tf_op jit(solution)/shard_map/ppermute | solution.py:519
  258.9 21.7 %collective-permute-done.13 = bf16[256,2048]{1,0:T(8,128)(2,1)} collective-permute-done((bf16[256,2048]{1,0:T(8,128)(2,1)}, bf16[256,2048]{1,0:T(8,128)(2,1)}, u32[]{:S(2)}, u32[]{:S(2)}) %collective-permute-start.13) | collective-permute-done | bytes 1048608 | tf_op jit(solution)/shard_map/ppermute | solution.py:519
  280.6 4.1 multiply_reduce_fusion.3
  291.8 19.3 %collective-permute-done.15 = bf16[256,2048]{1,0:T(8,128)(2,1)S(1)} collective-permute-done((bf16[256,2048]{1,0:T(8,128)(2,1)S(1)}, bf16[256,2048]{1,0:T(8,128)(2,1)S(1)}, u32[]{:S(2)}, u32[]{:S(2)}) %collective-permute-start.15) | collective-permute-done | bytes 1048608 | tf_op jit(solution)/shard_map/ppermute | solution.py:519
  311.2 23.7 %collective-permute-done.16 = bf16[256,2048]{1,0:T(8,128)(2,1)S(1)} collective-permute-done((bf16[256,2048]{1,0:T(8,128)(2,1)S(1)}, bf16[256,2048]{1,0:T(8,128)(2,1)S(1)}, u32[]{:S(2)}, u32[]{:S(2)}) %collective-permute-start.16) | collective-permute-done | bytes 1048608 | tf_op jit(solution)/shard_map/ppermute | solution.py:519
  342.5 14.4 %fusion.70 = f32[2048,1024]{1,0:T(8,128)} fusion(bf16[2048,2048]{1,0:T(8,128)(2,1)} %copy-done.16, bf16[2048,1024]{1,0:T(8,128)(2,1)} %all-gather.7.cloned.1.call-done), kind=kOutput, calls=%fused_computation.239 | convolution fusion | flops 8589934592 | bytes 20971520 | tf_op jit(solution)/shard_map/dot_general | solution.py:29
  357.0 14.4 %fusion.71 = f32[2048,1024]{1,0:T(8,128)} fusion(bf16[2048,2048]{1,0:T(8,128)(2,1)} %copy-done.16, bf16[2048,1024]{1,0:T(8,128)(2,1)} %all-gather.9.cloned.1.call-done), kind=kOutput, calls=%fused_computation.240 | convolution fusion | flops 8589934592 | bytes 20971520 | tf_op jit(solution)/shard_map/dot_general | solution.py:29
  371.4 22.1 %multiply_convert_fusion.1 = (bf16[2048,1024]{1,0:T(8,128)(2,1)}, bf16[2048,1024]{1,0:T(8,128)(2,1)S(1)}, bf16[2048,1024]{1,0:T(8,128)(2,1)}) fusion(f32[2048,1024]{1,0:T(8,128)} %fusion.71, f32[2048,1024]{1,0:T(8,128)} %fusion.70, f32[2048]{0:T(1024)S(1)} %add_rsqrt_fusion, bf16[2048,2048]{1,0:T(8,128)(2,1)} %copy-done.37, ...), kind=kOutput, calls=%fused_computation.6 | convolution fusion | flops 8631877632 | bytes 41951232 | tf_op jit(solution)/shard_map/dot_general | solution.py:29
  395.6 13.0 %convolution_convert_fusion.3 = bf16[2048,1024]{1,0:T(8,128)(2,1)} fusion(bf16[2048,2048]{1,0:T(8,128)(2,1)} %copy-done.37, bf16[2048,1024]{1,0:T(8,128)(2,1)S(1)} %get-tuple-element.76), kind=kOutput, calls=%fused_computation.16 | convolution fusion | flops 8592031744 | bytes 16777216 | tf_op jit(solution)/shard_map/dot_general | solution.py:39
  408.7 14.0 %convolution_convert_fusion.5 = bf16[2048,1024]{1,0:T(8,128)(2,1)} fusion(bf16[2048,2048]{1,0:T(8,128)(2,1)} %copy-done.16, bf16[2048,1024]{1,0:T(8,128)(2,1)} %get-tuple-element.75), kind=kOutput, calls=%fused_computation.18 | convolution fusion | flops 8592031744 | bytes 16777216 | tf_op jit(solution)/shard_map/dot_general | solution.py:39
  422.7 10.9 %fusion.17 = f32[1024,2048]{1,0:T(8,128)} fusion(bf16[2048,1024]{1,0:T(8,128)(2,1)} %all-gather.9.cloned.1.call-done, bf16[2048,1024]{1,0:T(8,128)(2,1)} %get-tuple-element.77), kind=kOutput, calls=%fused_computation.50 | convolution fusion | flops 4294967296 | bytes 14680064 | tf_op jit(solution)/shard_map/dot_general | solution.py:33
  433.6 8.8 %add_convert_fusion = bf16[1024,2048]{1,0:T(8,128)(2,1)} fusion(f32[1024,2048]{1,0:T(8,128)} %fusion.17, bf16[2048,1024]{1,0:T(8,128)(2,1)S(1)} %copy-done.45, bf16[2048,1024]{1,0:T(8,128)(2,1)S(1)} %copy-done.50), kind=kOutput, calls=%fused_computation.4 | convolution fusion | flops 4299161600 | bytes 18874368 | tf_op jit(solution)/shard_map/dot_general | solution.py:33
  442.6 7.9 %convolution_convert_fusion.2 = bf16[1024,2048]{1,0:T(8,128)(2,1)} fusion(bf16[2048,1024]{1,0:T(8,128)(2,1)S(1)} %copy-done.47, bf16[2048,1024]{1,0:T(8,128)(2,1)} %copy-done.48), kind=kOutput, calls=%fused_computation.15 | convolution fusion | flops 4297064448 | bytes 10485760 | tf_op jit(solution)/shard_map/dot_general | solution.py:33
  450.9 8.4 %fusion.20 = f32[1024,2048]{1,0:T(8,128)} fusion(bf16[2048,1024]{1,0:T(8,128)(2,1)S(1)} %copy-done.46, bf16[2048,1024]{1,0:T(8,128)(2,1)} %get-tuple-element.77), kind=kOutput, calls=%fused_computation.53 | convolution fusion | flops 4294967296 | bytes 14680064 | tf_op jit(solution)/shard_map/dot_general | solution.py:33
  459.3 6.7 fusion.22
  466.0 9.6 %fusion.59 = (bf16[1024,2048]{1,0:T(8,128)(2,1)S(1)}, f32[1024,2048]{1,0:T(8,128)}) fusion(bf16[1024,2048]{1,0:T(8,128)(2,1)S(1)} %collective-permute-done.43, f32[1024,2048]{1,0:T(8,128)} %fusion.22, f32[1024,2048]{1,0:T(8,128)} %fusion.20), kind=kLoop, calls=%fused_computation.229 | loop fusion | flops 8388608 | bytes 33554432 | tf_op jit(solution)/shard_map/convert_element_type | solution.py:532
  480.9 11.3 %convolution_convert_fusion.4 = bf16[2048,1024]{1,0:T(8,128)(2,1)} fusion(bf16[2048,2048]{1,0:T(8,128)(2,1)S(1)} %bitcast.71, bf16[2048,1024]{1,0:T(8,128)(2,1)S(1)} %copy-done.49), kind=kOutput, calls=%fused_computation.17 | convolution fusion | flops 8592031744 | bytes 16777216 | tf_op jit(solution)/shard_map/dot_general | solution.py:39
  492.9 10.7 %collective-permute-done.44 = bf16[256,2048]{1,0:T(8,128)(2,1)S(1)} collective-permute-done((bf16[256,2048]{1,0:T(8,128)(2,1)}, bf16[256,2048]{1,0:T(8,128)(2,1)S(1)}, u32[]{:S(2)}, u32[]{:S(2)}) %collective-permute-start.44) | collective-permute-done | bytes 1048608 | tf_op jit(solution)/shard_map/ppermute | solution.py:519
  503.6 22.9 %collective-permute-done.45 = bf16[256,2048]{1,0:T(8,128)(2,1)} collective-permute-done((bf16[256,2048]{1,0:T(8,128)(2,1)}, bf16[256,2048]{1,0:T(8,128)(2,1)}, u32[]{:S(2)}, u32[]{:S(2)}) %collective-permute-start.45) | collective-permute-done | bytes 1048608 | tf_op jit(solution)/shard_map/ppermute | solution.py:519
  530.1 4.8 constant_dynamic-update-slice_fusion.31
  538.3 12.0 %fusion.68 = (bf16[1024,2048]{1,0:T(8,128)(2,1)S(1)}, f32[1024,2048]{1,0:T(8,128)}) fusion(bf16[1024,2048]{1,0:T(8,128)(2,1)} %collective-permute-done.31, bf16[2048,1024]{1,0:T(8,128)(2,1)} %all-gather.11.cloned.1.call-done, bf16[2048,1024]{1,0:T(8,128)(2,1)} %copy-done.48), kind=kOutput, calls=%fused_computation.237 | convolution fusion | flops 4301258752 | bytes 23068672 | tf_op jit(solution)/shard_map/dot_general | solution.py:33
  550.4 10.6 %collective-permute-done.47 = bf16[256,2048]{1,0:T(8,128)(2,1)S(1)} collective-permute-done((bf16[256,2048]{1,0:T(8,128)(2,1)S(1)}, bf16[256,2048]{1,0:T(8,128)(2,1)S(1)}, u32[]{:S(2)}, u32[]{:S(2)}) %collective-permute-start.47) | collective-permute-done | bytes 1048608 | tf_op jit(solution)/shard_map/ppermute | solution.py:519
  563.8 19.6 %collective-permute-done.49 = bf16[256,2048]{1,0:T(8,128)(2,1)S(1)} collective-permute-done((bf16[256,2048]{1,0:T(8,128)(2,1)S(1)}, bf16[256,2048]{1,0:T(8,128)(2,1)S(1)}, u32[]{:S(2)}, u32[]{:S(2)}) %collective-permute-start.49) | collective-permute-done | bytes 1048608 | tf_op jit(solution)/shard_map/ppermute | solution.py:519
  595.7 6.1 fusion.1.grad_ref
  601.8 32.6 %attend_back.1 = bf16[2048,384]{1,0:T(8,128)(2,1)} custom-call(s32[8]{0:T(128)S(1)} %fusion.55.place_ref, bf16[2048,256]{1,0:T(8,128)(2,1)S(1)} %copy-done.5, bf16[2048,128]{1,0:T(8,128)(2,1)S(1)} %copy-done.9, f32[2048,4]{1,0:T(8,128)S(1)} %copy-done.7, bf16[2048,256]{1,0:T(8,128)(2,1)S(1)} %fusion.1.grad_ref, f32[2048,1]{1,0:T(8,128)S(1)} %copy.60.inv_ref, ...), custom_call_target="tpu_custom_call" | custom-call | tf_op jit(solution)/shard_map/attend_back/pallas_call | solution.py:474
  634.5 5.6 convolution_convert_fusion
  640.1 6.9 convolution_convert_fusion.6
  691.2 7.9 %fusion.69 = (bf16[1024,2048]{1,0:T(8,128)(2,1)S(1)}, f32[1024,2048]{1,0:T(8,128)}) fusion(bf16[1024,2048]{1,0:T(8,128)(2,1)} %collective-permute-done.54, bf16[2048,640]{1,0:T(8,128)(2,1)S(1)} %copy-done.19, bf16[2048,384]{1,0:T(8,128)(2,1)S(1)} %copy-done.26), kind=kOutput, calls=%fused_computation.238 | convolution fusion | flops 1616904192 | bytes 19136512 | tf_op jit(solution)/shard_map/dot_general | solution.py:33
  704.5 4.4 convert_multiply_fusion.2
  711.6 15.6 %collective-permute-done.55 = bf16[256,2048]{1,0:T(8,128)(2,1)S(1)} collective-permute-done((bf16[256,2048]{1,0:T(8,128)(2,1)}, bf16[256,2048]{1,0:T(8,128)(2,1)S(1)}, u32[]{:S(2)}, u32[]{:S(2)}) %collective-permute-start.55) | collective-permute-done | bytes 1048608 | tf_op jit(solution)/shard_map/ppermute | solution.py:519
  727.3 24.5 %collective-permute-done.56 = bf16[256,2048]{1,0:T(8,128)(2,1)S(1)} collective-permute-done((bf16[256,2048]{1,0:T(8,128)(2,1)}, bf16[256,2048]{1,0:T(8,128)(2,1)S(1)}, u32[]{:S(2)}, u32[]{:S(2)}) %collective-permute-start.56) | collective-permute-done | bytes 1048608 | tf_op jit(solution)/shard_map/ppermute | solution.py:519
  755.4 4.6 bitcast_dynamic-update-slice_fusion.1
  (386 shorter events, 197.6 us)
Async XLA Ops:
  7.2 126.0 %all-gather.5.cloned.1.call-start = ((), (), s32[]{:S(2)}) async-start(), calls=%async_computation.4 | async-start | bytes 3276800 | tf_op jit(solution)/shard_map/all_gather | solution.py:566
  27.5 315.0 %all-gather.7.cloned.1.call-start = ((), (), s32[]{:S(2)}) async-start(), calls=%async_computation.5 | async-start | bytes 5242880 | tf_op jit(solution)/shard_map/all_gather | solution.py:566
  27.7 24.9 %collective-permute-start.5 = (bf16[256,2048]{1,0:T(8,128)(2,1)S(1)}, bf16[256,2048]{1,0:T(8,128)(2,1)}, u32[]{:S(2)}, u32[]{:S(2)}) collective-permute-start(bf16[256,2048]{1,0:T(8,128)(2,1)S(1)} %dynamic-slice_bitcast_fusion.1), channel_id=1, source_target_pairs={{0,6},{2,4},{4,2},{6,0},{1,7},{3,5},{5,3},{7,1},{8,14},{10,12},{12... | collective-permute-start | bytes 3145736 | tf_op jit(solution)/shard_map/ppermute | solution.py:519
  66.9 290.1 %all-gather.9.cloned.1.call-start = ((), (), s32[]{:S(2)}) async-start(), calls=%async_computation.6 | async-start | bytes 5242880 | tf_op jit(solution)/shard_map/all_gather | solution.py:566
  82.7 42.7 %collective-permute-start.9 = (bf16[256,2048]{1,0:T(8,128)(2,1)}, bf16[256,2048]{1,0:T(8,128)(2,1)}, u32[]{:S(2)}, u32[]{:S(2)}) collective-permute-start(bf16[256,2048]{1,0:T(8,128)(2,1)} %collective-permute-done.5), channel_id=1, source_target_pairs={{0,1},{1,0},{2,3},{3,2},{4,5},{5,4},{6,7},{7,6},{8,9},{9,8},{10,11... | collective-permute-start | bytes 3145736 | tf_op jit(solution)/shard_map/ppermute | solution.py:522
  94.3 26.4 %collective-permute-start.7 = (bf16[256,2048]{1,0:T(8,128)(2,1)}, bf16[256,2048]{1,0:T(8,128)(2,1)}, u32[]{:S(2)}, u32[]{:S(2)}) collective-permute-start(bf16[256,2048]{1,0:T(8,128)(2,1)} %collective-permute-done.3), channel_id=1, source_target_pairs={{0,1},{1,0},{2,3},{3,2},{4,5},{5,4},{6,7},{7,6},{8,9},{9,8},{10,11... | collective-permute-start | bytes 3145736 | tf_op jit(solution)/shard_map/ppermute | solution.py:522
  94.5 28.5 %collective-permute-start.8 = (bf16[256,2048]{1,0:T(8,128)(2,1)}, bf16[256,2048]{1,0:T(8,128)(2,1)}, u32[]{:S(2)}, u32[]{:S(2)}) collective-permute-start(bf16[256,2048]{1,0:T(8,128)(2,1)} %collective-permute-done.4), channel_id=1, source_target_pairs={{0,1},{1,0},{2,3},{3,2},{4,5},{5,4},{6,7},{7,6},{8,9},{9,8},{10,11... | collective-permute-start | bytes 3145736 | tf_op jit(solution)/shard_map/ppermute | solution.py:522
  120.4 251.0 %all-gather.11.cloned.1.call-start = ((), (), s32[]{:S(2)}) async-start(), calls=%async_computation.7 | async-start | bytes 5242880 | tf_op jit(solution)/shard_map/all_gather | solution.py:566
  187.5 26.4 %collective-permute-start.36 = (bf16[256,2048]{1,0:T(8,128)(2,1)}, bf16[256,2048]{1,0:T(8,128)(2,1)}, u32[]{:S(2)}, u32[]{:S(2)}) collective-permute-start(bf16[256,2048]{1,0:T(8,128)(2,1)} %dynamic-slice_bitcast_fusion), channel_id=1, source_target_pairs={{0,2},{2,0},{4,6},{6,4},{1,3},{3,1},{5,7},{7,5},{8,10},{10,8},{12,... | collective-permute-start | bytes 3145736 | tf_op jit(solution)/shard_map/ppermute | solution.py:519
  188.3 48.4 %collective-permute-start.37 = (bf16[256,2048]{1,0:T(8,128)(2,1)}, bf16[256,2048]{1,0:T(8,128)(2,1)}, u32[]{:S(2)}, u32[]{:S(2)}) collective-permute-start(bf16[256,2048]{1,0:T(8,128)(2,1)} %dynamic-slice_bitcast_fusion), channel_id=1, source_target_pairs={{0,4},{2,6},{4,0},{6,2},{1,5},{3,7},{5,1},{7,3},{8,12},{10,14},{12... | collective-permute-start | bytes 3145736 | tf_op jit(solution)/shard_map/ppermute | solution.py:519
  189.6 48.1 %collective-permute-start.38 = (bf16[256,2048]{1,0:T(8,128)(2,1)}, bf16[256,2048]{1,0:T(8,128)(2,1)}, u32[]{:S(2)}, u32[]{:S(2)}) collective-permute-start(bf16[256,2048]{1,0:T(8,128)(2,1)} %dynamic-slice_bitcast_fusion), channel_id=1, source_target_pairs={{0,6},{2,4},{4,2},{6,0},{1,7},{3,5},{5,3},{7,1},{8,14},{10,12},{12... | collective-permute-start | bytes 3145736 | tf_op jit(solution)/shard_map/ppermute | solution.py:519
  200.0 58.9 %collective-permute-start.12 = (bf16[256,2048]{1,0:T(8,128)(2,1)}, bf16[256,2048]{1,0:T(8,128)(2,1)}, u32[]{:S(2)}, u32[]{:S(2)}) collective-permute-start(bf16[256,2048]{1,0:T(8,128)(2,1)} %get-tuple-element.87), channel_id=1, source_target_pairs={{0,2},{2,0},{4,6},{6,4},{1,3},{3,1},{5,7},{7,5},{8,10},{10,8},{12,... | collective-permute-start | bytes 3145736 | tf_op jit(solution)/shard_map/ppermute | solution.py:519
  200.8 79.8 %collective-permute-start.13 = (bf16[256,2048]{1,0:T(8,128)(2,1)}, bf16[256,2048]{1,0:T(8,128)(2,1)}, u32[]{:S(2)}, u32[]{:S(2)}) collective-permute-start(bf16[256,2048]{1,0:T(8,128)(2,1)} %get-tuple-element.89), channel_id=1, source_target_pairs={{0,4},{2,6},{4,0},{6,2},{1,5},{3,7},{5,1},{7,3},{8,12},{10,14},{12... | collective-permute-start | bytes 3145736 | tf_op jit(solution)/shard_map/ppermute | solution.py:519
  213.9 66.7 %collective-permute-start.14 = (bf16[256,2048]{1,0:T(8,128)(2,1)}, bf16[256,2048]{1,0:T(8,128)(2,1)}, u32[]{:S(2)}, u32[]{:S(2)}) collective-permute-start(bf16[256,2048]{1,0:T(8,128)(2,1)} %get-tuple-element.88), channel_id=1, source_target_pairs={{0,6},{2,4},{4,2},{6,0},{1,7},{3,5},{5,3},{7,1},{8,14},{10,12},{12... | collective-permute-start | bytes 3145736 | tf_op jit(solution)/shard_map/ppermute | solution.py:519
  215.5 442.7 %reduce-scatter.11.cloned.1.call-start = ((), (), s32[]{:S(2)}) async-start(), calls=%async_computation.11 | async-start | bytes 5242880 | tf_op jit(solution)/shard_map/reduce_scatter | solution.py:569
  236.7 50.1 %collective-permute-start.39 = (bf16[256,2048]{1,0:T(8,128)(2,1)S(1)}, bf16[256,2048]{1,0:T(8,128)(2,1)S(1)}, u32[]{:S(2)}, u32[]{:S(2)}) collective-permute-start(bf16[256,2048]{1,0:T(8,128)(2,1)S(1)} %copy-done.22), channel_id=1, source_target_pairs={{0,1},{1,0},{2,3},{3,2},{4,5},{5,4},{6,7},{7,6},{8,9},{9,8},{10,11... | collective-permute-start | bytes 3145736 | tf_op jit(solution)/shard_map/ppermute | solution.py:522
  237.7 51.9 %collective-permute-start.40 = (bf16[256,2048]{1,0:T(8,128)(2,1)}, bf16[256,2048]{1,0:T(8,128)(2,1)S(1)}, u32[]{:S(2)}, u32[]{:S(2)}) collective-permute-start(bf16[256,2048]{1,0:T(8,128)(2,1)} %collective-permute-done.36), channel_id=1, source_target_pairs={{0,1},{1,0},{2,3},{3,2},{4,5},{5,4},{6,7},{7,6},{8,9},{9,8},{10,11... | collective-permute-start | bytes 3145736 | tf_op jit(solution)/shard_map/ppermute | solution.py:522
  258.9 32.6 %collective-permute-start.41 = (bf16[256,2048]{1,0:T(8,128)(2,1)}, bf16[256,2048]{1,0:T(8,128)(2,1)S(1)}, u32[]{:S(2)}, u32[]{:S(2)}) collective-permute-start(bf16[256,2048]{1,0:T(8,128)(2,1)} %collective-permute-done.37), channel_id=1, source_target_pairs={{0,1},{1,0},{2,3},{3,2},{4,5},{5,4},{6,7},{7,6},{8,9},{9,8},{10,11... | collective-permute-start | bytes 3145736 | tf_op jit(solution)/shard_map/ppermute | solution.py:522
  280.6 30.5 %collective-permute-start.42 = (bf16[256,2048]{1,0:T(8,128)(2,1)}, bf16[256,2048]{1,0:T(8,128)(2,1)S(1)}, u32[]{:S(2)}, u32[]{:S(2)}) collective-permute-start(bf16[256,2048]{1,0:T(8,128)(2,1)} %collective-permute-done.38), channel_id=1, source_target_pairs={{0,1},{1,0},{2,3},{3,2},{4,5},{5,4},{6,7},{7,6},{8,9},{9,8},{10,11... | collective-permute-start | bytes 3145736 | tf_op jit(solution)/shard_map/ppermute | solution.py:522
  285.0 26.0 %collective-permute-start.15 = (bf16[256,2048]{1,0:T(8,128)(2,1)S(1)}, bf16[256,2048]{1,0:T(8,128)(2,1)S(1)}, u32[]{:S(2)}, u32[]{:S(2)}) collective-permute-start(bf16[256,2048]{1,0:T(8,128)(2,1)S(1)} %get-tuple-element.74), channel_id=1, source_target_pairs={{0,2},{2,0},{4,6},{6,4},{1,3},{3,1},{5,7},{7,5},{8,10},{10,8},{12,... | collective-permute-start | bytes 3145736 | tf_op jit(solution)/shard_map/ppermute | solution.py:519
  286.8 48.1 %collective-permute-start.16 = (bf16[256,2048]{1,0:T(8,128)(2,1)S(1)}, bf16[256,2048]{1,0:T(8,128)(2,1)S(1)}, u32[]{:S(2)}, u32[]{:S(2)}) collective-permute-start(bf16[256,2048]{1,0:T(8,128)(2,1)S(1)} %get-tuple-element.74), channel_id=1, source_target_pairs={{0,4},{2,6},{4,0},{6,2},{1,5},{3,7},{5,1},{7,3},{8,12},{10,14},{12... | collective-permute-start | bytes 3145736 | tf_op jit(solution)/shard_map/ppermute | solution.py:519
  289.6 45.5 %collective-permute-start.17 = (bf16[256,2048]{1,0:T(8,128)(2,1)S(1)}, bf16[256,2048]{1,0:T(8,128)(2,1)S(1)}, u32[]{:S(2)}, u32[]{:S(2)}) collective-permute-start(bf16[256,2048]{1,0:T(8,128)(2,1)S(1)} %get-tuple-element.74), channel_id=1, source_target_pairs={{0,6},{2,4},{4,2},{6,0},{1,7},{3,5},{5,3},{7,1},{8,14},{10,12},{12... | collective-permute-start | bytes 3145736 | tf_op jit(solution)/shard_map/ppermute | solution.py:519
  291.6 44.3 %collective-permute-start.18 = (bf16[256,2048]{1,0:T(8,128)(2,1)S(1)}, bf16[256,2048]{1,0:T(8,128)(2,1)S(1)}, u32[]{:S(2)}, u32[]{:S(2)}) collective-permute-start(bf16[256,2048]{1,0:T(8,128)(2,1)S(1)} %get-tuple-element.74), channel_id=1, source_target_pairs={{0,1},{1,0},{2,3},{3,2},{4,5},{5,4},{6,7},{7,6},{8,9},{9,8},{10,11... | collective-permute-start | bytes 3145736 | tf_op jit(solution)/shard_map/ppermute | solution.py:522
  311.0 24.9 %collective-permute-start.19 = (bf16[256,2048]{1,0:T(8,128)(2,1)S(1)}, bf16[256,2048]{1,0:T(8,128)(2,1)S(1)}, u32[]{:S(2)}, u32[]{:S(2)}) collective-permute-start(bf16[256,2048]{1,0:T(8,128)(2,1)S(1)} %collective-permute-done.15), channel_id=1, source_target_pairs={{0,1},{1,0},{2,3},{3,2},{4,5},{5,4},{6,7},{7,6},{8,9},{9,8},{10,11... | collective-permute-start | bytes 3145736 | tf_op jit(solution)/shard_map/ppermute | solution.py:522
  408.6 256.3 %reduce-scatter.7.cloned.1.call-start = ((), (), s32[]{:S(2)}) async-start(), calls=%async_computation.9 | async-start | bytes 5242880 | tf_op jit(solution)/shard_map/reduce_scatter | solution.py:569
  422.7 246.4 %reduce-scatter.9.cloned.1.call-start = ((), (), s32[]{:S(2)}) async-start(), calls=%async_computation.10 | async-start | bytes 5242880 | tf_op jit(solution)/shard_map/reduce_scatter | solution.py:569
  442.4 23.6 %collective-permute-start.43 = (bf16[1024,2048]{1,0:T(8,128)(2,1)}, bf16[1024,2048]{1,0:T(8,128)(2,1)S(1)}, u32[]{:S(2)}, u32[]{:S(2)}) collective-permute-start(bf16[1024,2048]{1,0:T(8,128)(2,1)} %add_convert_fusion), channel_id=1, source_target_pairs={{0,1},{1,0},{2,3},{3,2},{4,5},{5,4},{6,7},{7,6},{8,9},{9,8},{10,11... | collective-permute-start | bytes 12582920 | tf_op jit(solution)/shard_map/ppermute | solution.py:522
  450.5 87.8 %collective-permute-start.31 = (bf16[1024,2048]{1,0:T(8,128)(2,1)}, bf16[1024,2048]{1,0:T(8,128)(2,1)}, u32[]{:S(2)}, u32[]{:S(2)}) collective-permute-start(bf16[1024,2048]{1,0:T(8,128)(2,1)} %convolution_convert_fusion.2), channel_id=1, source_target_pairs={{0,1},{1,0},{2,3},{3,2},{4,5},{5,4},{6,7},{7,6},{8,9},{9,8},{10,11... | collective-permute-start | bytes 12582920 | tf_op jit(solution)/shard_map/ppermute | solution.py:522
  477.4 26.2 %collective-permute-start.44 = (bf16[256,2048]{1,0:T(8,128)(2,1)}, bf16[256,2048]{1,0:T(8,128)(2,1)S(1)}, u32[]{:S(2)}, u32[]{:S(2)}) collective-permute-start(bf16[256,2048]{1,0:T(8,128)(2,1)} %get-tuple-element.81), channel_id=1, source_target_pairs={{0,2},{2,0},{4,6},{6,4},{1,3},{3,1},{5,7},{7,5},{8,10},{10,8},{12,... | collective-permute-start | bytes 3145736 | tf_op jit(solution)/shard_map/ppermute | solution.py:519
  478.8 47.7 %collective-permute-start.45 = (bf16[256,2048]{1,0:T(8,128)(2,1)}, bf16[256,2048]{1,0:T(8,128)(2,1)}, u32[]{:S(2)}, u32[]{:S(2)}) collective-permute-start(bf16[256,2048]{1,0:T(8,128)(2,1)} %get-tuple-element.83), channel_id=1, source_target_pairs={{0,4},{2,6},{4,0},{6,2},{1,5},{3,7},{5,1},{7,3},{8,12},{10,14},{12... | collective-permute-start | bytes 3145736 | tf_op jit(solution)/shard_map/ppermute | solution.py:519
  479.2 47.3 %collective-permute-start.46 = (bf16[256,2048]{1,0:T(8,128)(2,1)}, bf16[256,2048]{1,0:T(8,128)(2,1)}, u32[]{:S(2)}, u32[]{:S(2)}) collective-permute-start(bf16[256,2048]{1,0:T(8,128)(2,1)} %get-tuple-element.82), channel_id=1, source_target_pairs={{0,6},{2,4},{4,2},{6,0},{1,7},{3,5},{5,3},{7,1},{8,14},{10,12},{12... | collective-permute-start | bytes 3145736 | tf_op jit(solution)/shard_map/ppermute | solution.py:519
  492.3 216.7 %reduce-scatter.5.cloned.1.call-start = ((), (), s32[]{:S(2)}) async-start(), calls=%async_computation.8 | async-start | bytes 3276800 | tf_op jit(solution)/shard_map/reduce_scatter | solution.py:569
  534.9 26.1 %collective-permute-start.47 = (bf16[256,2048]{1,0:T(8,128)(2,1)S(1)}, bf16[256,2048]{1,0:T(8,128)(2,1)S(1)}, u32[]{:S(2)}, u32[]{:S(2)}) collective-permute-start(bf16[256,2048]{1,0:T(8,128)(2,1)S(1)} %get-tuple-element.65), channel_id=1, source_target_pairs={{0,2},{2,0},{4,6},{6,4},{1,3},{3,1},{5,7},{7,5},{8,10},{10,8},{12,... | collective-permute-start | bytes 3145736 | tf_op jit(solution)/shard_map/ppermute | solution.py:519
  535.6 27.8 %collective-permute-start.48 = (bf16[256,2048]{1,0:T(8,128)(2,1)S(1)}, bf16[256,2048]{1,0:T(8,128)(2,1)S(1)}, u32[]{:S(2)}, u32[]{:S(2)}) collective-permute-start(bf16[256,2048]{1,0:T(8,128)(2,1)S(1)} %get-tuple-element.65), channel_id=1, source_target_pairs={{0,4},{2,6},{4,0},{6,2},{1,5},{3,7},{5,1},{7,3},{8,12},{10,14},{12... | collective-permute-start | bytes 3145736 | tf_op jit(solution)/shard_map/ppermute | solution.py:519
  536.7 46.7 %collective-permute-start.49 = (bf16[256,2048]{1,0:T(8,128)(2,1)S(1)}, bf16[256,2048]{1,0:T(8,128)(2,1)S(1)}, u32[]{:S(2)}, u32[]{:S(2)}) collective-permute-start(bf16[256,2048]{1,0:T(8,128)(2,1)S(1)} %get-tuple-element.65), channel_id=1, source_target_pairs={{0,6},{2,4},{4,2},{6,0},{1,7},{3,5},{5,3},{7,1},{8,14},{10,12},{12... | collective-permute-start | bytes 3145736 | tf_op jit(solution)/shard_map/ppermute | solution.py:519
  550.4 33.2 %collective-permute-start.50 = (bf16[256,2048]{1,0:T(8,128)(2,1)S(1)}, bf16[256,2048]{1,0:T(8,128)(2,1)S(1)}, u32[]{:S(2)}, u32[]{:S(2)}) collective-permute-start(bf16[256,2048]{1,0:T(8,128)(2,1)S(1)} %get-tuple-element.65), channel_id=1, source_target_pairs={{0,1},{1,0},{2,3},{3,2},{4,5},{5,4},{6,7},{7,6},{8,9},{9,8},{10,11... | collective-permute-start | bytes 3145736 | tf_op jit(solution)/shard_map/ppermute | solution.py:522
  560.9 24.4 %collective-permute-start.51 = (bf16[256,2048]{1,0:T(8,128)(2,1)S(1)}, bf16[256,2048]{1,0:T(8,128)(2,1)S(1)}, u32[]{:S(2)}, u32[]{:S(2)}) collective-permute-start(bf16[256,2048]{1,0:T(8,128)(2,1)S(1)} %collective-permute-done.47), channel_id=1, source_target_pairs={{0,1},{1,0},{2,3},{3,2},{4,5},{5,4},{6,7},{7,6},{8,9},{9,8},{10,11... | collective-permute-start | bytes 3145736 | tf_op jit(solution)/shard_map/ppermute | solution.py:522
  562.6 86.2 %collective-permute-start.32 = (bf16[256,2048]{1,0:T(8,128)(2,1)}, bf16[256,2048]{1,0:T(8,128)(2,1)}, u32[]{:S(2)}, u32[]{:S(2)}) collective-permute-start(bf16[256,2048]{1,0:T(8,128)(2,1)} %get-tuple-element.84), channel_id=1, source_target_pairs={{0,2},{2,0},{4,6},{6,4},{1,3},{3,1},{5,7},{7,5},{8,10},{10,8},{12,... | collective-permute-start | bytes 3145736 | tf_op jit(solution)/shard_map/ppermute | solution.py:519
  563.4 23.3 %collective-permute-start.52 = (bf16[256,2048]{1,0:T(8,128)(2,1)S(1)}, bf16[256,2048]{1,0:T(8,128)(2,1)S(1)}, u32[]{:S(2)}, u32[]{:S(2)}) collective-permute-start(bf16[256,2048]{1,0:T(8,128)(2,1)S(1)} %collective-permute-done.48), channel_id=1, source_target_pairs={{0,1},{1,0},{2,3},{3,2},{4,5},{5,4},{6,7},{7,6},{8,9},{9,8},{10,11... | collective-permute-start | bytes 3145736 | tf_op jit(solution)/shard_map/ppermute | solution.py:522
  583.6 65.2 %collective-permute-start.33 = (bf16[256,2048]{1,0:T(8,128)(2,1)}, bf16[256,2048]{1,0:T(8,128)(2,1)}, u32[]{:S(2)}, u32[]{:S(2)}) collective-permute-start(bf16[256,2048]{1,0:T(8,128)(2,1)} %get-tuple-element.86), channel_id=1, source_target_pairs={{0,4},{2,6},{4,0},{6,2},{1,5},{3,7},{5,1},{7,3},{8,12},{10,14},{12... | collective-permute-start | bytes 3145736 | tf_op jit(solution)/shard_map/ppermute | solution.py:519
  585.4 63.5 %collective-permute-start.34 = (bf16[256,2048]{1,0:T(8,128)(2,1)}, bf16[256,2048]{1,0:T(8,128)(2,1)}, u32[]{:S(2)}, u32[]{:S(2)}) collective-permute-start(bf16[256,2048]{1,0:T(8,128)(2,1)} %get-tuple-element.85), channel_id=1, source_target_pairs={{0,6},{2,4},{4,2},{6,0},{1,7},{3,5},{5,3},{7,1},{8,14},{10,12},{12... | collective-permute-start | bytes 3145736 | tf_op jit(solution)/shard_map/ppermute | solution.py:519
  640.1 51.1 %collective-permute-start.54 = (bf16[1024,2048]{1,0:T(8,128)(2,1)}, bf16[1024,2048]{1,0:T(8,128)(2,1)}, u32[]{:S(2)}, u32[]{:S(2)}) collective-permute-start(bf16[1024,2048]{1,0:T(8,128)(2,1)} %convolution_convert_fusion), channel_id=1, source_target_pairs={{0,1},{1,0},{2,3},{3,2},{4,5},{5,4},{6,7},{7,6},{8,9},{9,8},{10,11... | collective-permute-start | bytes 12582920 | tf_op jit(solution)/shard_map/ppermute | solution.py:522
  700.9 26.3 %collective-permute-start.55 = (bf16[256,2048]{1,0:T(8,128)(2,1)}, bf16[256,2048]{1,0:T(8,128)(2,1)S(1)}, u32[]{:S(2)}, u32[]{:S(2)}) collective-permute-start(bf16[256,2048]{1,0:T(8,128)(2,1)} %get-tuple-element.78), channel_id=1, source_target_pairs={{0,2},{2,0},{4,6},{6,4},{1,3},{3,1},{5,7},{7,5},{8,10},{10,8},{12,... | collective-permute-start | bytes 3145736 | tf_op jit(solution)/shard_map/ppermute | solution.py:519
  702.1 49.6 %collective-permute-start.56 = (bf16[256,2048]{1,0:T(8,128)(2,1)}, bf16[256,2048]{1,0:T(8,128)(2,1)S(1)}, u32[]{:S(2)}, u32[]{:S(2)}) collective-permute-start(bf16[256,2048]{1,0:T(8,128)(2,1)} %get-tuple-element.80), channel_id=1, source_target_pairs={{0,4},{2,6},{4,0},{6,2},{1,5},{3,7},{5,1},{7,3},{8,12},{10,14},{12... | collective-permute-start | bytes 3145736 | tf_op jit(solution)/shard_map/ppermute | solution.py:519
  702.2 49.6 %collective-permute-start.57 = (bf16[256,2048]{1,0:T(8,128)(2,1)}, bf16[256,2048]{1,0:T(8,128)(2,1)}, u32[]{:S(2)}, u32[]{:S(2)}) collective-permute-start(bf16[256,2048]{1,0:T(8,128)(2,1)} %get-tuple-element.79), channel_id=1, source_target_pairs={{0,6},{2,4},{4,2},{6,0},{1,7},{3,5},{5,3},{7,1},{8,14},{10,12},{12... | collective-permute-start | bytes 3145736 | tf_op jit(solution)/shard_map/ppermute | solution.py:519
  710.3 49.7 %collective-permute-start.59 = (bf16[128,640]{0,1:T(8,128)(2,1)S(1)}, bf16[128,640]{0,1:T(8,128)(2,1)S(1)}, u32[]{:S(2)}, u32[]{:S(2)}) collective-permute-start(bf16[128,640]{0,1:T(8,128)(2,1)S(1)} %get-tuple-element.125), channel_id=1, source_target_pairs={{0,2},{2,0},{4,6},{6,4},{1,3},{3,1},{5,7},{7,5},{8,10},{10,8},{12,... | collective-permute-start | bytes 491528 | tf_op jit(solution)/shard_map/ppermute | solution.py:519
  711.6 48.4 %collective-permute-start.60 = (bf16[128,640]{0,1:T(8,128)(2,1)S(1)}, bf16[128,640]{0,1:T(8,128)(2,1)S(1)}, u32[]{:S(2)}, u32[]{:S(2)}) collective-permute-start(bf16[128,640]{0,1:T(8,128)(2,1)S(1)} %get-tuple-element.124), channel_id=1, source_target_pairs={{0,4},{2,6},{4,0},{6,2},{1,5},{3,7},{5,1},{7,3},{8,12},{10,14},{12... | collective-permute-start | bytes 491528 | tf_op jit(solution)/shard_map/ppermute | solution.py:519
  727.2 32.9 %collective-permute-start.61 = (bf16[128,640]{0,1:T(8,128)(2,1)S(1)}, bf16[128,640]{0,1:T(8,128)(2,1)S(1)}, u32[]{:S(2)}, u32[]{:S(2)}) collective-permute-start(bf16[128,640]{0,1:T(8,128)(2,1)S(1)} %get-tuple-element.123), channel_id=1, source_target_pairs={{0,6},{2,4},{4,2},{6,0},{1,7},{3,5},{5,3},{7,1},{8,14},{10,12},{12... | collective-permute-start | bytes 491528 | tf_op jit(solution)/shard_map/ppermute | solution.py:519
  (86 other events, 1158.9 us)
Sparse Core Ops, SparseCore 0:
  27.6 55.1 all-gather.4
  84.3 79.5 all-gather.6
  165.5 79.2 all-gather.8
  246.2 79.2 all-gather.10
  408.7 77.7 reduce-scatter.10
  488.8 77.2 reduce-scatter.6
  568.4 77.2 reduce-scatter.8
  648.9 53.2 reduce-scatter.4

commit v2 on v1

--- a/solution.py
+++ b/solution.py
@@ -321,12 +321,11 @@
 
 
 def attend_kernel(
-    rows, window, heads, place_ref, qkv_ref, inv_ref, cos_ref, sin_ref, start_ref,
-    query_ref, kv_ref, mixed_ref, lse_ref, keys, values,
+    rows, window, heads, place_ref, qkv_ref, cos_ref, sin_ref, start_ref, *rest,
 ):
+    query_ref, kv_ref, mixed_ref, lse_ref, keys, values = rest[-6:]
     step = pl.program_id(1)
     _, low_half = half_lanes(rows)
-    inv = inv_ref[...]
     cosine, sine = cos_ref[...], sin_ref[...]
 
     @pl.when(step == 0)
@@ -335,7 +334,7 @@
         values[...] = jnp.zeros_like(values)
 
     width = heads * HD
-    raw = qkv_ref[:, width:] * inv
+    raw = qkv_ref[:, width:]
     kv = jnp.where(low_half, turn(raw, cosine, sine), raw)
     kv_ref[...] = kv.astype(jnp.bfloat16)
     moved = pltpu.roll(kv, HD, 1)
@@ -349,7 +348,7 @@
     allowed = window_mask(start_ref[...], step * rows, first_key, rows, window)
     for slab in range(width // LANES):
         at = slice(slab * LANES, (slab + 1) * LANES)
-        rot = turn(qkv_ref[:, at] * inv, cosine, sine).astype(jnp.bfloat16)
+        rot = turn(qkv_ref[:, at], cosine, sine).astype(jnp.bfloat16)
         query_ref[:, at] = rot
         both = []
         for part in range(2):
@@ -427,7 +426,7 @@
     out_ref[:, width:] = (jnp.where(low_half, d_key, d_value) * inv).astype(jnp.bfloat16)
 
 
-def attend(place, qkv, inv, cosine, sine, start, seqs, blocks, rows, heads):
+def attend(place, qkv, cosine, sine, start, seqs, blocks, rows, heads, others):
     tokens = qkv.shape[0]
     width = heads * HD
     window = min(blocks * rows, rows + -(-MAX_DOC // rows) * rows)
@@ -449,13 +448,14 @@
         grid_spec=pltpu.PrefetchScalarGridSpec(
             num_scalar_prefetch=1,
             grid=(seqs, blocks),
-            in_specs=[placed(width + LANES), placed(1), natural(LANES), natural(LANES), natural(1)],
+            in_specs=[placed(width + LANES), natural(LANES), natural(LANES), natural(1)]
+            + [ANYWHERE] * len(others),
             out_specs=[placed(width), placed(LANES), placed(width), placed(heads)],
             scratch_shapes=[pltpu.VMEM((blocks * rows, LANES), jnp.bfloat16)] * 2,
         ),
         compiler_params=pltpu.CompilerParams(vmem_limit_bytes=48 << 20),
         name="attend",
-    )(place, qkv, inv, cosine, sine, start)
+    )(place, qkv, cosine, sine, start, *others)
 
 
 def attend_back(place, query, kv, lse, grad, inv, cosine, sine, start, seqs, blocks, rows, heads):
@@ -492,12 +492,241 @@
             + [pltpu.VMEM((blocks * rows, LANES), jnp.float32)] * 2,
         ),
         compiler_params=pltpu.CompilerParams(vmem_limit_bytes=48 << 20),
+        cost_estimate=pl.CostEstimate(
+            flops=48 * tokens * window * heads * LANES,
+            transcendentals=tokens * window * heads,
+            bytes_accessed=tokens * (8 * width + 12 * LANES),
+        ),
         name="attend_back",
     )(place, query, kv, lse, grad, inv, cosine, sine, start)
 
 
-def tied(value, *others):
-    return lax.optimization_barrier((value, *others))[0]
+VMEM_LIMIT = 56 << 20
+ANYWHERE = pl.BlockSpec(memory_space=pl.ANY)
+
+
+def fetch(pieces, whole, sems):
+    copies, at = [], 0
+    for n, piece in enumerate(pieces):
+        span = slice(at, at + piece.shape[0])
+        copy = pltpu.make_async_copy(piece, whole.at[span, :], sems.at[n])
+        copy.start()
+        copies.append((copy, span))
+        at += piece.shape[0]
+    return copies
+
+
+def inverse_rms(values):
+    values = values.astype(jnp.float32)
+    return lax.rsqrt(jnp.mean(values * values, axis=-1, keepdims=True) + EPSILON)
+
+
+def rows_of(pieces):
+    return sum(piece.shape[0] for piece in pieces)
+
+
+def project_kernel(count, tokens, normed, factor, *refs):
+    pieces, rest = refs[:count], refs[count + tokens :]
+    weight_ref, out_ref = rest[:2]
+    whole, sems = rest[-2:]
+    for copy, span in fetch(pieces, whole, sems):
+        copy.wait()
+        values = whole[span, :]
+        product = jnp.dot(values, weight_ref[...], preferred_element_type=jnp.float32)
+        if normed:
+            inv = inverse_rms(values)
+            rest[2][span, :] = inv
+            product = product * inv
+        else:
+            product = product * factor
+        out_ref[span, :] = product.astype(out_ref.dtype)
+
+
+def project(pieces, weight, normed, factor, dtype, tokens=()):
+    count, width = rows_of(pieces), pieces[0].shape[1]
+    out_shape = [jax.ShapeDtypeStruct((count, weight.shape[1]), dtype)]
+    if normed:
+        out_shape.append(jax.ShapeDtypeStruct((count, 1), jnp.float32))
+    vmem = pl.BlockSpec(memory_space=pltpu.VMEM)
+    return pl.pallas_call(
+        functools.partial(project_kernel, len(pieces), len(tokens), normed, factor),
+        out_shape=out_shape,
+        in_specs=[ANYWHERE] * (len(pieces) + len(tokens)) + [vmem],
+        out_specs=[vmem] * len(out_shape),
+        scratch_shapes=[
+            pltpu.VMEM((count, width), jnp.bfloat16),
+            pltpu.SemaphoreType.DMA((len(pieces),)),
+        ],
+        compiler_params=pltpu.CompilerParams(vmem_limit_bytes=VMEM_LIMIT),
+        cost_estimate=pl.CostEstimate(
+            flops=4 * count * width * weight.shape[1],
+            transcendentals=0,
+            bytes_accessed=2 * count * width,
+        ),
+        name="project",
+    )(*pieces, *tokens, weight)
+
+
+def gated_kernel(count, chunk, *refs):
+    pieces, rest = refs[:count], refs[count:]
+    pair_w, gate_ref, up_ref, hidden_ref, inv_ref, whole, sems = rest
+    block = gate_ref.shape[1]
+
+    @pl.when(pl.program_id(0) == 0)
+    def _():
+        for copy, span in fetch(pieces, whole, sems):
+            copy.wait()
+            inv_ref[span, :] = inverse_rms(whole[span, :])
+
+    for at in range(0, whole.shape[0], chunk):
+        span = slice(at, at + chunk)
+        both = jnp.dot(whole[span, :], pair_w[...], preferred_element_type=jnp.float32)
+        both = both * inv_ref[span, :]
+        gate, up = both[:, :block], both[:, block:]
+        gate_ref[span, :] = gate.astype(jnp.bfloat16)
+        up_ref[span, :] = up.astype(jnp.bfloat16)
+        hidden_ref[span, :] = (gate * lax.logistic(gate) * up).astype(jnp.bfloat16)
+
+
+def gated(pieces, pair_w, block, chunk):
+    tokens, width = rows_of(pieces), pieces[0].shape[1]
+    units = pair_w.shape[1] // 2
+    low = jax.ShapeDtypeStruct((tokens, units), jnp.bfloat16)
+    out = pl.BlockSpec((tokens, block), lambda j: (0, j))
+    return pl.pallas_call(
+        functools.partial(gated_kernel, len(pieces), chunk),
+        out_shape=[low, low, low, jax.ShapeDtypeStruct((tokens, 1), jnp.float32)],
+        grid=(units // block,),
+        in_specs=[ANYWHERE] * len(pieces)
+        + [pl.BlockSpec((width, 2 * block), lambda j: (0, j))],
+        out_specs=[out, out, out, pl.BlockSpec((tokens, 1), lambda j: (0, 0))],
+        scratch_shapes=[
+            pltpu.VMEM((tokens, width), jnp.bfloat16),
+            pltpu.SemaphoreType.DMA((len(pieces),)),
+        ],
+        compiler_params=pltpu.CompilerParams(vmem_limit_bytes=VMEM_LIMIT),
+        name="gated",
+    )(*pieces, pair_w)
+
+
+def gated_back_kernel(count, tokens, chunk, *refs):
+    pieces, rest = refs[:count], refs[count + tokens :]
+    down_w, gate_ref, up_ref, inv_ref, out_ref, whole, sems = rest
+    block = gate_ref.shape[1]
+
+    @pl.when(pl.program_id(0) == 0)
+    def _():
+        for copy, _ in fetch(pieces, whole, sems):
+            copy.wait()
+
+    for at in range(0, whole.shape[0], chunk):
+        span = slice(at, at + chunk)
+        d_hidden = jnp.dot(whole[span, :], down_w[...], preferred_element_type=jnp.float32)
+        d_hidden = d_hidden * (RESIDUAL * inv_ref[span, :])
+        gate = gate_ref[span, :].astype(jnp.float32)
+        up = up_ref[span, :].astype(jnp.float32)
+        sigma = lax.logistic(gate)
+        out_ref[span, :block] = (d_hidden * up * sigma * (1.0 + gate * (1.0 - sigma))).astype(
+            jnp.bfloat16
+        )
+        out_ref[span, block:] = (d_hidden * gate * sigma).astype(jnp.bfloat16)
+
+
+def gated_back(pieces, down_w, gate, up, inv, block, chunk, others):
+    tokens, width = rows_of(pieces), pieces[0].shape[1]
+    units = down_w.shape[1]
+    tall = pl.BlockSpec((tokens, block), lambda j: (0, j))
+    return pl.pallas_call(
+        functools.partial(gated_back_kernel, len(pieces), len(others), chunk),
+        out_shape=jax.ShapeDtypeStruct((tokens, 2 * units), jnp.bfloat16),
+        grid=(units // block,),
+        in_specs=[ANYWHERE] * (len(pieces) + len(others))
+        + [
+            pl.BlockSpec((width, block), lambda j: (0, j)),
+            tall,
+            tall,
+            pl.BlockSpec((tokens, 1), lambda j: (0, 0)),
+        ],
+        out_specs=pl.BlockSpec((tokens, 2 * block), lambda j: (0, j)),
+        scratch_shapes=[
+            pltpu.VMEM((tokens, width), jnp.bfloat16),
+            pltpu.SemaphoreType.DMA((len(pieces),)),
+        ],
+        compiler_params=pltpu.CompilerParams(vmem_limit_bytes=VMEM_LIMIT),
+        name="gated_back",
+    )(*pieces, *others, down_w, gate, up, inv)
+
+
+def outer_kernel(counts, tokens, block, *refs):
+    sources, at = [], 0
+    for count, rights in counts:
+        sources.append((refs[at : at + count], refs[at + count : at + count + rights]))
+        at += count + rights
+    out_ref, scratch = refs[at + tokens], refs[at + tokens + 1 :]
+    step = pl.program_id(0)
+
+    @pl.when(step == 0)
+    def _():
+        copies = []
+        for n, (pieces, _) in enumerate(sources):
+            copies += fetch(pieces, scratch[2 * n], scratch[2 * n + 1])
+        for copy, _ in copies:
+            copy.wait()
+
+    first = 0
+    columns = pl.ds(pl.multiple_of(step * block, block), block)
+    for n, (_, rights) in enumerate(sources):
+        left = scratch[2 * n][:, columns]
+        for right in rights:
+            out_ref[:, first : first + right.shape[1]] = dot_tn(left, right[...]).astype(
+                out_ref.dtype
+            )
+            first += right.shape[1]
+
+
+def outer(sources, block, tokens=(), cost=None):
+    operands, in_specs, scratch, counts, total = [], [], [], [], 0
+    for pieces, rights in sources:
+        count, width = rows_of(pieces), pieces[0].shape[1]
+        operands += [*pieces, *rights]
+        in_specs += [ANYWHERE] * len(pieces)
+        in_specs += [pl.BlockSpec(right.shape, lambda j: (0, 0)) for right in rights]
+        scratch += [
+            pltpu.VMEM((count, width), jnp.bfloat16),
+            pltpu.SemaphoreType.DMA((len(pieces),)),
+        ]
+        counts.append((len(pieces), len(rights)))
+        total += sum(right.shape[1] for right in rights)
+    return pl.pallas_call(
+        functools.partial(outer_kernel, counts, len(tokens), block),
+        out_shape=jax.ShapeDtypeStruct((width, total), jnp.bfloat16),
+        grid=(width // block,),
+        in_specs=in_specs + [ANYWHERE] * len(tokens),
+        out_specs=pl.BlockSpec((block, total), lambda j: (j, 0)),
+        scratch_shapes=scratch,
+        compiler_params=pltpu.CompilerParams(vmem_limit_bytes=VMEM_LIMIT),
+        cost_estimate=cost,
+        name="outer",
+    )(*operands, *tokens)
+
+
+def add_low(one, other):
+    return (one.astype(jnp.float32) + other.astype(jnp.float32)).astype(jnp.bfloat16)
+
+
+def after_kernel(*refs):
+    del refs
+
+
+def after(value, *tokens):
+    return pl.pallas_call(
+        after_kernel,
+        out_shape=jax.ShapeDtypeStruct(value.shape, value.dtype),
+        in_specs=[ANYWHERE] * (1 + len(tokens)),
+        out_specs=ANYWHERE,
+        input_output_aliases={0: 0},
+        name="after",
+    )(value, *tokens)
 
 
 def group_shards(
@@ -512,8 +741,8 @@
     near = group // (length // rows_here)
     blocks = length // rows
     heads = HQ // KVH
-    me = lax.axis_index(("near", "ctx"))
-    me_core = lax.axis_index("tp")
+    me = lax.axis_index(("near", "ctx")).astype(jnp.uint32)
+    me_core = lax.axis_index("tp").astype(jnp.uint32)
 
     def swap(value, m):
         return lax.ppermute(value, ("near", "ctx"), [(i, i ^ m) for i in range(group)])
@@ -521,53 +750,120 @@
     def swap_core(value):
         return lax.ppermute(value, "tp", [(0, 1), (1, 0)])
 
-    def gather(own):
-        same = [own] + [swap(own, m) for m in range(1, group)]
-        return same, jnp.concatenate(same + [swap_core(v) for v in same], axis=0)
-
-    def scatter(product, left):
-        half = group * rows
-        other = swap_core(product(left[half:]).astype(bfloat))
-        mine = product(left[:half]) + other.astype(jnp.float32)
-        low = mine.astype(bfloat)
-        total = mine[:rows]
+    def gather(own, later=()):
+        half = own.shape[0] // 2
+        by_ctx, by_near = swap(own, 1), swap(own, 2)
+        if later:
+            by_ctx, by_near = after(by_ctx, *later), after(by_near, *later)
+        opposite = [swap(by_ctx[:half], 2), swap(by_near[half:], 1)]
+        same = [own, by_ctx, by_near, *opposite]
+        return same + [swap_core(v) for v in same]
+
+    def send_half(product):
+        side = group * rows
+        return swap_core(product(side, side, None, bfloat))
+
+    def own_side(product, other):
+        return product(0, group * rows, other, bfloat)
+
+    def scatter(mine):
+        half = rows // 2
+        ctx_low, near_low, opposite = (mine[m * rows : (m + 1) * rows] for m in range(1, group))
+        from_near, from_ctx = swap(opposite[:half], 2), swap(opposite[half:], 1)
+        near_first, ctx_last = swap(near_low[:half], 2), swap(ctx_low[half:], 1)
+        ctx_first = swap(add_low(ctx_low[:half], from_near), 1)
+        near_last = swap(add_low(near_low[half:], from_ctx), 2)
+        total = jnp.concatenate(
+            [
+                mine[:half].astype(jnp.float32)
+                + ctx_first.astype(jnp.float32)
+                + near_first.astype(jnp.float32),
+                mine[half:rows].astype(jnp.float32)
+                + ctx_last.astype(jnp.float32)
+                + near_last.astype(jnp.float32),
+            ]
+        )
+        return total
+
+    def scatter_direct(mine):
+        total = mine[:rows].astype(jnp.float32)
         for m in range(1, group):
-            total = total + swap(low[m * rows : (m + 1) * rows], m).astype(jnp.float32)
+            total = total + swap(mine[m * rows : (m + 1) * rows], m).astype(jnp.float32)
         return total
 
+    def plain(left, weight):
+        def product(first, size, add, dtype):
+            out = matmul_trans(left[first : first + size], weight)
+            return (out if add is None else out + add.astype(jnp.float32)).astype(dtype)
+
+        return product
+
     def own_half(value):
-        return lax.dynamic_slice_in_dim(value, me_core * rows, rows, 0)
+        return cut(value, me_core, rows, 0)
 
     def both_halves(own):
         other = swap_core(own)
         whole = jnp.zeros((rows_here, own.shape[1]), own.dtype)
-        whole = lax.dynamic_update_slice_in_dim(whole, own, me_core * rows, 0)
-        return lax.dynamic_update_slice_in_dim(whole, other, (1 - me_core) * rows, 0)
-
-    def to_columns(weight):
-        deep, cols = weight.shape[0], weight.shape[1] // group
-        whole = jnp.zeros((group * deep, cols), weight.dtype)
+        whole = put(whole, own, me_core, 0)
+        return put(whole, other, me_core ^ jnp.uint32(1), 0)
+
+    def cut(value, index, size, axis):
+        starts = [jnp.uint32(0)] * value.ndim
+        starts[axis] = index * jnp.uint32(size)
+        sizes = list(value.shape)
+        sizes[axis] = size
+        return lax.dynamic_slice(value, starts, sizes)
+
+    def put(whole, piece, index, axis):
+        starts = [jnp.uint32(0)] * whole.ndim
+        starts[axis] = index * jnp.uint32(piece.shape[axis])
+        return lax.dynamic_update_slice(whole, piece, starts)
+
+    def to_columns(*weights, parts=1):
+        whole = None
         for m in range(group):
-            piece = lax.dynamic_slice_in_dim(weight, (me ^ m) * cols, cols, 1)
+            there = me ^ jnp.uint32(m)
+            own = [cut(w, there, w.shape[1] // group, 1) for w in weights]
+            sizes = [w.shape[1] // parts for w in own]
+            piece = jnp.concatenate(
+                [w[:, n * size : (n + 1) * size] for n in range(parts) for w, size in zip(own, sizes)],
+                axis=1,
+            )
             piece = swap(piece, m) if m else piece
-            whole = lax.dynamic_update_slice_in_dim(whole, piece, (me ^ m) * deep, 0)
+            if whole is None:
+                whole = jnp.zeros((group * piece.shape[0], piece.shape[1]), piece.dtype)
+            whole = put(whole, piece, there, 0)
         return whole
 
     def to_rows(grad):
-        deep, cols = grad.shape[0] // group, grad.shape[1]
-        whole = jnp.zeros((deep, group * cols), grad.dtype)
-        for m in range(group):
-            piece = lax.dynamic_slice_in_dim(grad, (me ^ m) * deep, deep, 0)
-            piece = swap(piece, m) if m else piece
-            whole = lax.dynamic_update_slice_in_dim(whole, piece, (me ^ m) * cols, 1)
-        return whole
+        deep = grad.shape[0] // group
+        pieces = [cut(grad, me ^ jnp.uint32(m), deep, 0) for m in range(group)]
+        return [swap(piece, m) if m else piece for m, piece in enumerate(pieces)]
+
+    def unpack(pieces, widths, factors, parts=1):
+        first, wholes, turn_width = 0, [], sum(widths) // parts
+        for cols, factor in zip(widths, factors):
+            size = cols // parts
+            whole = jnp.zeros((pieces[0].shape[0], group * cols), jnp.float32)
+            for m, piece in enumerate(pieces):
+                part = jnp.concatenate(
+                    [
+                        piece[:, n * turn_width + first : n * turn_width + first + size]
+                        for n in range(parts)
+                    ],
+                    axis=1,
+                )
+                part = part.astype(jnp.float32) * factor
+                whole = put(whole, part, me ^ jnp.uint32(m), 1)
+            first += size
+            wholes.append(whole)
+        return wholes
 
     def far_gather(weight):
         return lax.all_gather(weight, "far", axis=0, tiled=True)
 
     def far_scatter(grad):
-        low = lax.psum_scatter(grad.astype(bfloat), "far", scatter_dimension=0, tiled=True)
-        return to_rows(low).astype(jnp.float32)
+        return lax.psum_scatter(grad.astype(bfloat), "far", scatter_dimension=0, tiled=True)
 
     deep = query_weight.shape[0]
     col_gain_a, col_gain_f = gain_attn[:, None], gain_ffn[:, None]
@@ -575,34 +871,28 @@
     def scaled(weight, gain):
         return (weight.astype(jnp.float32) * gain).astype(bfloat)
 
-    def chunks(weight):
-        return weight.reshape(deep, group, weight.shape[1] // group)
-
-    attn_local = jnp.concatenate(
-        [
-            chunks(scaled(query_weight, col_gain_a)),
-            chunks(scaled(key_weight, col_gain_a)),
-            chunks(scaled(value_weight, col_gain_a)),
-            chunks(out_weight),
-        ],
-        axis=2,
-    ).reshape(deep, -1)
-    attn_cols = to_columns(attn_local)
+    attn_cols = to_columns(
+        scaled(query_weight, col_gain_a),
+        scaled(key_weight, col_gain_a),
+        scaled(value_weight, col_gain_a),
+        out_weight,
+    )
     attn_w = far_gather(attn_cols)
     head_cols = heads * HD
     in_w, out_w = attn_w[:, : head_cols + 2 * HD], attn_w[:, head_cols + 2 * HD :]
 
-    own_in = tied(own_half(hidden_in.reshape(rows_here, width)), attn_cols)
-    pieces, inputs = gather(own_in)
-    last = pieces[-1]
-    gate_cols = to_columns(tied(scaled(gate_weight, col_gain_f), last))
-    up_cols = to_columns(tied(scaled(up_weight, col_gain_f), gate_cols))
-    down_cols = to_columns(tied(down_weight, up_cols))
-    gate_w = far_gather(gate_cols)
-    up_w = far_gather(up_cols)
+    gain_later = after(col_gain_f, attn_cols)
+    units = down_weight.shape[1] // group
+    block = min(units, 256)
+    pair_cols = to_columns(
+        scaled(gate_weight, gain_later), scaled(up_weight, gain_later), parts=units // block
+    )
+    own_in = after(own_half(hidden_in.reshape(rows_here, width)), pair_cols)
+    inputs = gather(own_in)
+    pair_w = far_gather(pair_cols)
+    own_cot = own_half(cotangent.reshape(rows_here, width))
+    down_cols = to_columns(down_weight)
     down_w = far_gather(down_cols)
-    own_cot = own_half(cotangent.reshape(rows_here, width))
-    _, cots = gather(tied(own_cot, down_cols))
 
     seg_all = jnp.concatenate(
         [segments]
@@ -621,73 +911,79 @@
     in_seq = at % blocks
     here_ctx = lax.axis_index("ctx")
     place = (
-        ((in_seq % cores) ^ me_core) * group
+        ((in_seq % cores) ^ lax.axis_index("tp")) * group
         + (at // blocks) * (group // near)
         + ((in_seq // cores) ^ here_ctx)
     ).astype(jnp.int32)
 
-    def inverse_rms(values):
-        values = values.astype(jnp.float32)
-        return lax.rsqrt(jnp.mean(values * values, axis=-1, keepdims=True) + EPSILON)
-
-    inv_a = inverse_rms(inputs)
-    qkv = matmul_low(inputs, in_w)
+    qkv, inv_a = project(inputs, in_w, True, None, jnp.float32)
     query, kv, mixed, lse = attend(
-        place, qkv, inv_a, cosine, sine, start, near, blocks, rows, heads
-    )
-    branch_a = scatter(lambda left: matmul_trans(left, out_w), mixed)
+        place, qkv, cosine, sine, start, near, blocks, rows, heads, (down_cols,)
+    )
+    product = plain(mixed, out_w)
+    branch_a = scatter(own_side(product, send_half(product)))
     own_f = own_in.astype(jnp.float32)
     middle = own_f + RESIDUAL * branch_a
 
-    _, mids = gather(middle.astype(bfloat))
-    inv_f = inverse_rms(mids)
-    gate_pre = matmul_low(mids, gate_w) * inv_f
-    upward = matmul_low(mids, up_w) * inv_f
-    sigma = jax.nn.sigmoid(gate_pre)
-    active = gate_pre * sigma
-    hidden = (active * upward).astype(bfloat)
-    branch_f = scatter(lambda left: matmul_trans(left, down_w), hidden)
-    layer_out = both_halves((middle + RESIDUAL * branch_f).astype(bfloat))
-    grad_down = far_scatter(matmul_outer(cots, hidden)) * RESIDUAL
-    d_hidden = matmul_low(cots, down_w) * RESIDUAL
-    d_gate = (inv_f * (d_hidden * upward * sigma * (1.0 + gate_pre * (1.0 - sigma)))).astype(bfloat)
-    d_up = (inv_f * (d_hidden * active)).astype(bfloat)
-    grad_gate = far_scatter(matmul_outer(mids, d_gate))
-    grad_up = far_scatter(matmul_outer(mids, d_up))
-    both = jnp.concatenate([d_gate, d_up], axis=1)
-    back_f = scatter(
-        lambda left: matmul_trans(left[:, : d_gate.shape[1]], gate_w)
-        + matmul_trans(left[:, d_gate.shape[1] :], up_w),
-        both,
-    )
+    mids = gather(middle.astype(bfloat))
+    gate_pre, upward, hidden, inv_f = gated(mids, pair_w, block, 512)
+    cots = gather(after(own_cot, *mids[1 : len(mids) // 2]), (inv_f,))
+    down_part = outer([(cots, [hidden])], 256)
+    down_far = far_scatter(down_part)
+    d_both = gated_back(cots, down_w, gate_pre, upward, inv_f, block, 512, (down_part,))
+    product = plain(d_both, pair_w)
+    other = send_half(product)
+    pair_part = outer([(mids, [d_both])], 256, (other,))
+    pair_far = far_scatter(pair_part)
+    back_mine = own_side(product, after(other, pair_part, down_far))
+    back_f = scatter(back_mine)
+    product = plain(after(hidden, back_mine), down_w)
+    branch_mine = own_side(product, send_half(product))
 
     def through_norm(grad, unit):
         return grad - unit * jnp.mean(grad * unit, axis=-1, keepdims=True)
 
     d_middle = own_cot.astype(jnp.float32) + through_norm(back_f, middle * inverse_rms(middle))
 
-    _, d_mids = gather(d_middle.astype(bfloat))
-    d_mixed = (matmul_low(d_mids, out_w) * RESIDUAL).astype(bfloat)
-    grad_out_part = matmul_outer(d_mids, mixed) * RESIDUAL
+    d_mids = gather(after(d_middle.astype(bfloat), branch_mine))
+    branch_f = scatter_direct(after(branch_mine, *d_mids[1 : len(d_mids) // 2]))
+    middle_out = (middle + RESIDUAL * branch_f).astype(bfloat)
+    (d_mixed,) = project(d_mids, out_w, False, RESIDUAL, bfloat)
+    down_rows = to_rows(after(down_far, d_mixed))
     d_qkv = attend_back(
         place, query, kv, lse, d_mixed, inv_a, cosine, sine, start, near, blocks, rows, heads
     )
-    grad_attn = jnp.concatenate(
-        [matmul_outer(inputs, d_qkv).astype(bfloat), grad_out_part.astype(bfloat)], axis=1
-    )
-    grad_attn = far_scatter(grad_attn).reshape(deep, group, -1)
-    back_a = scatter(lambda left: matmul_trans(left, in_w), d_qkv)
+    attn_cols_all = d_qkv.shape[1] + head_cols
+    attn_part = outer(
+        [(inputs, [d_qkv]), (d_mids, [mixed])],
+        256,
+        (pair_far, middle_out, *down_rows),
+        pl.CostEstimate(
+            flops=4 * d_qkv.shape[0] * width * attn_cols_all,
+            transcendentals=0,
+            bytes_accessed=8 * d_qkv.shape[0] * width,
+        ),
+    )
+    attn_far = far_scatter(attn_part)
+    pair_rows = to_rows(pair_far)
+    product = plain(after(d_qkv, attn_part, *pair_rows), in_w)
+    back_mine = own_side(product, send_half(product))
+    back_a = scatter(back_mine)
+    layer_out = both_halves(middle_out)
     input_grad = d_middle + through_norm(back_a, own_f * inverse_rms(own_f))
     input_grad = both_halves(input_grad)
 
-    def cut(first, size):
-        return grad_attn[:, :, first : first + size].reshape(deep, group * size)
-
-    grad_query, grad_key, grad_value, grad_out = (
-        cut(0, head_cols),
-        cut(head_cols, HD),
-        cut(head_cols + HD, HD),
-        cut(head_cols + 2 * HD, head_cols),
+    one = jnp.ones_like(col_gain_a)
+    (grad_down,) = unpack(
+        [after(piece, back_mine) for piece in down_rows], [units], [RESIDUAL]
+    )
+    grad_gate, grad_up = unpack(
+        [after(piece, back_mine) for piece in pair_rows], [units, units], [one, one], parts=units // block
+    )
+    grad_query, grad_key, grad_value, grad_out = unpack(
+        to_rows(after(attn_far, back_a)),
+        [head_cols, HD, HD, head_cols],
+        [one, one, one, RESIDUAL],
     )
 
     def row_sum(*pairs):
@@ -728,7 +1024,7 @@
         and near > 0
         and group * tp == KVH
         and fsdp % near == 0
-        and group & (group - 1) == 0
+        and near == ctx == 2
     )
     if fits:
         mesh = Mesh(

time: 788 us -> 724 us (0.919)
  matrix products: 197 us -> 57.4 us
  Pallas kernels: 53.3 us -> 182 us
  waiting for transfers between devices: 304 us -> 245 us
    pallas_call x0 -> x27, Pallas kernels: none -> 129 us  [the longest x3 62.2 us: outer(): pl.pallas_call(functools.partial(outer_kernel, counts, len(tokens), block...]
    dot_general x10 -> x0, matrix products: 116 us -> none  [the longest x5 67.1 us: matmul_low(): return jnp.dot(left, right, preferred_element_type=jnp.float32)]
    ppermute x49 -> x56, waiting for transfers between devices: 299 us -> 212 us  [swap(): lax.ppermute(value, ('near', 'ctx'), [(i, i ^ m) for i in range(group)])]
    dot_general x10 -> x8, matrix products: 81.1 us -> 57.4 us  [matmul_trans(): lax.dot_general(left, right, (((1,), (1,)), ((), ())), preferred_element_...]
    unnamed x143 -> x151, local copies, waits for them, and re-layouts: 39.8 us -> 18.4 us
    ppermute x23 -> x27, waiting for transfers between devices: 5.22 us -> 26 us  [swap_core(): return lax.ppermute(value, 'tp', [(0, 1), (1, 0)])]
    dynamic_update_slice x2 -> x19, other arithmetic: 7.9 us -> 26.4 us  [put(): return lax.dynamic_update_slice(whole, piece, starts)]
    slice x6 -> x18, local copies, waits for them, and re-layouts: 7.05 us -> 25.4 us  [the longest x8 11.1 us: gather(): opposite = [swap(by_ctx[:half], 2), swap(by_near[half:], 1)]]
  transfers between devices with their start and end apart: 80 -> 89, of which waited for: 32 -> 39; matrix products, arithmetic and copies ran while one was open for 37% -> 24% of each run, Pallas kernels for 7% -> 25%
where the time goes in v2:
time: 724 us; the launch traced here: 719 us
  waiting for transfers between devices  245 us (34%)
  Pallas kernels  182 us (25%)
  local copies, waits for them, and re-layouts  83.9 us (12%)
  starting transfers between devices  69.5 us (10%)
  other arithmetic  65.9 us (9%)
  matrix products  57.4 us (8%)
  between operations  15.6 us (2%)
    ppermute x56, waiting for transfers between devices, swap(): lax.ppermute(value, ('near', 'ctx'), [(i, i ^ m) for i in range(group)])  212 us
    ppermute x56, starting transfers between devices, swap(): lax.ppermute(value, ('near', 'ctx'), [(i, i ^ m) for i in range(group)])  65.3 us
    pallas_call x3, Pallas kernels, outer(): pl.pallas_call(functools.partial(outer_kernel, counts, len(tokens), block...  62.2 us
    dot_general x8, matrix products, matmul_trans(): lax.dot_general(left, right, (((1,), (1,)), ((), ())), preferred_element_...  57.4 us
    pallas_call x1, Pallas kernels, attend_back(): pl.pallas_call(functools.partial(attend_back_kernel, rows, window, heads,...  32.2 us
    dynamic_update_slice x19, other arithmetic, put(): return lax.dynamic_update_slice(whole, piece, starts)  26.4 us
    ppermute x27, waiting for transfers between devices, swap_core(): return lax.ppermute(value, 'tp', [(0, 1), (1, 0)])  26 us
    pallas_call x1, Pallas kernels, gated(): pl.pallas_call(functools.partial(gated_kernel, len(pieces), chunk), out_s...  25.8 us
  transfers between devices with their start and end apart: 89, of which 39 were waited for; matrix products, arithmetic and copies ran while one was open for 24% of the time, Pallas kernels for 25%

profile of v2, /device:TPU:0, one launch (start us, length us, event | category | flops | bytes accessed | tf_op | source)
XLA Modules:
  0.0 718.7 jit_solution(8557716227308006170)
XLA Ops:
  12.0 3.0 collective-permute-start
  19.7 4.7 collective-permute-done.1
  38.2 9.0 %collective-permute-done.3 = bf16[128,2048]{1,0:T(8,128)(2,1)S(1)} collective-permute-done((bf16[128,2048]{1,0:T(8,128)(2,1)S(1)}, bf16[128,2048]{1,0:T(8,128)(2,1)S(1)}, u32[]{:S(2)}, u32[]{:S(2)}) %collective-permute-start.3) | collective-permute-done | bytes 524320 | tf_op jit(solution)/shard_map/ppermute | solution.py:748
  48.0 7.2 collective-permute-done.4
  66.6 24.3 %collective-permute-done.15 = s32[1,1024]{1,0:T(1,128)S(1)} collective-permute-done((s32[1,1024]{1,0:T(1,128)S(1)}, s32[1,1024]{1,0:T(1,128)S(1)}, u32[]{:S(2)}, u32[]{:S(2)}) %collective-permute-start.15) | collective-permute-done | bytes 4128 | tf_op jit(solution)/shard_map/ppermute | solution.py:748
  100.3 5.5 fusion.27
  118.0 10.7 %project.2 = (f32[2048,384]{1,0:T(8,128)}, f32[2048,1]{1,0:T(8,128)}) custom-call(bf16[256,2048]{1,0:T(8,128)(2,1)} %after.21.refs_0_, bf16[256,2048]{1,0:T(8,128)(2,1)} %collective-permute-done.6.refs_1_, bf16[256,2048]{1,0:T(8,128)(2,1)} %collective-permute-done.7.refs_2_, bf16[128,2048]{1,0:T(8,128)(2,1)} %collective-permute-done.8.refs_3_, ...), custom_call_target="tpu_custom_call" | custom-call | flops 6442450944 | bytes 8388608 | tf_op jit(solution)/shard_map/project/pallas_call | solution.py:551
  128.8 20.3 %attend.1 = (bf16[2048,256]{1,0:T(8,128)(2,1)S(1)}, bf16[2048,128]{1,0:T(8,128)(2,1)S(1)}, bf16[2048,256]{1,0:T(8,128)(2,1)S(1)}, f32[2048,4]{1,0:T(8,128)S(1)}) custom-call(s32[8]{0:T(128)S(1)} %fusion.35.place_ref, f32[2048,384]{1,0:T(8,128)} %get-tuple-element.21.qkv_ref, f32[2048,128]{1,0:T(8,128)S(1)} %pad_maximum_fusion.2.cos_ref, ...), custom_call_target="tpu_custom_call" | custom-call | tf_op jit(solution)/shard_map/attend/pallas_call | solution.py:440
  151.0 6.8 collective-permute-done.19
  165.5 10.9 %collective-permute-done.20 = bf16[128,2048]{1,0:T(8,128)(2,1)S(1)} collective-permute-done((bf16[128,2048]{1,0:T(8,128)(2,1)S(1)}, bf16[128,2048]{1,0:T(8,128)(2,1)S(1)}, u32[]{:S(2)}, u32[]{:S(2)}) %collective-permute-start.20) | collective-permute-done | bytes 524320 | tf_op jit(solution)/shard_map/ppermute | solution.py:748
  179.7 7.4 %collective-permute-done.22 = bf16[128,2048]{1,0:T(8,128)(2,1)S(1)} collective-permute-done((bf16[128,2048]{1,0:T(8,128)(2,1)}, bf16[128,2048]{1,0:T(8,128)(2,1)S(1)}, u32[]{:S(2)}, u32[]{:S(2)}) %collective-permute-start.22) | collective-permute-done | bytes 524320 | tf_op jit(solution)/shard_map/ppermute | solution.py:748
  187.1 5.4 collective-permute-done.21
  195.9 6.0 collective-permute-done.23
  209.6 19.1 %collective-permute-done.26.refs_1_ = bf16[256,2048]{1,0:T(8,128)(2,1)} collective-permute-done((bf16[256,2048]{1,0:T(8,128)(2,1)}, bf16[256,2048]{1,0:T(8,128)(2,1)}, u32[]{:S(2)}, u32[]{:S(2)}) %collective-permute-start.26) | collective-permute-done | bytes 1048608 | tf_op jit(solution)/shard_map/ppermute | solution.py:748
  235.2 6.2 collective-permute-done.28.refs_3_
  241.4 5.7 collective-permute-done.29.refs_4_
  252.2 25.8 %gated.1 = (bf16[2048,1024]{1,0:T(8,128)(2,1)}, bf16[2048,1024]{1,0:T(8,128)(2,1)}, bf16[2048,1024]{1,0:T(8,128)(2,1)}, f32[2048,1]{1,0:T(8,128)}) custom-call(bf16[256,2048]{1,0:T(8,128)(2,1)} %get-tuple-element.58.refs_0_, bf16[256,2048]{1,0:T(8,128)(2,1)} %collective-permute-done.26.refs_1_, bf16[256,2048]{1,0:T(8,128)(2,1)} %collective-permute-done.27.refs_2_, ...), custom_call_target="tpu_custom_call" | custom-call | tf_op jit(solution)/shard_map/gated/pallas_call | solution.py:596
  283.2 11.4 %collective-permute-done.38.refs_4_ = bf16[128,2048]{1,0:T(8,128)(2,1)} collective-permute-done((bf16[128,2048]{1,0:T(8,128)(2,1)}, bf16[128,2048]{1,0:T(8,128)(2,1)}, u32[]{:S(2)}, u32[]{:S(2)}) %collective-permute-start.38) | collective-permute-done | bytes 524320 | tf_op jit(solution)/shard_map/ppermute | solution.py:748
  298.5 17.1 %outer.3.refs_10_ = bf16[2048,1024]{1,0:T(8,128)(2,1)} custom-call(bf16[256,2048]{1,0:T(8,128)(2,1)} %after.22.refs_0_, bf16[256,2048]{1,0:T(8,128)(2,1)} %after.23.refs_1_, bf16[256,2048]{1,0:T(8,128)(2,1)} %after.24.refs_2_, bf16[128,2048]{1,0:T(8,128)(2,1)} %copy-done.50, bf16[128,2048]{1,0:T(8,128)(2,1)} %collective-permute-done.38.refs_4_, ...), custom_call_target="tpu_custom_call" | custom-call | tf_op jit(solution)/shard_map/outer/pallas_call | solution.py:700
  315.8 21.3 %gated_back.1.refs_10_ = bf16[2048,2048]{1,0:T(8,128)(2,1)} custom-call(bf16[256,2048]{1,0:T(8,128)(2,1)} %after.22.refs_0_, bf16[256,2048]{1,0:T(8,128)(2,1)} %after.23.refs_1_, bf16[256,2048]{1,0:T(8,128)(2,1)} %after.24.refs_2_, bf16[128,2048]{1,0:T(8,128)(2,1)} %copy-done.50, bf16[128,2048]{1,0:T(8,128)(2,1)} %collective-permute-done.38.refs_4_, ...), custom_call_target="tpu_custom_call" | custom-call | tf_op jit(solution)/shard_map/gated_back/pallas_call | solution.py:639
  337.0 12.6 %fusion.4 = bf16[1024,2048]{1,0:T(8,128)(2,1)S(1)} fusion(bf16[2048,2048]{1,0:T(8,128)(2,1)} %all-gather.6.cloned.1.call-done.refs_10_, bf16[2048,2048]{1,0:T(8,128)(2,1)} %gated_back.1.refs_10_), kind=kOutput, calls=%fused_computation.10 | convolution fusion | flops 8592031744 | bytes 16777216 | tf_op jit(solution)/shard_map/dot_general | solution.py:33
  349.8 7.1 collective-permute-done.44.refs_11_.refs_0_
  358.8 27.2 %outer.4.refs_1_ = bf16[2048,2048]{1,0:T(8,128)(2,1)} custom-call(bf16[256,2048]{1,0:T(8,128)(2,1)} %get-tuple-element.58.refs_0_, bf16[256,2048]{1,0:T(8,128)(2,1)} %collective-permute-done.26.refs_1_, bf16[256,2048]{1,0:T(8,128)(2,1)} %collective-permute-done.27.refs_2_, bf16[128,2048]{1,0:T(8,128)(2,1)} %collective-permute-done.28.refs_3_, ...), custom_call_target="tpu_custom_call" | custom-call | tf_op jit(solution)/shard_map/outer/pallas_call | solution.py:700
  386.1 6.2 reduce-scatter.4.cloned.1.call-done.refs_2_.refs_0_
  392.3 14.8 %add_convert_fusion.2.refs_1_ = bf16[1024,2048]{1,0:T(8,128)(2,1)} fusion(bf16[1024,2048]{1,0:T(8,128)(2,1)} %after.25, bf16[2048,2048]{1,0:T(8,128)(2,1)} %all-gather.6.cloned.1.call-done.refs_10_, bf16[2048,2048]{1,0:T(8,128)(2,1)} %gated_back.1.refs_10_), kind=kOutput, calls=%fused_computation.2 | convolution fusion | flops 8596226048 | bytes 20971520 | tf_op jit(solution)/shard_map/dot_general | solution.py:33
  407.2 7.5 %convolution_convert_fusion.2 = bf16[1024,2048]{1,0:T(8,128)(2,1)S(1)} fusion(bf16[2048,1024]{1,0:T(8,128)(2,1)} %all-gather.8.cloned.1.call-done.refs_11_, bf16[2048,1024]{1,0:T(8,128)(2,1)} %after.26), kind=kOutput, calls=%fused_computation.12 | convolution fusion | flops 4297064448 | bytes 10485760 | tf_op jit(solution)/shard_map/dot_general | solution.py:33
  418.5 11.2 %collective-permute-done.46 = bf16[128,2048]{1,0:T(8,128)(2,1)S(1)} collective-permute-done((bf16[128,2048]{1,0:T(8,128)(2,1)S(1)}, bf16[128,2048]{1,0:T(8,128)(2,1)S(1)}, u32[]{:S(2)}, u32[]{:S(2)}) %collective-permute-start.46) | collective-permute-done | bytes 524320 | tf_op jit(solution)/shard_map/ppermute | solution.py:748
  432.0 8.6 %collective-permute-done.48 = bf16[128,2048]{1,0:T(8,128)(2,1)S(1)} collective-permute-done((bf16[128,2048]{1,0:T(8,128)(2,1)S(1)}, bf16[128,2048]{1,0:T(8,128)(2,1)S(1)}, u32[]{:S(2)}, u32[]{:S(2)}) %collective-permute-start.48) | collective-permute-done | bytes 524320 | tf_op jit(solution)/shard_map/ppermute | solution.py:748
  440.6 4.2 collective-permute-done.47
  446.8 7.6 %collective-permute-done.49 = bf16[128,2048]{1,0:T(8,128)(2,1)S(1)} collective-permute-done((bf16[128,2048]{1,0:T(8,128)(2,1)S(1)}, bf16[128,2048]{1,0:T(8,128)(2,1)S(1)}, u32[]{:S(2)}, u32[]{:S(2)}) %collective-permute-start.49) | collective-permute-done | bytes 524320 | tf_op jit(solution)/shard_map/ppermute | solution.py:748
  461.5 6.5 add_convert_fusion.1.refs_1_.refs_0_
  471.0 19.5 %collective-permute-done.52.refs_1_.refs_12_ = bf16[256,2048]{1,0:T(8,128)(2,1)} collective-permute-done((bf16[256,2048]{1,0:T(8,128)(2,1)}, bf16[256,2048]{1,0:T(8,128)(2,1)}, u32[]{:S(2)}, u32[]{:S(2)}) %collective-permute-start.52) | collective-permute-done | bytes 1048608 | tf_op jit(solution)/shard_map/ppermute | solution.py:748
  498.5 4.4 collective-permute-done.54.refs_3_.refs_14_
  504.1 3.6 fusion.46
  511.2 9.3 %project.3.grad_ref.refs_1_ = bf16[2048,256]{1,0:T(8,128)(2,1)} custom-call(bf16[256,2048]{1,0:T(8,128)(2,1)} %after.27.refs_0_.refs_11_, bf16[256,2048]{1,0:T(8,128)(2,1)} %collective-permute-done.52.refs_1_.refs_12_, bf16[256,2048]{1,0:T(8,128)(2,1)} %collective-permute-done.53.refs_2_.refs_13_, ...), custom_call_target="tpu_custom_call" | custom-call | flops 4294967296 | bytes 8388608 | tf_op jit(solution)/shard_map/project/pallas_call | solution.py:551
  526.3 32.2 %attend_back.1.refs_10_.refs_0_ = bf16[2048,384]{1,0:T(8,128)(2,1)} custom-call(s32[8]{0:T(128)S(1)} %fusion.35.place_ref, bf16[2048,256]{1,0:T(8,128)(2,1)S(1)} %get-tuple-element.27.query_ref, bf16[2048,128]{1,0:T(8,128)(2,1)S(1)} %copy-done.8, f32[2048,4]{1,0:T(8,128)S(1)} %copy-done.6, bf16[2048,256]{1,0:T(8,128)(2,1)S(1)} %copy-done.4, ...), custom_call_target="tpu_custom_call" | custom-call | flops 38654705664 | bytes 7340032 | tf_op jit(solution)/shard_map/attend_back/pallas_call | solution.py:474
  561.5 4.7 bitcast_dynamic-update-slice_fusion.3
  572.4 17.9 %outer.5.refs_1_ = bf16[2048,640]{1,0:T(8,128)(2,1)} custom-call(bf16[256,2048]{1,0:T(8,128)(2,1)} %after.21.refs_0_, bf16[256,2048]{1,0:T(8,128)(2,1)} %collective-permute-done.6.refs_1_, bf16[256,2048]{1,0:T(8,128)(2,1)} %collective-permute-done.7.refs_2_, bf16[128,2048]{1,0:T(8,128)(2,1)} %collective-permute-done.8.refs_3_, ...), custom_call_target="tpu_custom_call" | custom-call | flops 10737418240 | bytes 33554432 | tf_op jit(solution)/shard_map/outer/pallas_call | solution.py:700
  590.3 3.9 collective-permute-done.69.refs_4_.refs_0_
  595.2 6.1 convolution_convert_fusion
  601.8 7.8 %collective-permute-done.59 = bf16[256,2048]{1,0:T(8,128)(2,1)S(1)} collective-permute-done((bf16[256,2048]{1,0:T(8,128)(2,1)S(1)}, bf16[256,2048]{1,0:T(8,128)(2,1)S(1)}, u32[]{:S(2)}, u32[]{:S(2)}) %collective-permute-start.59) | collective-permute-done | bytes 1048608 | tf_op jit(solution)/shard_map/ppermute | solution.py:751
  610.7 7.3 %add_convert_fusion.refs_1_ = bf16[1024,2048]{1,0:T(8,128)(2,1)} fusion(bf16[1024,2048]{1,0:T(8,128)(2,1)} %collective-permute-done.71, bf16[2048,384]{1,0:T(8,128)(2,1)} %after.30, bf16[2048,640]{1,0:T(8,128)(2,1)} %all-gather.4.cloned.1.call-done), kind=kOutput, calls=%fused_computation | convolution fusion | flops 1616904192 | bytes 10747904 | tf_op jit(solution)/shard_map/dot_general | solution.py:33
  618.0 2.9 fusion.45
  640.7 5.3 broadcast_multiply_fusion
  646.6 12.6 %collective-permute-done.73 = bf16[128,2048]{1,0:T(8,128)(2,1)S(1)} collective-permute-done((bf16[128,2048]{1,0:T(8,128)(2,1)S(1)}, bf16[128,2048]{1,0:T(8,128)(2,1)S(1)}, u32[]{:S(2)}, u32[]{:S(2)}) %collective-permute-start.73) | collective-permute-done | bytes 524320 | tf_op jit(solution)/shard_map/ppermute | solution.py:748
  667.3 7.8 %collective-permute-done.77 = bf16[128,2048]{1,0:T(8,128)(2,1)} collective-permute-done((bf16[128,2048]{1,0:T(8,128)(2,1)S(1)}, bf16[128,2048]{1,0:T(8,128)(2,1)}, u32[]{:S(2)}, u32[]{:S(2)}) %collective-permute-start.77) | collective-permute-done | bytes 524320 | tf_op jit(solution)/shard_map/ppermute | solution.py:748
  687.0 3.8 bitcast_dynamic-update-slice_fusion.1
  708.4 3.3 bitcast_dynamic-update-slice_fusion
  (449 shorter events, 209.5 us)
Async XLA Ops:
  7.2 108.1 %all-gather.4.cloned.1.call-start = ((), (), s32[]{:S(2)}) async-start(), calls=%async_computation.3 | async-start | bytes 3276800 | tf_op jit(solution)/shard_map/all_gather | solution.py:863
  27.2 225.0 %all-gather.6.cloned.1.call-start = ((), (), s32[]{:S(2)}) async-start(), calls=%async_computation.4 | async-start | bytes 10485760 | tf_op jit(solution)/shard_map/all_gather | solution.py:863
  32.4 22.7 %collective-permute-start.4 = (bf16[128,2048]{1,0:T(8,128)(2,1)S(1)}, bf16[128,2048]{1,0:T(8,128)(2,1)S(1)}, u32[]{:S(2)}, u32[]{:S(2)}) collective-permute-start(bf16[128,2048]{1,0:T(8,128)(2,1)S(1)} %get-tuple-element.97), channel_id=1, source_target_pairs={{0,4},{2,6},{4,0},{6,2},{1,5},{3,7},{5,1},{7,3},{8,12},{10,14},{12... | collective-permute-start | bytes 1572872 | tf_op jit(solution)/shard_map/ppermute | solution.py:748
  34.4 22.6 %collective-permute-start.5 = (bf16[128,2048]{1,0:T(8,128)(2,1)S(1)}, bf16[128,2048]{1,0:T(8,128)(2,1)S(1)}, u32[]{:S(2)}, u32[]{:S(2)}) collective-permute-start(bf16[128,2048]{1,0:T(8,128)(2,1)S(1)} %get-tuple-element.73), channel_id=1, source_target_pairs={{0,6},{2,4},{4,2},{6,0},{1,7},{3,5},{5,3},{7,1},{8,14},{10,12},{12... | collective-permute-start | bytes 1572872 | tf_op jit(solution)/shard_map/ppermute | solution.py:748
  57.9 257.9 %all-gather.8.cloned.1.call-start = ((), (), s32[]{:S(2)}) async-start(), calls=%async_computation.5 | async-start | bytes 5242880 | tf_op jit(solution)/shard_map/all_gather | solution.py:863
  59.1 34.3 %collective-permute-start.6 = (bf16[256,2048]{1,0:T(8,128)(2,1)}, bf16[256,2048]{1,0:T(8,128)(2,1)}, u32[]{:S(2)}, u32[]{:S(2)}) collective-permute-start(bf16[256,2048]{1,0:T(8,128)(2,1)} %after.21.refs_0_), channel_id=1, source_target_pairs={{0,2},{2,0},{4,6},{6,4},{1,3},{3,1},{5,7},{7,5},{8,10},{10,8},{12,... | collective-permute-start | bytes 3145736 | tf_op jit(solution)/shard_map/ppermute | solution.py:748
  60.5 34.9 %collective-permute-start.7 = (bf16[256,2048]{1,0:T(8,128)(2,1)}, bf16[256,2048]{1,0:T(8,128)(2,1)}, u32[]{:S(2)}, u32[]{:S(2)}) collective-permute-start(bf16[256,2048]{1,0:T(8,128)(2,1)} %after.21.refs_0_), channel_id=1, source_target_pairs={{0,4},{2,6},{4,0},{6,2},{1,5},{3,7},{5,1},{7,3},{8,12},{10,14},{12... | collective-permute-start | bytes 3145736 | tf_op jit(solution)/shard_map/ppermute | solution.py:748
  64.2 33.2 %collective-permute-start.16 = (bf16[128,1024]{1,0:T(8,128)(2,1)S(1)}, bf16[128,1024]{1,0:T(8,128)(2,1)S(1)}, u32[]{:S(2)}, u32[]{:S(2)}) collective-permute-start(bf16[128,1024]{1,0:T(8,128)(2,1)S(1)} %get-tuple-element.104), channel_id=1, source_target_pairs={{0,2},{2,0},{4,6},{6,4},{1,3},{3,1},{5,7},{7,5},{8,10},{10,8},{12,... | collective-permute-start | bytes 786440 | tf_op jit(solution)/shard_map/ppermute | solution.py:748
  64.5 35.0 %collective-permute-start.17 = (bf16[128,1024]{1,0:T(8,128)(2,1)S(1)}, bf16[128,1024]{1,0:T(8,128)(2,1)S(1)}, u32[]{:S(2)}, u32[]{:S(2)}) collective-permute-start(bf16[128,1024]{1,0:T(8,128)(2,1)S(1)} %get-tuple-element.106), channel_id=1, source_target_pairs={{0,4},{2,6},{4,0},{6,2},{1,5},{3,7},{5,1},{7,3},{8,12},{10,14},{12... | collective-permute-start | bytes 786440 | tf_op jit(solution)/shard_map/ppermute | solution.py:748
  65.1 25.8 %collective-permute-start.15 = (s32[1,1024]{1,0:T(1,128)S(1)}, s32[1,1024]{1,0:T(1,128)S(1)}, u32[]{:S(2)}, u32[]{:S(2)}) collective-permute-start(s32[1,1024]{1,0:T(1,128)S(1)} %copy-done.66), channel_id=1, source_target_pairs={{0,4},{2,6},{4,0},{6,2},{1,5},{3,7},{5,1},{7,3},{8,12},{10,14},{12... | collective-permute-start | bytes 12296 | tf_op jit(solution)/shard_map/ppermute | solution.py:748
  93.5 24.5 %collective-permute-start.10 = (bf16[256,2048]{1,0:T(8,128)(2,1)S(1)}, bf16[256,2048]{1,0:T(8,128)(2,1)}, u32[]{:S(2)}, u32[]{:S(2)}) collective-permute-start(bf16[256,2048]{1,0:T(8,128)(2,1)S(1)} %copy-done.10), channel_id=1, source_target_pairs={{0,1},{1,0},{2,3},{3,2},{4,5},{5,4},{6,7},{7,6},{8,9},{9,8},{10,11... | collective-permute-start | bytes 3145736 | tf_op jit(solution)/shard_map/ppermute | solution.py:751
  99.5 18.5 %collective-permute-start.11 = (bf16[256,2048]{1,0:T(8,128)(2,1)}, bf16[256,2048]{1,0:T(8,128)(2,1)}, u32[]{:S(2)}, u32[]{:S(2)}) collective-permute-start(bf16[256,2048]{1,0:T(8,128)(2,1)} %collective-permute-done.6.refs_1_), channel_id=1, source_target_pairs={{0,1},{1,0},{2,3},{3,2},{4,5},{5,4},{6,7},{7,6},{8,9},{9,8},{10,11... | collective-permute-start | bytes 3145736 | tf_op jit(solution)/shard_map/ppermute | solution.py:751
  99.5 18.5 %collective-permute-start.12 = (bf16[256,2048]{1,0:T(8,128)(2,1)}, bf16[256,2048]{1,0:T(8,128)(2,1)}, u32[]{:S(2)}, u32[]{:S(2)}) collective-permute-start(bf16[256,2048]{1,0:T(8,128)(2,1)} %collective-permute-done.7.refs_2_), channel_id=1, source_target_pairs={{0,1},{1,0},{2,3},{3,2},{4,5},{5,4},{6,7},{7,6},{8,9},{9,8},{10,11... | collective-permute-start | bytes 3145736 | tf_op jit(solution)/shard_map/ppermute | solution.py:751
  163.3 229.0 %reduce-scatter.4.cloned.1.call-start = ((), (), s32[]{:S(2)}) async-start(), calls=%async_computation.6 | async-start | bytes 5242880 | tf_op jit(solution)/shard_map/reduce_scatter | solution.py:866
  163.4 23.7 %collective-permute-start.22 = (bf16[128,2048]{1,0:T(8,128)(2,1)}, bf16[128,2048]{1,0:T(8,128)(2,1)S(1)}, u32[]{:S(2)}, u32[]{:S(2)}) collective-permute-start(bf16[128,2048]{1,0:T(8,128)(2,1)} %get-tuple-element.57), channel_id=1, source_target_pairs={{0,4},{2,6},{4,0},{6,2},{1,5},{3,7},{5,1},{7,3},{8,12},{10,14},{12... | collective-permute-start | bytes 1572872 | tf_op jit(solution)/shard_map/ppermute | solution.py:748
  163.8 23.3 %collective-permute-start.24 = (bf16[128,2048]{1,0:T(8,128)(2,1)}, bf16[128,2048]{1,0:T(8,128)(2,1)S(1)}, u32[]{:S(2)}, u32[]{:S(2)}) collective-permute-start(bf16[128,2048]{1,0:T(8,128)(2,1)} %get-tuple-element.55), channel_id=1, source_target_pairs={{0,2},{2,0},{4,6},{6,4},{1,3},{3,1},{5,7},{7,5},{8,10},{10,8},{12,... | collective-permute-start | bytes 1572872 | tf_op jit(solution)/shard_map/ppermute | solution.py:748
  179.4 22.4 %collective-permute-start.23 = (bf16[128,2048]{1,0:T(8,128)(2,1)}, bf16[128,2048]{1,0:T(8,128)(2,1)S(1)}, u32[]{:S(2)}, u32[]{:S(2)}) collective-permute-start(bf16[128,2048]{1,0:T(8,128)(2,1)} %get-tuple-element.56), channel_id=1, source_target_pairs={{0,2},{2,0},{4,6},{6,4},{1,3},{3,1},{5,7},{7,5},{8,10},{10,8},{12,... | collective-permute-start | bytes 1572872 | tf_op jit(solution)/shard_map/ppermute | solution.py:748
  207.6 21.1 %collective-permute-start.26 = (bf16[256,2048]{1,0:T(8,128)(2,1)}, bf16[256,2048]{1,0:T(8,128)(2,1)}, u32[]{:S(2)}, u32[]{:S(2)}) collective-permute-start(bf16[256,2048]{1,0:T(8,128)(2,1)} %get-tuple-element.58.refs_0_), channel_id=1, source_target_pairs={{0,2},{2,0},{4,6},{6,4},{1,3},{3,1},{5,7},{7,5},{8,10},{10,8},{12,... | collective-permute-start | bytes 3145736 | tf_op jit(solution)/shard_map/ppermute | solution.py:748
  209.4 23.6 %collective-permute-start.27 = (bf16[256,2048]{1,0:T(8,128)(2,1)}, bf16[256,2048]{1,0:T(8,128)(2,1)}, u32[]{:S(2)}, u32[]{:S(2)}) collective-permute-start(bf16[256,2048]{1,0:T(8,128)(2,1)} %get-tuple-element.58.refs_0_), channel_id=1, source_target_pairs={{0,4},{2,6},{4,0},{6,2},{1,5},{3,7},{5,1},{7,3},{8,12},{10,14},{12... | collective-permute-start | bytes 3145736 | tf_op jit(solution)/shard_map/ppermute | solution.py:748
  209.6 39.5 %collective-permute-start.30 = (bf16[256,2048]{1,0:T(8,128)(2,1)}, bf16[256,2048]{1,0:T(8,128)(2,1)}, u32[]{:S(2)}, u32[]{:S(2)}) collective-permute-start(bf16[256,2048]{1,0:T(8,128)(2,1)} %get-tuple-element.58.refs_0_), channel_id=1, source_target_pairs={{0,1},{1,0},{2,3},{3,2},{4,5},{5,4},{6,7},{7,6},{8,9},{9,8},{10,11... | collective-permute-start | bytes 3145736 | tf_op jit(solution)/shard_map/ppermute | solution.py:751
  231.5 17.7 %collective-permute-start.31 = (bf16[256,2048]{1,0:T(8,128)(2,1)}, bf16[256,2048]{1,0:T(8,128)(2,1)}, u32[]{:S(2)}, u32[]{:S(2)}) collective-permute-start(bf16[256,2048]{1,0:T(8,128)(2,1)} %collective-permute-done.26.refs_1_), channel_id=1, source_target_pairs={{0,1},{1,0},{2,3},{3,2},{4,5},{5,4},{6,7},{7,6},{8,9},{9,8},{10,11... | collective-permute-start | bytes 3145736 | tf_op jit(solution)/shard_map/ppermute | solution.py:751
  234.1 15.6 %collective-permute-start.32 = (bf16[256,2048]{1,0:T(8,128)(2,1)}, bf16[256,2048]{1,0:T(8,128)(2,1)}, u32[]{:S(2)}, u32[]{:S(2)}) collective-permute-start(bf16[256,2048]{1,0:T(8,128)(2,1)} %collective-permute-done.27.refs_2_), channel_id=1, source_target_pairs={{0,1},{1,0},{2,3},{3,2},{4,5},{5,4},{6,7},{7,6},{8,9},{9,8},{10,11... | collective-permute-start | bytes 3145736 | tf_op jit(solution)/shard_map/ppermute | solution.py:751
  247.1 30.9 %collective-permute-start.36 = (bf16[256,2048]{1,0:T(8,128)(2,1)}, bf16[256,2048]{1,0:T(8,128)(2,1)}, u32[]{:S(2)}, u32[]{:S(2)}) collective-permute-start(bf16[256,2048]{1,0:T(8,128)(2,1)} %after.22.refs_0_), channel_id=1, source_target_pairs={{0,4},{2,6},{4,0},{6,2},{1,5},{3,7},{5,1},{7,3},{8,12},{10,14},{12... | collective-permute-start | bytes 3145736 | tf_op jit(solution)/shard_map/ppermute | solution.py:748
  247.5 32.9 %collective-permute-start.35 = (bf16[256,2048]{1,0:T(8,128)(2,1)}, bf16[256,2048]{1,0:T(8,128)(2,1)}, u32[]{:S(2)}, u32[]{:S(2)}) collective-permute-start(bf16[256,2048]{1,0:T(8,128)(2,1)} %after.22.refs_0_), channel_id=1, source_target_pairs={{0,2},{2,0},{4,6},{6,4},{1,3},{3,1},{5,7},{7,5},{8,10},{10,8},{12,... | collective-permute-start | bytes 3145736 | tf_op jit(solution)/shard_map/ppermute | solution.py:748
  249.7 45.7 %collective-permute-start.39 = (bf16[256,2048]{1,0:T(8,128)(2,1)}, bf16[256,2048]{1,0:T(8,128)(2,1)}, u32[]{:S(2)}, u32[]{:S(2)}) collective-permute-start(bf16[256,2048]{1,0:T(8,128)(2,1)} %after.22.refs_0_), channel_id=1, source_target_pairs={{0,1},{1,0},{2,3},{3,2},{4,5},{5,4},{6,7},{7,6},{8,9},{9,8},{10,11... | collective-permute-start | bytes 3145736 | tf_op jit(solution)/shard_map/ppermute | solution.py:751
  279.9 16.8 %collective-permute-start.41 = (bf16[256,2048]{1,0:T(8,128)(2,1)}, bf16[256,2048]{1,0:T(8,128)(2,1)}, u32[]{:S(2)}, u32[]{:S(2)}) collective-permute-start(bf16[256,2048]{1,0:T(8,128)(2,1)} %after.24.refs_2_), channel_id=1, source_target_pairs={{0,1},{1,0},{2,3},{3,2},{4,5},{5,4},{6,7},{7,6},{8,9},{9,8},{10,11... | collective-permute-start | bytes 3145736 | tf_op jit(solution)/shard_map/ppermute | solution.py:751
  315.7 250.5 %reduce-scatter.6.cloned.1.call-start = ((), (), s32[]{:S(2)}) async-start(), calls=%async_computation.7 | async-start | bytes 10485760 | tf_op jit(solution)/shard_map/reduce_scatter | solution.py:866
  386.0 292.4 %reduce-scatter.8.cloned.1.call-start = ((), (), s32[]{:S(2)}) async-start(), calls=%async_computation.8 | async-start | bytes 3276800 | tf_op jit(solution)/shard_map/reduce_scatter | solution.py:866
  414.7 45.4 %collective-permute-start.45 = (bf16[1024,2048]{1,0:T(8,128)(2,1)S(1)}, bf16[1024,2048]{1,0:T(8,128)(2,1)S(1)}, u32[]{:S(2)}, u32[]{:S(2)}) collective-permute-start(bf16[1024,2048]{1,0:T(8,128)(2,1)S(1)} %convolution_convert_fusion.2), channel_id=1, source_target_pairs={{0,1},{1,0},{2,3},{3,2},{4,5},{5,4},{6,7},{7,6},{8,9},{9,8},{10,11... | collective-permute-start | bytes 12582920 | tf_op jit(solution)/shard_map/ppermute | solution.py:751
  416.5 24.1 %collective-permute-start.48 = (bf16[128,2048]{1,0:T(8,128)(2,1)S(1)}, bf16[128,2048]{1,0:T(8,128)(2,1)S(1)}, u32[]{:S(2)}, u32[]{:S(2)}) collective-permute-start(bf16[128,2048]{1,0:T(8,128)(2,1)S(1)} %get-tuple-element.51), channel_id=1, source_target_pairs={{0,4},{2,6},{4,0},{6,2},{1,5},{3,7},{5,1},{7,3},{8,12},{10,14},{12... | collective-permute-start | bytes 1572872 | tf_op jit(solution)/shard_map/ppermute | solution.py:748
  417.1 23.5 %collective-permute-start.50 = (bf16[128,2048]{1,0:T(8,128)(2,1)S(1)}, bf16[128,2048]{1,0:T(8,128)(2,1)S(1)}, u32[]{:S(2)}, u32[]{:S(2)}) collective-permute-start(bf16[128,2048]{1,0:T(8,128)(2,1)S(1)} %get-tuple-element.49), channel_id=1, source_target_pairs={{0,2},{2,0},{4,6},{6,4},{1,3},{3,1},{5,7},{7,5},{8,10},{10,8},{12,... | collective-permute-start | bytes 1572872 | tf_op jit(solution)/shard_map/ppermute | solution.py:748
  431.4 23.0 %collective-permute-start.49 = (bf16[128,2048]{1,0:T(8,128)(2,1)S(1)}, bf16[128,2048]{1,0:T(8,128)(2,1)S(1)}, u32[]{:S(2)}, u32[]{:S(2)}) collective-permute-start(bf16[128,2048]{1,0:T(8,128)(2,1)S(1)} %get-tuple-element.50), channel_id=1, source_target_pairs={{0,2},{2,0},{4,6},{6,4},{1,3},{3,1},{5,7},{7,5},{8,10},{10,8},{12,... | collective-permute-start | bytes 1572872 | tf_op jit(solution)/shard_map/ppermute | solution.py:748
  468.0 22.5 %collective-permute-start.52 = (bf16[256,2048]{1,0:T(8,128)(2,1)}, bf16[256,2048]{1,0:T(8,128)(2,1)}, u32[]{:S(2)}, u32[]{:S(2)}) collective-permute-start(bf16[256,2048]{1,0:T(8,128)(2,1)} %after.27.refs_0_.refs_11_), channel_id=1, source_target_pairs={{0,2},{2,0},{4,6},{6,4},{1,3},{3,1},{5,7},{7,5},{8,10},{10,8},{12,... | collective-permute-start | bytes 3145736 | tf_op jit(solution)/shard_map/ppermute | solution.py:748
  469.5 23.6 %collective-permute-start.53 = (bf16[256,2048]{1,0:T(8,128)(2,1)}, bf16[256,2048]{1,0:T(8,128)(2,1)}, u32[]{:S(2)}, u32[]{:S(2)}) collective-permute-start(bf16[256,2048]{1,0:T(8,128)(2,1)} %after.27.refs_0_.refs_11_), channel_id=1, source_target_pairs={{0,4},{2,6},{4,0},{6,2},{1,5},{3,7},{5,1},{7,3},{8,12},{10,14},{12... | collective-permute-start | bytes 3145736 | tf_op jit(solution)/shard_map/ppermute | solution.py:748
  507.7 50.8 %collective-permute-start.56 = (bf16[256,2048]{1,0:T(8,128)(2,1)}, bf16[256,2048]{1,0:T(8,128)(2,1)}, u32[]{:S(2)}, u32[]{:S(2)}) collective-permute-start(bf16[256,2048]{1,0:T(8,128)(2,1)} %get-tuple-element.43), channel_id=1, source_target_pairs={{0,2},{2,0},{4,6},{6,4},{1,3},{3,1},{5,7},{7,5},{8,10},{10,8},{12,... | collective-permute-start | bytes 3145736 | tf_op jit(solution)/shard_map/ppermute | solution.py:748
  509.2 50.7 %collective-permute-start.57 = (bf16[256,2048]{1,0:T(8,128)(2,1)}, bf16[256,2048]{1,0:T(8,128)(2,1)}, u32[]{:S(2)}, u32[]{:S(2)}) collective-permute-start(bf16[256,2048]{1,0:T(8,128)(2,1)} %get-tuple-element.45), channel_id=1, source_target_pairs={{0,4},{2,6},{4,0},{6,2},{1,5},{3,7},{5,1},{7,3},{8,12},{10,14},{12... | collective-permute-start | bytes 3145736 | tf_op jit(solution)/shard_map/ppermute | solution.py:748
  509.8 50.1 %collective-permute-start.58 = (bf16[256,2048]{1,0:T(8,128)(2,1)}, bf16[256,2048]{1,0:T(8,128)(2,1)}, u32[]{:S(2)}, u32[]{:S(2)}) collective-permute-start(bf16[256,2048]{1,0:T(8,128)(2,1)} %get-tuple-element.44), channel_id=1, source_target_pairs={{0,6},{2,4},{4,2},{6,0},{1,7},{3,5},{5,3},{7,1},{8,14},{10,12},{12... | collective-permute-start | bytes 3145736 | tf_op jit(solution)/shard_map/ppermute | solution.py:748
  522.9 48.1 %collective-permute-start.65 = (bf16[128,1024]{1,0:T(8,128)(2,1)}, bf16[128,1024]{1,0:T(8,128)(2,1)S(1)}, u32[]{:S(2)}, u32[]{:S(2)}) collective-permute-start(bf16[128,1024]{1,0:T(8,128)(2,1)} %get-tuple-element.71), channel_id=1, source_target_pairs={{0,2},{2,0},{4,6},{6,4},{1,3},{3,1},{5,7},{7,5},{8,10},{10,8},{12,... | collective-permute-start | bytes 786440 | tf_op jit(solution)/shard_map/ppermute | solution.py:748
  524.4 48.0 %collective-permute-start.66 = (bf16[128,1024]{1,0:T(8,128)(2,1)}, bf16[128,1024]{1,0:T(8,128)(2,1)}, u32[]{:S(2)}, u32[]{:S(2)}) collective-permute-start(bf16[128,1024]{1,0:T(8,128)(2,1)} %get-tuple-element.70), channel_id=1, source_target_pairs={{0,4},{2,6},{4,0},{6,2},{1,5},{3,7},{5,1},{7,3},{8,12},{10,14},{12... | collective-permute-start | bytes 786440 | tf_op jit(solution)/shard_map/ppermute | solution.py:748
  568.9 21.4 %collective-permute-start.68 = (bf16[128,2048]{1,0:T(8,128)(2,1)}, bf16[128,2048]{1,0:T(8,128)(2,1)S(1)}, u32[]{:S(2)}, u32[]{:S(2)}) collective-permute-start(bf16[128,2048]{1,0:T(8,128)(2,1)} %get-tuple-element.67), channel_id=1, source_target_pairs={{0,2},{2,0},{4,6},{6,4},{1,3},{3,1},{5,7},{7,5},{8,10},{10,8},{12,... | collective-permute-start | bytes 1572872 | tf_op jit(solution)/shard_map/ppermute | solution.py:748
  570.4 23.8 %collective-permute-start.69 = (bf16[128,2048]{1,0:T(8,128)(2,1)}, bf16[128,2048]{1,0:T(8,128)(2,1)S(1)}, u32[]{:S(2)}, u32[]{:S(2)}) collective-permute-start(bf16[128,2048]{1,0:T(8,128)(2,1)} %get-tuple-element.66), channel_id=1, source_target_pairs={{0,4},{2,6},{4,0},{6,2},{1,5},{3,7},{5,1},{7,3},{8,12},{10,14},{12... | collective-permute-start | bytes 1572872 | tf_op jit(solution)/shard_map/ppermute | solution.py:748
  571.1 23.2 %collective-permute-start.70 = (bf16[128,2048]{1,0:T(8,128)(2,1)S(1)}, bf16[128,2048]{1,0:T(8,128)(2,1)S(1)}, u32[]{:S(2)}, u32[]{:S(2)}) collective-permute-start(bf16[128,2048]{1,0:T(8,128)(2,1)S(1)} %get-tuple-element.65), channel_id=1, source_target_pairs={{0,6},{2,4},{4,2},{6,0},{1,7},{3,5},{5,3},{7,1},{8,14},{10,12},{12... | collective-permute-start | bytes 1572872 | tf_op jit(solution)/shard_map/ppermute | solution.py:748
  620.9 17.0 %collective-permute-start.72 = (bf16[128,2048]{1,0:T(8,128)(2,1)}, bf16[128,2048]{1,0:T(8,128)(2,1)S(1)}, u32[]{:S(2)}, u32[]{:S(2)}) collective-permute-start(bf16[128,2048]{1,0:T(8,128)(2,1)} %get-tuple-element.39), channel_id=1, source_target_pairs={{0,4},{2,6},{4,0},{6,2},{1,5},{3,7},{5,1},{7,3},{8,12},{10,14},{12... | collective-permute-start | bytes 1572872 | tf_op jit(solution)/shard_map/ppermute | solution.py:748
  621.5 25.1 %collective-permute-start.74 = (bf16[128,2048]{1,0:T(8,128)(2,1)}, bf16[128,2048]{1,0:T(8,128)(2,1)}, u32[]{:S(2)}, u32[]{:S(2)}) collective-permute-start(bf16[128,2048]{1,0:T(8,128)(2,1)} %get-tuple-element.42), channel_id=1, source_target_pairs={{0,4},{2,6},{4,0},{6,2},{1,5},{3,7},{5,1},{7,3},{8,12},{10,14},{12... | collective-permute-start | bytes 1572872 | tf_op jit(solution)/shard_map/ppermute | solution.py:748
  622.9 23.7 %collective-permute-start.76 = (bf16[128,2048]{1,0:T(8,128)(2,1)}, bf16[128,2048]{1,0:T(8,128)(2,1)}, u32[]{:S(2)}, u32[]{:S(2)}) collective-permute-start(bf16[128,2048]{1,0:T(8,128)(2,1)} %get-tuple-element.40), channel_id=1, source_target_pairs={{0,2},{2,0},{4,6},{6,4},{1,3},{3,1},{5,7},{7,5},{8,10},{10,8},{12,... | collective-permute-start | bytes 1572872 | tf_op jit(solution)/shard_map/ppermute | solution.py:748
  623.5 43.1 %collective-permute-start.75 = (bf16[128,2048]{1,0:T(8,128)(2,1)}, bf16[128,2048]{1,0:T(8,128)(2,1)S(1)}, u32[]{:S(2)}, u32[]{:S(2)}) collective-permute-start(bf16[128,2048]{1,0:T(8,128)(2,1)} %get-tuple-element.41), channel_id=1, source_target_pairs={{0,2},{2,0},{4,6},{6,4},{1,3},{3,1},{5,7},{7,5},{8,10},{10,8},{12,... | collective-permute-start | bytes 1572872 | tf_op jit(solution)/shard_map/ppermute | solution.py:748
  639.1 20.2 %collective-permute-start.73 = (bf16[128,2048]{1,0:T(8,128)(2,1)S(1)}, bf16[128,2048]{1,0:T(8,128)(2,1)S(1)}, u32[]{:S(2)}, u32[]{:S(2)}) collective-permute-start(bf16[128,2048]{1,0:T(8,128)(2,1)S(1)} %add_convert_fusion.6), channel_id=1, source_target_pairs={{0,2},{2,0},{4,6},{6,4},{1,3},{3,1},{5,7},{7,5},{8,10},{10,8},{12,... | collective-permute-start | bytes 1572872 | tf_op jit(solution)/shard_map/ppermute | solution.py:748
  680.2 15.9 %collective-permute-start.79 = (bf16[128,640]{1,0:T(8,128)(2,1)}, bf16[128,640]{1,0:T(8,128)(2,1)S(1)}, u32[]{:S(2)}, u32[]{:S(2)}) collective-permute-start(bf16[128,640]{1,0:T(8,128)(2,1)} %get-tuple-element.111), channel_id=1, source_target_pairs={{0,2},{2,0},{4,6},{6,4},{1,3},{3,1},{5,7},{7,5},{8,10},{10,8},{12,... | collective-permute-start | bytes 491528 | tf_op jit(solution)/shard_map/ppermute | solution.py:748
  (111 other events, 935.5 us)
Sparse Core Ops, SparseCore 0:
  27.3 55.1 all-gather.3
  84.6 148.3 all-gather.5
  235.2 78.9 all-gather.7
  316.4 75.8 reduce-scatter.3
  394.6 144.9 reduce-scatter.5
  610.8 51.2 reduce-scatter.7

commit v3 on v2

--- a/solution.py
+++ b/solution.py
@@ -320,6 +320,14 @@
     return (key <= query) & (key >= start)
 
 
+def each_window(step, rows, window, body):
+    last = window // rows - 1
+    for early in range(last):
+        pl.when(step == early)(functools.partial(body, (early + 1) * rows, 0))
+    first = pl.multiple_of(jnp.maximum(step - last, 0) * rows, rows)
+    pl.when(step >= last)(functools.partial(body, window, first))
+
+
 def attend_kernel(
     rows, window, heads, place_ref, qkv_ref, cos_ref, sin_ref, start_ref, *rest,
 ):
@@ -342,29 +350,31 @@
     keys[own, :] = jnp.where(low_half, kv, moved).astype(jnp.bfloat16)
     values[own, :] = jnp.where(low_half, moved, kv).astype(jnp.bfloat16)
 
-    first_key = pl.multiple_of(jnp.maximum((step + 1) * rows - window, 0), rows)
-    keys_w = keys[pl.ds(first_key, window), :]
-    values_w = values[pl.ds(first_key, window), :]
-    allowed = window_mask(start_ref[...], step * rows, first_key, rows, window)
-    for slab in range(width // LANES):
-        at = slice(slab * LANES, (slab + 1) * LANES)
-        rot = turn(qkv_ref[:, at], cosine, sine).astype(jnp.bfloat16)
-        query_ref[:, at] = rot
-        both = []
-        for part in range(2):
-            mine = low_half if part == 0 else jnp.logical_not(low_half)
-            one = jnp.where(mine, rot, jnp.zeros_like(rot))
-            scores = jnp.where(allowed, dot_nt(one, keys_w) * SCALE, NEG)
-            highest = jnp.max(scores, axis=1, keepdims=True)
-            raised = jnp.exp(scores - highest)
-            total = jnp.sum(raised, axis=1, keepdims=True)
-            mixed = jnp.dot(
-                raised.astype(jnp.bfloat16), values_w, preferred_element_type=jnp.float32
-            )
-            both.append(mixed / total)
-            head = slab * 2 + part
-            lse_ref[:, head : head + 1] = highest + jnp.log(total)
-        mixed_ref[:, at] = jnp.where(low_half, both[0], both[1]).astype(jnp.bfloat16)
+    def windowed(count, first_key):
+        keys_w = keys[pl.ds(first_key, count), :]
+        values_w = values[pl.ds(first_key, count), :]
+        allowed = window_mask(start_ref[...], step * rows, first_key, rows, count)
+        for slab in range(width // LANES):
+            at = slice(slab * LANES, (slab + 1) * LANES)
+            rot = turn(qkv_ref[:, at], cosine, sine).astype(jnp.bfloat16)
+            query_ref[:, at] = rot
+            both = []
+            for part in range(2):
+                mine = low_half if part == 0 else jnp.logical_not(low_half)
+                one = jnp.where(mine, rot, jnp.zeros_like(rot))
+                scores = jnp.where(allowed, dot_nt(one, keys_w) * SCALE, NEG)
+                highest = jnp.max(scores, axis=1, keepdims=True)
+                raised = jnp.exp(scores - highest)
+                total = jnp.sum(raised, axis=1, keepdims=True)
+                mixed = jnp.dot(
+                    raised.astype(jnp.bfloat16), values_w, preferred_element_type=jnp.float32
+                )
+                both.append(mixed / total)
+                head = slab * 2 + part
+                lse_ref[:, head : head + 1] = highest + jnp.log(total)
+            mixed_ref[:, at] = jnp.where(low_half, both[0], both[1]).astype(jnp.bfloat16)
+
+    each_window(step, rows, window, windowed)
 
 
 def attend_back_kernel(
@@ -389,35 +399,38 @@
         d_keys[...] = jnp.zeros_like(d_keys)
         d_values[...] = jnp.zeros_like(d_values)
 
-    first_key = pl.multiple_of(jnp.maximum((step + 1) * rows - window, 0), rows)
-    span = pl.ds(first_key, window)
-    keys_w = keys[span, :]
-    values_w = values[span, :]
-    allowed = window_mask(start_ref[...], step * rows, first_key, rows, window)
-    d_keys_w = jnp.zeros((window, LANES), jnp.float32)
-    d_values_w = jnp.zeros((window, LANES), jnp.float32)
     width = heads * HD
-    for slab in range(width // LANES):
-        at = slice(slab * LANES, (slab + 1) * LANES)
-        query, grad = query_ref[:, at], grad_ref[:, at]
-        both = []
-        for part in range(2):
-            mine = low_half if part == 0 else jnp.logical_not(low_half)
-            head = slab * 2 + part
-            one = jnp.where(mine, query, jnp.zeros_like(query))
-            one_grad = jnp.where(mine, grad, jnp.zeros_like(grad))
-            scores = dot_nt(one, keys_w) * SCALE - lse_ref[:, head : head + 1]
-            probs = jnp.exp(jnp.where(allowed, scores, NEG))
-            d_probs = dot_nt(one_grad, values_w)
-            inner = jnp.sum(probs * d_probs, axis=1, keepdims=True)
-            d_scores = (probs * (d_probs - inner)).astype(jnp.bfloat16)
-            both.append(jnp.dot(d_scores, keys_w, preferred_element_type=jnp.float32))
-            d_keys_w = d_keys_w + dot_tn(d_scores, one)
-            d_values_w = d_values_w + dot_tn(probs.astype(jnp.bfloat16), one_grad)
-        d_query = jnp.where(low_half, both[0], both[1]) * SCALE
-        out_ref[:, at] = (turn(d_query, cosine, -sine) * inv).astype(jnp.bfloat16)
-    d_keys[span, :] += d_keys_w
-    d_values[span, :] += d_values_w
+
+    def windowed(count, first_key):
+        span = pl.ds(first_key, count)
+        keys_w = keys[span, :]
+        values_w = values[span, :]
+        allowed = window_mask(start_ref[...], step * rows, first_key, rows, count)
+        d_keys_w = jnp.zeros((count, LANES), jnp.float32)
+        d_values_w = jnp.zeros((count, LANES), jnp.float32)
+        for slab in range(width // LANES):
+            at = slice(slab * LANES, (slab + 1) * LANES)
+            query, grad = query_ref[:, at], grad_ref[:, at]
+            both = []
+            for part in range(2):
+                mine = low_half if part == 0 else jnp.logical_not(low_half)
+                head = slab * 2 + part
+                one = jnp.where(mine, query, jnp.zeros_like(query))
+                one_grad = jnp.where(mine, grad, jnp.zeros_like(grad))
+                scores = dot_nt(one, keys_w) * SCALE - lse_ref[:, head : head + 1]
+                probs = jnp.exp(jnp.where(allowed, scores, NEG))
+                d_probs = dot_nt(one_grad, values_w)
+                inner = jnp.sum(probs * d_probs, axis=1, keepdims=True)
+                d_scores = (probs * (d_probs - inner)).astype(jnp.bfloat16)
+                both.append(jnp.dot(d_scores, keys_w, preferred_element_type=jnp.float32))
+                d_keys_w = d_keys_w + dot_tn(d_scores, one)
+                d_values_w = d_values_w + dot_tn(probs.astype(jnp.bfloat16), one_grad)
+            d_query = jnp.where(low_half, both[0], both[1]) * SCALE
+            out_ref[:, at] = (turn(d_query, cosine, -sine) * inv).astype(jnp.bfloat16)
+        d_keys[span, :] += d_keys_w
+        d_values[span, :] += d_values_w
+
+    each_window(step, rows, window, windowed)
     own = pl.ds(pl.multiple_of(step * rows, rows), rows)
     d_key = d_keys[own, :] * SCALE
     d_key = turn(d_key + pltpu.roll(d_key, HD, 1), cosine, -sine)
@@ -710,8 +723,55 @@
     )(*operands, *tokens)
 
 
-def add_low(one, other):
-    return (one.astype(jnp.float32) + other.astype(jnp.float32)).astype(jnp.bfloat16)
+def rows_kernel(added, left_ref, weight_ref, *rest):
+    product = dot_nt(left_ref[...], weight_ref[...])
+    if added:
+        product = product + rest[0][...].astype(jnp.float32)
+    rest[-1][...] = product.astype(rest[-1].dtype)
+
+
+def rows_product(left, weight, first, size, add, block):
+    width, depth = weight.shape
+    out = pl.BlockSpec((size, block), lambda j: (0, j))
+    extra = [] if add is None else [add]
+    return pl.pallas_call(
+        functools.partial(rows_kernel, len(extra)),
+        out_shape=jax.ShapeDtypeStruct((size, width), jnp.bfloat16),
+        grid=(width // block,),
+        in_specs=[
+            pl.BlockSpec((size, depth), lambda j: (first // size, 0)),
+            pl.BlockSpec((block, depth), lambda j: (j, 0)),
+        ]
+        + [out] * len(extra),
+        out_specs=out,
+        compiler_params=pltpu.CompilerParams(vmem_limit_bytes=VMEM_LIMIT),
+        name="rows_product",
+    )(left, weight, *extra)
+
+
+def fold_kernel(tokens, mine, from_near, from_ctx, *rest):
+    to_ctx, to_near = rest[tokens:]
+    rows, half = mine.shape[0] // 4, mine.shape[0] // 8
+    ctx_first, near_last = slice(rows, rows + half), slice(2 * rows + half, 3 * rows)
+    to_ctx[...] = (
+        mine[ctx_first, :].astype(jnp.float32) + from_near[...].astype(jnp.float32)
+    ).astype(jnp.bfloat16)
+    to_near[...] = (
+        mine[near_last, :].astype(jnp.float32) + from_ctx[...].astype(jnp.float32)
+    ).astype(jnp.bfloat16)
+
+
+def fold(mine, from_near, from_ctx, tokens):
+    half = jax.ShapeDtypeStruct(from_near.shape, jnp.bfloat16)
+    vmem = pl.BlockSpec(memory_space=pltpu.VMEM)
+    return pl.pallas_call(
+        functools.partial(fold_kernel, len(tokens)),
+        out_shape=[half, half],
+        in_specs=[vmem] * 3 + [ANYWHERE] * len(tokens),
+        out_specs=[vmem] * 2,
+        compiler_params=pltpu.CompilerParams(vmem_limit_bytes=VMEM_LIMIT),
+        name="fold",
+    )(mine, from_near, from_ctx, *tokens)
 
 
 def after_kernel(*refs):
@@ -759,20 +819,19 @@
         same = [own, by_ctx, by_near, *opposite]
         return same + [swap_core(v) for v in same]
 
-    def send_half(product):
-        side = group * rows
-        return swap_core(product(side, side, None, bfloat))
+    def other_side(product):
+        return product(group * rows, group * rows, None)
 
     def own_side(product, other):
-        return product(0, group * rows, other, bfloat)
-
-    def scatter(mine):
+        return product(0, group * rows, other)
+
+    def scatter(mine, *tokens):
         half = rows // 2
         ctx_low, near_low, opposite = (mine[m * rows : (m + 1) * rows] for m in range(1, group))
         from_near, from_ctx = swap(opposite[:half], 2), swap(opposite[half:], 1)
         near_first, ctx_last = swap(near_low[:half], 2), swap(ctx_low[half:], 1)
-        ctx_first = swap(add_low(ctx_low[:half], from_near), 1)
-        near_last = swap(add_low(near_low[half:], from_ctx), 2)
+        to_ctx, to_near = fold(mine, from_near, from_ctx, tokens)
+        ctx_first, near_last = swap(to_ctx, 1), swap(to_near, 2)
         total = jnp.concatenate(
             [
                 mine[:half].astype(jnp.float32)
@@ -783,7 +842,7 @@
                 + near_last.astype(jnp.float32),
             ]
         )
-        return total
+        return total, to_ctx
 
     def scatter_direct(mine):
         total = mine[:rows].astype(jnp.float32)
@@ -792,9 +851,12 @@
         return total
 
     def plain(left, weight):
-        def product(first, size, add, dtype):
+        return lambda first, size, add: rows_product(left, weight, first, size, add, 512)
+
+    def narrow(left, weight):
+        def product(first, size, add):
             out = matmul_trans(left[first : first + size], weight)
-            return (out if add is None else out + add.astype(jnp.float32)).astype(dtype)
+            return (out if add is None else out + add.astype(jnp.float32)).astype(bfloat)
 
         return product
 
@@ -887,16 +949,14 @@
     pair_cols = to_columns(
         scaled(gate_weight, gain_later), scaled(up_weight, gain_later), parts=units // block
     )
-    own_in = after(own_half(hidden_in.reshape(rows_here, width)), pair_cols)
+    seg_others = [swap(segments, n * (group // near)) for n in range(1, near)]
+    own_in = after(own_half(hidden_in.reshape(rows_here, width)), pair_cols, *seg_others)
     inputs = gather(own_in)
     pair_w = far_gather(pair_cols)
     own_cot = own_half(cotangent.reshape(rows_here, width))
-    down_cols = to_columns(down_weight)
-    down_w = far_gather(down_cols)
 
     seg_all = jnp.concatenate(
-        [segments]
-        + [swap(segments, n * (group // near)) for n in range(1, near)],
+        [segments] + seg_others,
         axis=0,
     )
     start = jnp.sum((seg_all[:, None, :] < seg_all[:, :, None]).astype(jnp.int32), axis=2)
@@ -917,11 +977,13 @@
     ).astype(jnp.int32)
 
     qkv, inv_a = project(inputs, in_w, True, None, jnp.float32)
+    down_cols = to_columns(after(down_weight, inv_a))
+    down_w = far_gather(down_cols)
     query, kv, mixed, lse = attend(
-        place, qkv, cosine, sine, start, near, blocks, rows, heads, (down_cols,)
-    )
-    product = plain(mixed, out_w)
-    branch_a = scatter(own_side(product, send_half(product)))
+        place, qkv, cosine, sine, start, near, blocks, rows, heads, ()
+    )
+    product = narrow(after(mixed, down_cols), out_w)
+    branch_a, _ = scatter(own_side(product, swap_core(other_side(product))))
     own_f = own_in.astype(jnp.float32)
     middle = own_f + RESIDUAL * branch_a
 
@@ -932,13 +994,14 @@
     down_far = far_scatter(down_part)
     d_both = gated_back(cots, down_w, gate_pre, upward, inv_f, block, 512, (down_part,))
     product = plain(d_both, pair_w)
-    other = send_half(product)
+    other = other_side(product)
     pair_part = outer([(mids, [d_both])], 256, (other,))
     pair_far = far_scatter(pair_part)
-    back_mine = own_side(product, after(other, pair_part, down_far))
-    back_f = scatter(back_mine)
+    back_mine = own_side(product, after(swap_core(other), pair_part))
     product = plain(after(hidden, back_mine), down_w)
-    branch_mine = own_side(product, send_half(product))
+    other = other_side(product)
+    back_f, _ = scatter(back_mine, other, down_far)
+    branch_mine = own_side(product, swap_core(other))
 
     def through_norm(grad, unit):
         return grad - unit * jnp.mean(grad * unit, axis=-1, keepdims=True)
@@ -957,7 +1020,7 @@
     attn_part = outer(
         [(inputs, [d_qkv]), (d_mids, [mixed])],
         256,
-        (pair_far, middle_out, *down_rows),
+        (pair_far,),
         pl.CostEstimate(
             flops=4 * d_qkv.shape[0] * width * attn_cols_all,
             transcendentals=0,
@@ -966,10 +1029,10 @@
     )
     attn_far = far_scatter(attn_part)
     pair_rows = to_rows(pair_far)
-    product = plain(after(d_qkv, attn_part, *pair_rows), in_w)
-    back_mine = own_side(product, send_half(product))
-    back_a = scatter(back_mine)
-    layer_out = both_halves(middle_out)
+    product = narrow(after(d_qkv, attn_part, middle_out, *down_rows, *pair_rows), in_w)
+    back_mine = own_side(product, swap_core(other_side(product)))
+    back_a, _ = scatter(back_mine)
+    layer_out = both_halves(after(middle_out, back_mine))
     input_grad = d_middle + through_norm(back_a, own_f * inverse_rms(own_f))
     input_grad = both_halves(input_grad)
 

time: 724 us -> 687 us (0.949)
  Pallas kernels: 182 us -> 233 us
  matrix products: 57.4 us -> 18.9 us
  waiting for transfers between devices: 245 us -> 210 us
  other arithmetic: 65.9 us -> 46.4 us
    pallas_call x0 -> x7, Pallas kernels: none -> 56.8 us  [the longest x4 46 us: rows_product(): pl.pallas_call(functools.partial(rows_kernel, len(extra)), out_shape=jax....]
    dot_general x8 -> x4, matrix products: 57.4 us -> 18.9 us  [matmul_trans(): lax.dot_general(left, right, (((1,), (1,)), ((), ())), preferred_element_...]
    ppermute x56, waiting for transfers between devices: 212 us -> 190 us  [swap(): lax.ppermute(value, ('near', 'ctx'), [(i, i ^ m) for i in range(group)])]
    dynamic_update_slice x19, other arithmetic: 26.4 us -> 11.1 us  [put(): return lax.dynamic_update_slice(whole, piece, starts)]
    unnamed x151 -> x183, local copies, waits for them, and re-layouts: 18.4 us -> 30.9 us
    dynamic_update_slice x20 -> x21, local copies, waits for them, and re-layouts: 16.7 us -> 19.5 us  [put(): return lax.dynamic_update_slice(whole, piece, starts)]
  transfers between devices with their start and end apart: 89 -> 89, of which waited for: 39 -> 39; matrix products, arithmetic and copies ran while one was open for 24% -> 17% of each run, Pallas kernels for 25% -> 34%
where the time goes in v3:
time: 687 us; the launch traced here: 682 us
  Pallas kernels  233 us (34%)
  waiting for transfers between devices  210 us (31%)
  local copies, waits for them, and re-layouts  87.1 us (13%)
  starting transfers between devices  71.7 us (10%)
  other arithmetic  46.4 us (7%)
  matrix products  18.9 us (3%)
  between operations  16 us (2%)
    ppermute x56, waiting for transfers between devices, swap(): lax.ppermute(value, ('near', 'ctx'), [(i, i ^ m) for i in range(group)])  190 us
    ppermute x56, starting transfers between devices, swap(): lax.ppermute(value, ('near', 'ctx'), [(i, i ^ m) for i in range(group)])  68 us
    pallas_call x3, Pallas kernels, outer(): pl.pallas_call(functools.partial(outer_kernel, counts, len(tokens), block...  62.5 us
    pallas_call x4, Pallas kernels, rows_product(): pl.pallas_call(functools.partial(rows_kernel, len(extra)), out_shape=jax....  46 us
    unnamed x183, local copies, waits for them, and re-layouts  30.9 us
    pallas_call x1, Pallas kernels, attend_back(): pl.pallas_call(functools.partial(attend_back_kernel, rows, window, heads,...  29 us
    pallas_call x1, Pallas kernels, gated(): pl.pallas_call(functools.partial(gated_kernel, len(pieces), chunk), out_s...  26 us
    pallas_call x1, Pallas kernels, gated_back(): pl.pallas_call(functools.partial(gated_back_kernel, len(pieces), len(othe...  20.7 us
  transfers between devices with their start and end apart: 89, of which 39 were waited for; matrix products, arithmetic and copies ran while one was open for 17% of the time, Pallas kernels for 34%

profile of v3, /device:TPU:0, one launch (start us, length us, event | category | flops | bytes accessed | tf_op | source)
XLA Modules:
  0.0 682.3 jit_solution(11397440445917868043)
XLA Ops:
  10.9 3.0 collective-permute-start
  18.7 4.7 collective-permute-done.1
  37.1 9.0 %collective-permute-done.3 = bf16[128,2048]{1,0:T(8,128)(2,1)S(1)} collective-permute-done((bf16[128,2048]{1,0:T(8,128)(2,1)S(1)}, bf16[128,2048]{1,0:T(8,128)(2,1)S(1)}, u32[]{:S(2)}, u32[]{:S(2)}) %collective-permute-start.3) | collective-permute-done | bytes 524320 | tf_op jit(solution)/shard_map/ppermute | solution.py:808
  46.9 7.2 %collective-permute-done.4 = bf16[128,2048]{1,0:T(8,128)(2,1)S(1)} collective-permute-done((bf16[128,2048]{1,0:T(8,128)(2,1)S(1)}, bf16[128,2048]{1,0:T(8,128)(2,1)S(1)}, u32[]{:S(2)}, u32[]{:S(2)}) %collective-permute-start.4) | collective-permute-done | bytes 524320 | tf_op jit(solution)/shard_map/ppermute | solution.py:808
  64.5 19.9 %collective-permute-done.7.refs_1_ = bf16[256,2048]{1,0:T(8,128)(2,1)S(1)} collective-permute-done((bf16[256,2048]{1,0:T(8,128)(2,1)}, bf16[256,2048]{1,0:T(8,128)(2,1)S(1)}, u32[]{:S(2)}, u32[]{:S(2)}) %collective-permute-start.7) | collective-permute-done | bytes 1048608 | tf_op jit(solution)/shard_map/ppermute | solution.py:808
  84.7 4.0 collective-permute-start.10
  90.4 4.6 collective-permute-done.9.refs_3_
  96.0 5.5 fusion.16
  101.5 2.7 slice.495.refs_10_
  104.3 10.7 %project.2 = (f32[2048,384]{1,0:T(8,128)}, f32[2048,1]{1,0:T(8,128)}) custom-call(bf16[256,2048]{1,0:T(8,128)(2,1)} %after.24.refs_0_, bf16[256,2048]{1,0:T(8,128)(2,1)} %copy-done.71, bf16[256,2048]{1,0:T(8,128)(2,1)} %copy-done.72, bf16[128,2048]{1,0:T(8,128)(2,1)} %collective-permute-done.9.refs_3_, bf16[128,2048]{1,0:T(8,128)(2,1)} %collective-permute-done.10.refs_4_, ...), custom_call_target="tpu_custom_call" | custom-call | flops 6442450944 | bytes 8388608 | tf_op jit(solution)/shard_map/project/pallas_call | solution.py:564
  124.9 17.5 %attend.1 = (bf16[2048,256]{1,0:T(8,128)(2,1)S(1)}, bf16[2048,128]{1,0:T(8,128)(2,1)S(1)}, bf16[2048,256]{1,0:T(8,128)(2,1)S(1)}, f32[2048,4]{1,0:T(8,128)S(1)}) custom-call(s32[8]{0:T(128)S(1)} %fusion.24.place_ref, f32[2048,384]{1,0:T(8,128)} %get-tuple-element.27.qkv_ref, f32[2048,128]{1,0:T(8,128)S(1)} %get-tuple-element.209.cos_ref, ...), custom_call_target="tpu_custom_call" | custom-call | tf_op jit(solution)/shard_map/attend/pallas_call | solution.py:453
  149.3 4.8 convolution_convert_fusion.1
  154.1 7.4 %collective-permute-done.19 = bf16[1024,2048]{1,0:T(8,128)(2,1)} collective-permute-done((bf16[1024,2048]{1,0:T(8,128)(2,1)}, bf16[1024,2048]{1,0:T(8,128)(2,1)}, u32[]{:S(2)}, u32[]{:S(2)}) %collective-permute-start.19) | collective-permute-done | bytes 4194336 | tf_op jit(solution)/shard_map/ppermute | solution.py:811
  161.6 3.8 add_convert_fusion.1.mine
  171.5 10.7 %collective-permute-done.20.from_near = bf16[128,2048]{1,0:T(8,128)(2,1)S(1)} collective-permute-done((bf16[128,2048]{1,0:T(8,128)(2,1)S(1)}, bf16[128,2048]{1,0:T(8,128)(2,1)S(1)}, u32[]{:S(2)}, u32[]{:S(2)}) %collective-permute-start.20) | collective-permute-done | bytes 524320 | tf_op jit(solution)/shard_map/ppermute | solution.py:808
  183.8 3.6 fold.3
  190.6 2.8 collective-permute-done.23
  194.0 10.2 %collective-permute-done.22 = bf16[128,2048]{1,0:T(8,128)(2,1)S(1)} collective-permute-done((bf16[128,2048]{1,0:T(8,128)(2,1)}, bf16[128,2048]{1,0:T(8,128)(2,1)S(1)}, u32[]{:S(2)}, u32[]{:S(2)}) %collective-permute-start.22) | collective-permute-done | bytes 524320 | tf_op jit(solution)/shard_map/ppermute | solution.py:808
  210.9 21.3 %collective-permute-done.26.refs_1_ = bf16[256,2048]{1,0:T(8,128)(2,1)} collective-permute-done((bf16[256,2048]{1,0:T(8,128)(2,1)}, bf16[256,2048]{1,0:T(8,128)(2,1)}, u32[]{:S(2)}, u32[]{:S(2)}) %collective-permute-start.26) | collective-permute-done | bytes 1048608 | tf_op jit(solution)/shard_map/ppermute | solution.py:808
  239.0 6.7 collective-permute-done.28.refs_3_
  245.6 5.0 collective-permute-done.29.refs_4_
  255.7 26.0 %gated.1 = (bf16[2048,1024]{1,0:T(8,128)(2,1)}, bf16[2048,1024]{1,0:T(8,128)(2,1)}, bf16[2048,1024]{1,0:T(8,128)(2,1)}, f32[2048,1]{1,0:T(8,128)}) custom-call(bf16[256,2048]{1,0:T(8,128)(2,1)} %get-tuple-element.68.refs_0_, bf16[256,2048]{1,0:T(8,128)(2,1)} %collective-permute-done.26.refs_1_, bf16[256,2048]{1,0:T(8,128)(2,1)} %collective-permute-done.27.refs_2_, ...), custom_call_target="tpu_custom_call" | custom-call | tf_op jit(solution)/shard_map/gated/pallas_call | solution.py:609
  286.9 11.4 %collective-permute-done.38.refs_4_ = bf16[128,2048]{1,0:T(8,128)(2,1)} collective-permute-done((bf16[128,2048]{1,0:T(8,128)(2,1)}, bf16[128,2048]{1,0:T(8,128)(2,1)}, u32[]{:S(2)}, u32[]{:S(2)}) %collective-permute-start.38) | collective-permute-done | bytes 524320 | tf_op jit(solution)/shard_map/ppermute | solution.py:808
  302.2 17.1 %outer.3.refs_10_ = bf16[2048,1024]{1,0:T(8,128)(2,1)} custom-call(bf16[256,2048]{1,0:T(8,128)(2,1)} %after.27.refs_0_, bf16[256,2048]{1,0:T(8,128)(2,1)} %after.28.refs_1_, bf16[256,2048]{1,0:T(8,128)(2,1)} %after.29.refs_2_, bf16[128,2048]{1,0:T(8,128)(2,1)} %copy-done.57, bf16[128,2048]{1,0:T(8,128)(2,1)} %collective-permute-done.38.refs_4_, ...), custom_call_target="tpu_custom_call" | custom-call | tf_op jit(solution)/shard_map/outer/pallas_call | solution.py:713
  319.4 20.7 %gated_back.1.left_ref.refs_10_ = bf16[2048,2048]{1,0:T(8,128)(2,1)} custom-call(bf16[256,2048]{1,0:T(8,128)(2,1)} %after.27.refs_0_, bf16[256,2048]{1,0:T(8,128)(2,1)} %after.28.refs_1_, bf16[256,2048]{1,0:T(8,128)(2,1)} %after.29.refs_2_, bf16[128,2048]{1,0:T(8,128)(2,1)} %copy-done.57, bf16[128,2048]{1,0:T(8,128)(2,1)} %collective-permute-done.38.refs_4_, ...), custom_call_target="tpu_custom_call" | custom-call | tf_op jit(solution)/shard_map/gated_back/pallas_call | solution.py:652
  340.1 13.3 %rows_product.4.refs_11_ = bf16[1024,2048]{1,0:T(8,128)(2,1)} custom-call(bf16[2048,2048]{1,0:T(8,128)(2,1)} %gated_back.1.left_ref.refs_10_, bf16[2048,2048]{1,0:T(8,128)(2,1)} %all-gather.6.cloned.1.call-done.refs_10_.weight_ref), custom_call_target="tpu_custom_call" | custom-call | tf_op jit(solution)/shard_map/rows_product/pallas_call | solution.py:737
  353.5 27.3 %outer.4.refs_1_ = bf16[2048,2048]{1,0:T(8,128)(2,1)} custom-call(bf16[256,2048]{1,0:T(8,128)(2,1)} %get-tuple-element.68.refs_0_, bf16[256,2048]{1,0:T(8,128)(2,1)} %collective-permute-done.26.refs_1_, bf16[256,2048]{1,0:T(8,128)(2,1)} %collective-permute-done.27.refs_2_, bf16[128,2048]{1,0:T(8,128)(2,1)} %collective-permute-done.28.refs_3_, ...), custom_call_target="tpu_custom_call" | custom-call | tf_op jit(solution)/shard_map/outer/pallas_call | solution.py:713
  380.8 14.5 %rows_product.5.refs_1_.mine = bf16[1024,2048]{1,0:T(8,128)(2,1)} custom-call(bf16[2048,2048]{1,0:T(8,128)(2,1)} %gated_back.1.left_ref.refs_10_, bf16[2048,2048]{1,0:T(8,128)(2,1)} %all-gather.6.cloned.1.call-done.refs_10_.weight_ref, bf16[1024,2048]{1,0:T(8,128)(2,1)} %after.30.rest_0_), custom_call_target="tpu_custom_call" | custom-call | tf_op jit(solution)/shard_map/rows_product/pallas_call | solution.py:737
  395.3 8.7 %rows_product.6.rest_0_ = bf16[1024,2048]{1,0:T(8,128)(2,1)} custom-call(bf16[2048,1024]{1,0:T(8,128)(2,1)} %after.31.left_ref, bf16[2048,1024]{1,0:T(8,128)(2,1)} %all-gather.8.cloned.1.call-done.refs_11_.weight_ref), custom_call_target="tpu_custom_call" | custom-call | tf_op jit(solution)/shard_map/rows_product/pallas_call | solution.py:737
  409.8 10.8 %collective-permute-done.46.from_near = bf16[128,2048]{1,0:T(8,128)(2,1)} collective-permute-done((bf16[128,2048]{1,0:T(8,128)(2,1)S(1)}, bf16[128,2048]{1,0:T(8,128)(2,1)}, u32[]{:S(2)}, u32[]{:S(2)}) %collective-permute-start.46) | collective-permute-done | bytes 524320 | tf_op jit(solution)/shard_map/ppermute | solution.py:808
  422.3 3.6 fold.4
  428.0 9.6 %rows_product.7.refs_1_.refs_0_ = bf16[1024,2048]{1,0:T(8,128)(2,1)} custom-call(bf16[2048,1024]{1,0:T(8,128)(2,1)} %after.31.left_ref, bf16[2048,1024]{1,0:T(8,128)(2,1)} %all-gather.8.cloned.1.call-done.refs_11_.weight_ref, bf16[1024,2048]{1,0:T(8,128)(2,1)} %collective-permute-done.45.rest_0_), custom_call_target="tpu_custom_call" | custom-call | tf_op jit(solution)/shard_map/rows_product/pallas_call | solution.py:737
  437.6 5.7 collective-permute-done.48
  451.6 22.0 %collective-permute-done.52.refs_1_.refs_12_ = bf16[256,2048]{1,0:T(8,128)(2,1)S(1)} collective-permute-done((bf16[256,2048]{1,0:T(8,128)(2,1)}, bf16[256,2048]{1,0:T(8,128)(2,1)S(1)}, u32[]{:S(2)}, u32[]{:S(2)}) %collective-permute-start.52) | collective-permute-done | bytes 1048608 | tf_op jit(solution)/shard_map/ppermute | solution.py:808
  479.9 6.3 collective-permute-done.54.refs_3_.refs_14_
  487.8 3.7 fusion.35
  495.0 9.3 %project.3.grad_ref.refs_1_ = bf16[2048,256]{1,0:T(8,128)(2,1)} custom-call(bf16[256,2048]{1,0:T(8,128)(2,1)} %after.32.refs_0_.refs_11_, bf16[256,2048]{1,0:T(8,128)(2,1)} %copy-done.56, bf16[256,2048]{1,0:T(8,128)(2,1)} %collective-permute-done.53.refs_2_.refs_13_, bf16[128,2048]{1,0:T(8,128)(2,1)} %collective-permute-done.54.refs_3_.refs_14_, ...), custom_call_target="tpu_custom_call" | custom-call | flops 4294967296 | bytes 8388608 | tf_op jit(solution)/shard_map/project/pallas_call | solution.py:564
  510.2 29.0 %attend_back.1.refs_10_.refs_0_ = bf16[2048,384]{1,0:T(8,128)(2,1)} custom-call(s32[8]{0:T(128)S(1)} %fusion.24.place_ref, bf16[2048,256]{1,0:T(8,128)(2,1)S(1)} %copy-done.7, bf16[2048,128]{1,0:T(8,128)(2,1)S(1)} %copy-done.11, f32[2048,4]{1,0:T(8,128)S(1)} %copy-done.9, bf16[2048,256]{1,0:T(8,128)(2,1)S(1)} %copy-done.4, f32[2048,1]{1,0:T(8,128)S(1)} %copy-done.3, ...), custom_call_target="tpu_custom_call" | custom-call | flops 38654705664 | bytes 7340032 | tf_op jit(solution)/shard_map/attend_back/pallas_call | solution.py:487
  541.4 4.4 add_convert_fusion.2.refs_2_.refs_0_
  552.0 18.2 %outer.5.refs_1_ = bf16[2048,640]{1,0:T(8,128)(2,1)} custom-call(bf16[256,2048]{1,0:T(8,128)(2,1)} %after.24.refs_0_, bf16[256,2048]{1,0:T(8,128)(2,1)} %copy-done.71, bf16[256,2048]{1,0:T(8,128)(2,1)} %copy-done.72, bf16[128,2048]{1,0:T(8,128)(2,1)} %collective-permute-done.9.refs_3_, bf16[128,2048]{1,0:T(8,128)(2,1)} %collective-permute-done.10.refs_4_, ...), custom_call_target="tpu_custom_call" | custom-call | flops 10737418240 | bytes 33554432 | tf_op jit(solution)/shard_map/outer/pallas_call | solution.py:713
  570.2 4.1 collective-permute-done.68.refs_9_.refs_0_
  577.0 5.5 convolution_convert_fusion
  582.5 7.5 %collective-permute-done.70 = bf16[1024,2048]{1,0:T(8,128)(2,1)} collective-permute-done((bf16[1024,2048]{1,0:T(8,128)(2,1)}, bf16[1024,2048]{1,0:T(8,128)(2,1)}, u32[]{:S(2)}, u32[]{:S(2)}) %collective-permute-start.70) | collective-permute-done | bytes 4194336 | tf_op jit(solution)/shard_map/ppermute | solution.py:811
  590.0 4.8 add_convert_fusion.refs_1_.mine
  608.6 2.8 broadcast_multiply_fusion
  614.9 3.6 fold.5
  625.4 10.1 %collective-permute-done.74 = bf16[128,2048]{1,0:T(8,128)(2,1)S(1)} collective-permute-done((bf16[128,2048]{1,0:T(8,128)(2,1)}, bf16[128,2048]{1,0:T(8,128)(2,1)S(1)}, u32[]{:S(2)}, u32[]{:S(2)}) %collective-permute-start.74) | collective-permute-done | bytes 524320 | tf_op jit(solution)/shard_map/ppermute | solution.py:808
  647.7 3.8 bitcast_dynamic-update-slice_fusion.1
  (481 shorter events, 197.4 us)
Async XLA Ops:
  7.3 94.3 %all-gather.4.cloned.1.call-start = ((), (), s32[]{:S(2)}) async-start(), calls=%async_computation.3 | async-start | bytes 3276800 | tf_op jit(solution)/shard_map/all_gather | solution.py:925
  26.1 229.6 %all-gather.6.cloned.1.call-start = ((), (), s32[]{:S(2)}) async-start(), calls=%async_computation.4 | async-start | bytes 10485760 | tf_op jit(solution)/shard_map/all_gather | solution.py:925
  31.4 22.7 %collective-permute-start.4 = (bf16[128,2048]{1,0:T(8,128)(2,1)S(1)}, bf16[128,2048]{1,0:T(8,128)(2,1)S(1)}, u32[]{:S(2)}, u32[]{:S(2)}) collective-permute-start(bf16[128,2048]{1,0:T(8,128)(2,1)S(1)} %get-tuple-element.111), channel_id=1, source_target_pairs={{0,4},{2,6},{4,0},{6,2},{1,5},{3,7},{5,1},{7,3},{8,12},{10,14},{12... | collective-permute-start | bytes 1572872 | tf_op jit(solution)/shard_map/ppermute | solution.py:808
  33.3 22.6 %collective-permute-start.5 = (bf16[128,2048]{1,0:T(8,128)(2,1)S(1)}, bf16[128,2048]{1,0:T(8,128)(2,1)S(1)}, u32[]{:S(2)}, u32[]{:S(2)}) collective-permute-start(bf16[128,2048]{1,0:T(8,128)(2,1)S(1)} %get-tuple-element.87), channel_id=1, source_target_pairs={{0,6},{2,4},{4,2},{6,0},{1,7},{3,5},{5,3},{7,1},{8,14},{10,12},{12... | collective-permute-start | bytes 1572872 | tf_op jit(solution)/shard_map/ppermute | solution.py:808
  56.8 262.6 %all-gather.8.cloned.1.call-start = ((), (), s32[]{:S(2)}) async-start(), calls=%async_computation.5 | async-start | bytes 5242880 | tf_op jit(solution)/shard_map/all_gather | solution.py:925
  61.3 23.2 %collective-permute-start.7 = (bf16[256,2048]{1,0:T(8,128)(2,1)}, bf16[256,2048]{1,0:T(8,128)(2,1)S(1)}, u32[]{:S(2)}, u32[]{:S(2)}) collective-permute-start(bf16[256,2048]{1,0:T(8,128)(2,1)} %after.24.refs_0_), channel_id=1, source_target_pairs={{0,2},{2,0},{4,6},{6,4},{1,3},{3,1},{5,7},{7,5},{8,10},{10,8},{12,... | collective-permute-start | bytes 3145736 | tf_op jit(solution)/shard_map/ppermute | solution.py:808
  62.7 21.9 %collective-permute-start.8 = (bf16[256,2048]{1,0:T(8,128)(2,1)}, bf16[256,2048]{1,0:T(8,128)(2,1)S(1)}, u32[]{:S(2)}, u32[]{:S(2)}) collective-permute-start(bf16[256,2048]{1,0:T(8,128)(2,1)} %after.24.refs_0_), channel_id=1, source_target_pairs={{0,4},{2,6},{4,0},{6,2},{1,5},{3,7},{5,1},{7,3},{8,12},{10,14},{12... | collective-permute-start | bytes 3145736 | tf_op jit(solution)/shard_map/ppermute | solution.py:808
  64.5 39.8 %collective-permute-start.11 = (bf16[256,2048]{1,0:T(8,128)(2,1)}, bf16[256,2048]{1,0:T(8,128)(2,1)}, u32[]{:S(2)}, u32[]{:S(2)}) collective-permute-start(bf16[256,2048]{1,0:T(8,128)(2,1)} %after.24.refs_0_), channel_id=1, source_target_pairs={{0,1},{1,0},{2,3},{3,2},{4,5},{5,4},{6,7},{7,6},{8,9},{9,8},{10,11... | collective-permute-start | bytes 3145736 | tf_op jit(solution)/shard_map/ppermute | solution.py:811
  118.3 26.9 %collective-permute-start.16 = (bf16[128,1024]{1,0:T(8,128)(2,1)}, bf16[128,1024]{1,0:T(8,128)(2,1)}, u32[]{:S(2)}, u32[]{:S(2)}) collective-permute-start(bf16[128,1024]{1,0:T(8,128)(2,1)} %get-tuple-element.85), channel_id=1, source_target_pairs={{0,2},{2,0},{4,6},{6,4},{1,3},{3,1},{5,7},{7,5},{8,10},{10,8},{12,... | collective-permute-start | bytes 786440 | tf_op jit(solution)/shard_map/ppermute | solution.py:808
  120.3 26.5 %collective-permute-start.17 = (bf16[128,1024]{1,0:T(8,128)(2,1)}, bf16[128,1024]{1,0:T(8,128)(2,1)}, u32[]{:S(2)}, u32[]{:S(2)}) collective-permute-start(bf16[128,1024]{1,0:T(8,128)(2,1)} %get-tuple-element.84), channel_id=1, source_target_pairs={{0,4},{2,6},{4,0},{6,2},{1,5},{3,7},{5,1},{7,3},{8,12},{10,14},{12... | collective-permute-start | bytes 786440 | tf_op jit(solution)/shard_map/ppermute | solution.py:808
  120.8 27.8 %collective-permute-start.18 = (bf16[128,1024]{1,0:T(8,128)(2,1)}, bf16[128,1024]{1,0:T(8,128)(2,1)S(1)}, u32[]{:S(2)}, u32[]{:S(2)}) collective-permute-start(bf16[128,1024]{1,0:T(8,128)(2,1)} %get-tuple-element.83), channel_id=1, source_target_pairs={{0,6},{2,4},{4,2},{6,0},{1,7},{3,5},{5,3},{7,1},{8,14},{10,12},{12... | collective-permute-start | bytes 786440 | tf_op jit(solution)/shard_map/ppermute | solution.py:808
  154.1 268.2 %reduce-scatter.4.cloned.1.call-start = ((), (), s32[]{:S(2)}) async-start(), calls=%async_computation.6 | async-start | bytes 5242880 | tf_op jit(solution)/shard_map/reduce_scatter | solution.py:928
  169.8 23.6 %collective-permute-start.23 = (bf16[128,2048]{1,0:T(8,128)(2,1)S(1)}, bf16[128,2048]{1,0:T(8,128)(2,1)S(1)}, u32[]{:S(2)}, u32[]{:S(2)}) collective-permute-start(bf16[128,2048]{1,0:T(8,128)(2,1)S(1)} %get-tuple-element.64), channel_id=1, source_target_pairs={{0,4},{2,6},{4,0},{6,2},{1,5},{3,7},{5,1},{7,3},{8,12},{10,14},{12... | collective-permute-start | bytes 1572872 | tf_op jit(solution)/shard_map/ppermute | solution.py:808
  171.4 22.6 %collective-permute-start.24 = (bf16[128,2048]{1,0:T(8,128)(2,1)S(1)}, bf16[128,2048]{1,0:T(8,128)(2,1)S(1)}, u32[]{:S(2)}, u32[]{:S(2)}) collective-permute-start(bf16[128,2048]{1,0:T(8,128)(2,1)S(1)} %get-tuple-element.65), channel_id=1, source_target_pairs={{0,2},{2,0},{4,6},{6,4},{1,3},{3,1},{5,7},{7,5},{8,10},{10,8},{12,... | collective-permute-start | bytes 1572872 | tf_op jit(solution)/shard_map/ppermute | solution.py:808
  187.4 16.9 %collective-permute-start.22 = (bf16[128,2048]{1,0:T(8,128)(2,1)}, bf16[128,2048]{1,0:T(8,128)(2,1)S(1)}, u32[]{:S(2)}, u32[]{:S(2)}) collective-permute-start(bf16[128,2048]{1,0:T(8,128)(2,1)} %get-tuple-element.30), channel_id=1, source_target_pairs={{0,2},{2,0},{4,6},{6,4},{1,3},{3,1},{5,7},{7,5},{8,10},{10,8},{12,... | collective-permute-start | bytes 1572872 | tf_op jit(solution)/shard_map/ppermute | solution.py:808
  207.6 24.6 %collective-permute-start.26 = (bf16[256,2048]{1,0:T(8,128)(2,1)}, bf16[256,2048]{1,0:T(8,128)(2,1)}, u32[]{:S(2)}, u32[]{:S(2)}) collective-permute-start(bf16[256,2048]{1,0:T(8,128)(2,1)} %get-tuple-element.68.refs_0_), channel_id=1, source_target_pairs={{0,2},{2,0},{4,6},{6,4},{1,3},{3,1},{5,7},{7,5},{8,10},{10,8},{12,... | collective-permute-start | bytes 3145736 | tf_op jit(solution)/shard_map/ppermute | solution.py:808
  209.3 25.7 %collective-permute-start.27 = (bf16[256,2048]{1,0:T(8,128)(2,1)}, bf16[256,2048]{1,0:T(8,128)(2,1)}, u32[]{:S(2)}, u32[]{:S(2)}) collective-permute-start(bf16[256,2048]{1,0:T(8,128)(2,1)} %get-tuple-element.68.refs_0_), channel_id=1, source_target_pairs={{0,4},{2,6},{4,0},{6,2},{1,5},{3,7},{5,1},{7,3},{8,12},{10,14},{12... | collective-permute-start | bytes 3145736 | tf_op jit(solution)/shard_map/ppermute | solution.py:808
  210.9 41.8 %collective-permute-start.30 = (bf16[256,2048]{1,0:T(8,128)(2,1)}, bf16[256,2048]{1,0:T(8,128)(2,1)}, u32[]{:S(2)}, u32[]{:S(2)}) collective-permute-start(bf16[256,2048]{1,0:T(8,128)(2,1)} %get-tuple-element.68.refs_0_), channel_id=1, source_target_pairs={{0,1},{1,0},{2,3},{3,2},{4,5},{5,4},{6,7},{7,6},{8,9},{9,8},{10,11... | collective-permute-start | bytes 3145736 | tf_op jit(solution)/shard_map/ppermute | solution.py:811
  235.0 17.7 %collective-permute-start.31 = (bf16[256,2048]{1,0:T(8,128)(2,1)}, bf16[256,2048]{1,0:T(8,128)(2,1)}, u32[]{:S(2)}, u32[]{:S(2)}) collective-permute-start(bf16[256,2048]{1,0:T(8,128)(2,1)} %collective-permute-done.26.refs_1_), channel_id=1, source_target_pairs={{0,1},{1,0},{2,3},{3,2},{4,5},{5,4},{6,7},{7,6},{8,9},{9,8},{10,11... | collective-permute-start | bytes 3145736 | tf_op jit(solution)/shard_map/ppermute | solution.py:811
  250.6 31.1 %collective-permute-start.36 = (bf16[256,2048]{1,0:T(8,128)(2,1)}, bf16[256,2048]{1,0:T(8,128)(2,1)}, u32[]{:S(2)}, u32[]{:S(2)}) collective-permute-start(bf16[256,2048]{1,0:T(8,128)(2,1)} %after.27.refs_0_), channel_id=1, source_target_pairs={{0,4},{2,6},{4,0},{6,2},{1,5},{3,7},{5,1},{7,3},{8,12},{10,14},{12... | collective-permute-start | bytes 3145736 | tf_op jit(solution)/shard_map/ppermute | solution.py:808
  251.0 33.1 %collective-permute-start.35 = (bf16[256,2048]{1,0:T(8,128)(2,1)}, bf16[256,2048]{1,0:T(8,128)(2,1)}, u32[]{:S(2)}, u32[]{:S(2)}) collective-permute-start(bf16[256,2048]{1,0:T(8,128)(2,1)} %after.27.refs_0_), channel_id=1, source_target_pairs={{0,2},{2,0},{4,6},{6,4},{1,3},{3,1},{5,7},{7,5},{8,10},{10,8},{12,... | collective-permute-start | bytes 3145736 | tf_op jit(solution)/shard_map/ppermute | solution.py:808
  253.2 45.9 %collective-permute-start.39 = (bf16[256,2048]{1,0:T(8,128)(2,1)}, bf16[256,2048]{1,0:T(8,128)(2,1)}, u32[]{:S(2)}, u32[]{:S(2)}) collective-permute-start(bf16[256,2048]{1,0:T(8,128)(2,1)} %after.27.refs_0_), channel_id=1, source_target_pairs={{0,1},{1,0},{2,3},{3,2},{4,5},{5,4},{6,7},{7,6},{8,9},{9,8},{10,11... | collective-permute-start | bytes 3145736 | tf_op jit(solution)/shard_map/ppermute | solution.py:811
  283.6 16.8 %collective-permute-start.41 = (bf16[256,2048]{1,0:T(8,128)(2,1)}, bf16[256,2048]{1,0:T(8,128)(2,1)}, u32[]{:S(2)}, u32[]{:S(2)}) collective-permute-start(bf16[256,2048]{1,0:T(8,128)(2,1)} %after.29.refs_2_), channel_id=1, source_target_pairs={{0,1},{1,0},{2,3},{3,2},{4,5},{5,4},{6,7},{7,6},{8,9},{9,8},{10,11... | collective-permute-start | bytes 3145736 | tf_op jit(solution)/shard_map/ppermute | solution.py:811
  319.3 226.5 %reduce-scatter.6.cloned.1.call-start = ((), (), s32[]{:S(2)}) async-start(), calls=%async_computation.7 | async-start | bytes 10485760 | tf_op jit(solution)/shard_map/reduce_scatter | solution.py:928
  353.5 27.4 %collective-permute-start.44 = (bf16[1024,2048]{1,0:T(8,128)(2,1)}, bf16[1024,2048]{1,0:T(8,128)(2,1)}, u32[]{:S(2)}, u32[]{:S(2)}) collective-permute-start(bf16[1024,2048]{1,0:T(8,128)(2,1)} %rows_product.4.refs_11_), channel_id=1, source_target_pairs={{0,1},{1,0},{2,3},{3,2},{4,5},{5,4},{6,7},{7,6},{8,9},{9,8},{10,11... | collective-permute-start | bytes 12582920 | tf_op jit(solution)/shard_map/ppermute | solution.py:811
  380.8 258.4 %reduce-scatter.8.cloned.1.call-start = ((), (), s32[]{:S(2)}) async-start(), calls=%async_computation.8 | async-start | bytes 3276800 | tf_op jit(solution)/shard_map/reduce_scatter | solution.py:928
  404.0 24.0 %collective-permute-start.45 = (bf16[1024,2048]{1,0:T(8,128)(2,1)}, bf16[1024,2048]{1,0:T(8,128)(2,1)}, u32[]{:S(2)}, u32[]{:S(2)}) collective-permute-start(bf16[1024,2048]{1,0:T(8,128)(2,1)} %rows_product.6.rest_0_), channel_id=1, source_target_pairs={{0,1},{1,0},{2,3},{3,2},{4,5},{5,4},{6,7},{7,6},{8,9},{9,8},{10,11... | collective-permute-start | bytes 12582920 | tf_op jit(solution)/shard_map/ppermute | solution.py:811
  408.9 28.8 %collective-permute-start.49 = (bf16[128,2048]{1,0:T(8,128)(2,1)}, bf16[128,2048]{1,0:T(8,128)(2,1)}, u32[]{:S(2)}, u32[]{:S(2)}) collective-permute-start(bf16[128,2048]{1,0:T(8,128)(2,1)} %get-tuple-element.58), channel_id=1, source_target_pairs={{0,4},{2,6},{4,0},{6,2},{1,5},{3,7},{5,1},{7,3},{8,12},{10,14},{12... | collective-permute-start | bytes 1572872 | tf_op jit(solution)/shard_map/ppermute | solution.py:808
  409.5 28.1 %collective-permute-start.50 = (bf16[128,2048]{1,0:T(8,128)(2,1)}, bf16[128,2048]{1,0:T(8,128)(2,1)}, u32[]{:S(2)}, u32[]{:S(2)}) collective-permute-start(bf16[128,2048]{1,0:T(8,128)(2,1)} %get-tuple-element.59), channel_id=1, source_target_pairs={{0,2},{2,0},{4,6},{6,4},{1,3},{3,1},{5,7},{7,5},{8,10},{10,8},{12,... | collective-permute-start | bytes 1572872 | tf_op jit(solution)/shard_map/ppermute | solution.py:808
  425.8 17.5 %collective-permute-start.48 = (bf16[128,2048]{1,0:T(8,128)(2,1)}, bf16[128,2048]{1,0:T(8,128)(2,1)S(1)}, u32[]{:S(2)}, u32[]{:S(2)}) collective-permute-start(bf16[128,2048]{1,0:T(8,128)(2,1)} %get-tuple-element.36), channel_id=1, source_target_pairs={{0,2},{2,0},{4,6},{6,4},{1,3},{3,1},{5,7},{7,5},{8,10},{10,8},{12,... | collective-permute-start | bytes 1572872 | tf_op jit(solution)/shard_map/ppermute | solution.py:808
  449.4 24.2 %collective-permute-start.52 = (bf16[256,2048]{1,0:T(8,128)(2,1)}, bf16[256,2048]{1,0:T(8,128)(2,1)S(1)}, u32[]{:S(2)}, u32[]{:S(2)}) collective-permute-start(bf16[256,2048]{1,0:T(8,128)(2,1)} %after.32.refs_0_.refs_11_), channel_id=1, source_target_pairs={{0,2},{2,0},{4,6},{6,4},{1,3},{3,1},{5,7},{7,5},{8,10},{10,8},{12,... | collective-permute-start | bytes 3145736 | tf_op jit(solution)/shard_map/ppermute | solution.py:808
  451.0 24.4 %collective-permute-start.53 = (bf16[256,2048]{1,0:T(8,128)(2,1)}, bf16[256,2048]{1,0:T(8,128)(2,1)}, u32[]{:S(2)}, u32[]{:S(2)}) collective-permute-start(bf16[256,2048]{1,0:T(8,128)(2,1)} %after.32.refs_0_.refs_11_), channel_id=1, source_target_pairs={{0,4},{2,6},{4,0},{6,2},{1,5},{3,7},{5,1},{7,3},{8,12},{10,14},{12... | collective-permute-start | bytes 3145736 | tf_op jit(solution)/shard_map/ppermute | solution.py:808
  477.1 17.9 %collective-permute-start.60 = (bf16[256,2048]{1,0:T(8,128)(2,1)S(1)}, bf16[256,2048]{1,0:T(8,128)(2,1)}, u32[]{:S(2)}, u32[]{:S(2)}) collective-permute-start(bf16[256,2048]{1,0:T(8,128)(2,1)S(1)} %collective-permute-done.52.refs_1_.refs_12_), channel_id=1, source_target_pairs={{0,1},{1,0},{2,3},{3,2},{4,5},{5,4},{6,7},{7,6},{8,9},{9,8},{10,11... | collective-permute-start | bytes 3145736 | tf_op jit(solution)/shard_map/ppermute | solution.py:811
  477.6 17.4 %collective-permute-start.61 = (bf16[256,2048]{1,0:T(8,128)(2,1)}, bf16[256,2048]{1,0:T(8,128)(2,1)}, u32[]{:S(2)}, u32[]{:S(2)}) collective-permute-start(bf16[256,2048]{1,0:T(8,128)(2,1)} %collective-permute-done.53.refs_2_.refs_13_), channel_id=1, source_target_pairs={{0,1},{1,0},{2,3},{3,2},{4,5},{5,4},{6,7},{7,6},{8,9},{9,8},{10,11... | collective-permute-start | bytes 3145736 | tf_op jit(solution)/shard_map/ppermute | solution.py:811
  491.5 47.7 %collective-permute-start.56 = (bf16[256,2048]{1,0:T(8,128)(2,1)}, bf16[256,2048]{1,0:T(8,128)(2,1)}, u32[]{:S(2)}, u32[]{:S(2)}) collective-permute-start(bf16[256,2048]{1,0:T(8,128)(2,1)} %get-tuple-element.53), channel_id=1, source_target_pairs={{0,2},{2,0},{4,6},{6,4},{1,3},{3,1},{5,7},{7,5},{8,10},{10,8},{12,... | collective-permute-start | bytes 3145736 | tf_op jit(solution)/shard_map/ppermute | solution.py:808
  492.6 48.8 %collective-permute-start.57 = (bf16[256,2048]{1,0:T(8,128)(2,1)}, bf16[256,2048]{1,0:T(8,128)(2,1)}, u32[]{:S(2)}, u32[]{:S(2)}) collective-permute-start(bf16[256,2048]{1,0:T(8,128)(2,1)} %get-tuple-element.55), channel_id=1, source_target_pairs={{0,4},{2,6},{4,0},{6,2},{1,5},{3,7},{5,1},{7,3},{8,12},{10,14},{12... | collective-permute-start | bytes 3145736 | tf_op jit(solution)/shard_map/ppermute | solution.py:808
  493.9 47.4 %collective-permute-start.58 = (bf16[256,2048]{1,0:T(8,128)(2,1)}, bf16[256,2048]{1,0:T(8,128)(2,1)}, u32[]{:S(2)}, u32[]{:S(2)}) collective-permute-start(bf16[256,2048]{1,0:T(8,128)(2,1)} %get-tuple-element.54), channel_id=1, source_target_pairs={{0,6},{2,4},{4,2},{6,0},{1,7},{3,5},{5,3},{7,1},{8,14},{10,12},{12... | collective-permute-start | bytes 3145736 | tf_op jit(solution)/shard_map/ppermute | solution.py:808
  506.7 43.5 %collective-permute-start.64 = (bf16[128,1024]{1,0:T(8,128)(2,1)}, bf16[128,1024]{1,0:T(8,128)(2,1)S(1)}, u32[]{:S(2)}, u32[]{:S(2)}) collective-permute-start(bf16[128,1024]{1,0:T(8,128)(2,1)} %get-tuple-element.81), channel_id=1, source_target_pairs={{0,2},{2,0},{4,6},{6,4},{1,3},{3,1},{5,7},{7,5},{8,10},{10,8},{12,... | collective-permute-start | bytes 786440 | tf_op jit(solution)/shard_map/ppermute | solution.py:808
  507.8 62.3 %collective-permute-start.65 = (bf16[128,1024]{1,0:T(8,128)(2,1)}, bf16[128,1024]{1,0:T(8,128)(2,1)}, u32[]{:S(2)}, u32[]{:S(2)}) collective-permute-start(bf16[128,1024]{1,0:T(8,128)(2,1)} %get-tuple-element.80), channel_id=1, source_target_pairs={{0,4},{2,6},{4,0},{6,2},{1,5},{3,7},{5,1},{7,3},{8,12},{10,14},{12... | collective-permute-start | bytes 786440 | tf_op jit(solution)/shard_map/ppermute | solution.py:808
  539.2 30.9 %collective-permute-start.66 = (bf16[128,1024]{1,0:T(8,128)(2,1)}, bf16[128,1024]{1,0:T(8,128)(2,1)S(1)}, u32[]{:S(2)}, u32[]{:S(2)}) collective-permute-start(bf16[128,1024]{1,0:T(8,128)(2,1)} %get-tuple-element.79), channel_id=1, source_target_pairs={{0,6},{2,4},{4,2},{6,0},{1,7},{3,5},{5,3},{7,1},{8,14},{10,12},{12... | collective-permute-start | bytes 786440 | tf_op jit(solution)/shard_map/ppermute | solution.py:808
  548.5 21.7 %collective-permute-start.67 = (bf16[128,2048]{1,0:T(8,128)(2,1)}, bf16[128,2048]{1,0:T(8,128)(2,1)S(1)}, u32[]{:S(2)}, u32[]{:S(2)}) collective-permute-start(bf16[128,2048]{1,0:T(8,128)(2,1)} %get-tuple-element.77), channel_id=1, source_target_pairs={{0,2},{2,0},{4,6},{6,4},{1,3},{3,1},{5,7},{7,5},{8,10},{10,8},{12,... | collective-permute-start | bytes 1572872 | tf_op jit(solution)/shard_map/ppermute | solution.py:808
  549.3 25.0 %collective-permute-start.68 = (bf16[128,2048]{1,0:T(8,128)(2,1)S(1)}, bf16[128,2048]{1,0:T(8,128)(2,1)S(1)}, u32[]{:S(2)}, u32[]{:S(2)}) collective-permute-start(bf16[128,2048]{1,0:T(8,128)(2,1)S(1)} %get-tuple-element.76), channel_id=1, source_target_pairs={{0,4},{2,6},{4,0},{6,2},{1,5},{3,7},{5,1},{7,3},{8,12},{10,14},{12... | collective-permute-start | bytes 1572872 | tf_op jit(solution)/shard_map/ppermute | solution.py:808
  550.2 24.1 %collective-permute-start.69 = (bf16[128,2048]{1,0:T(8,128)(2,1)S(1)}, bf16[128,2048]{1,0:T(8,128)(2,1)S(1)}, u32[]{:S(2)}, u32[]{:S(2)}) collective-permute-start(bf16[128,2048]{1,0:T(8,128)(2,1)S(1)} %get-tuple-element.75), channel_id=1, source_target_pairs={{0,6},{2,4},{4,2},{6,0},{1,7},{3,5},{5,3},{7,1},{8,14},{10,12},{12... | collective-permute-start | bytes 1572872 | tf_op jit(solution)/shard_map/ppermute | solution.py:808
  599.8 24.4 %collective-permute-start.75 = (bf16[128,2048]{1,0:T(8,128)(2,1)}, bf16[128,2048]{1,0:T(8,128)(2,1)S(1)}, u32[]{:S(2)}, u32[]{:S(2)}) collective-permute-start(bf16[128,2048]{1,0:T(8,128)(2,1)} %get-tuple-element.49), channel_id=1, source_target_pairs={{0,4},{2,6},{4,0},{6,2},{1,5},{3,7},{5,1},{7,3},{8,12},{10,14},{12... | collective-permute-start | bytes 1572872 | tf_op jit(solution)/shard_map/ppermute | solution.py:808
  601.0 24.4 %collective-permute-start.76 = (bf16[128,2048]{1,0:T(8,128)(2,1)}, bf16[128,2048]{1,0:T(8,128)(2,1)S(1)}, u32[]{:S(2)}, u32[]{:S(2)}) collective-permute-start(bf16[128,2048]{1,0:T(8,128)(2,1)} %get-tuple-element.50), channel_id=1, source_target_pairs={{0,2},{2,0},{4,6},{6,4},{1,3},{3,1},{5,7},{7,5},{8,10},{10,8},{12,... | collective-permute-start | bytes 1572872 | tf_op jit(solution)/shard_map/ppermute | solution.py:808
  602.1 66.1 %collective-permute-start.71 = (bf16[256,2048]{1,0:T(8,128)(2,1)}, bf16[256,2048]{1,0:T(8,128)(2,1)}, u32[]{:S(2)}, u32[]{:S(2)}) collective-permute-start(bf16[256,2048]{1,0:T(8,128)(2,1)} %after.36), channel_id=1, source_target_pairs={{0,1},{1,0},{2,3},{3,2},{4,5},{5,4},{6,7},{7,6},{8,9},{9,8},{10,11... | collective-permute-start | bytes 3145736 | tf_op jit(solution)/shard_map/ppermute | solution.py:811
  618.5 17.0 %collective-permute-start.74 = (bf16[128,2048]{1,0:T(8,128)(2,1)}, bf16[128,2048]{1,0:T(8,128)(2,1)S(1)}, u32[]{:S(2)}, u32[]{:S(2)}) collective-permute-start(bf16[128,2048]{1,0:T(8,128)(2,1)} %get-tuple-element.41), channel_id=1, source_target_pairs={{0,2},{2,0},{4,6},{6,4},{1,3},{3,1},{5,7},{7,5},{8,10},{10,8},{12,... | collective-permute-start | bytes 1572872 | tf_op jit(solution)/shard_map/ppermute | solution.py:808
  642.6 16.9 %collective-permute-start.80 = (bf16[128,640]{1,0:T(8,128)(2,1)}, bf16[128,640]{1,0:T(8,128)(2,1)S(1)}, u32[]{:S(2)}, u32[]{:S(2)}) collective-permute-start(bf16[128,640]{1,0:T(8,128)(2,1)} %get-tuple-element.120), channel_id=1, source_target_pairs={{0,4},{2,6},{4,0},{6,2},{1,5},{3,7},{5,1},{7,3},{8,12},{10,14},{12... | collective-permute-start | bytes 491528 | tf_op jit(solution)/shard_map/ppermute | solution.py:808
  (126 other events, 1308.7 us)
Sparse Core Ops, SparseCore 0:
  26.3 55.1 all-gather.3
  83.6 148.3 all-gather.5
  233.6 78.9 all-gather.7
  319.4 76.2 reduce-scatter.3
  398.0 144.9 reduce-scatter.5
  582.7 52.0 reduce-scatter.7

commit v4 on v3

--- a/solution.py
+++ b/solution.py
@@ -362,7 +362,7 @@
             for part in range(2):
                 mine = low_half if part == 0 else jnp.logical_not(low_half)
                 one = jnp.where(mine, rot, jnp.zeros_like(rot))
-                scores = jnp.where(allowed, dot_nt(one, keys_w) * SCALE, NEG)
+                scores = jnp.where(allowed, dot_nt(one * SCALE, keys_w), NEG)
                 highest = jnp.max(scores, axis=1, keepdims=True)
                 raised = jnp.exp(scores - highest)
                 total = jnp.sum(raised, axis=1, keepdims=True)
@@ -415,9 +415,9 @@
             for part in range(2):
                 mine = low_half if part == 0 else jnp.logical_not(low_half)
                 head = slab * 2 + part
-                one = jnp.where(mine, query, jnp.zeros_like(query))
+                one = jnp.where(mine, query, jnp.zeros_like(query)) * SCALE
                 one_grad = jnp.where(mine, grad, jnp.zeros_like(grad))
-                scores = dot_nt(one, keys_w) * SCALE - lse_ref[:, head : head + 1]
+                scores = dot_nt(one, keys_w) - lse_ref[:, head : head + 1]
                 probs = jnp.exp(jnp.where(allowed, scores, NEG))
                 d_probs = dot_nt(one_grad, values_w)
                 inner = jnp.sum(probs * d_probs, axis=1, keepdims=True)
@@ -432,7 +432,7 @@
 
     each_window(step, rows, window, windowed)
     own = pl.ds(pl.multiple_of(step * rows, rows), rows)
-    d_key = d_keys[own, :] * SCALE
+    d_key = d_keys[own, :]
     d_key = turn(d_key + pltpu.roll(d_key, HD, 1), cosine, -sine)
     d_value = d_values[own, :]
     d_value = d_value + pltpu.roll(d_value, HD, 1)
@@ -774,6 +774,45 @@
     )(mine, from_near, from_ctx, *tokens)
 
 
+def finish_kernel(group, me_ref, *refs):
+    pieces, rest = refs[:group], refs[group:]
+    query_w, key_w, value_w, gain_ref, grad_q, grad_k, grad_v, grad_o, sums = rest
+    me, gain = me_ref[0], gain_ref[...]
+    lows = [piece[...].astype(jnp.float32) for piece in pieces]
+    total = jnp.zeros(sums.shape, jnp.float32)
+    for owner in range(group):
+        mine = lows[0]
+        for m in range(1, group):
+            mine = jnp.where(me == (owner ^ m), lows[m], mine)
+        first = 0
+        for weight, out in ((query_w, grad_q), (key_w, grad_k), (value_w, grad_v)):
+            size = weight.shape[1] // group
+            grad = mine[:, first : first + size]
+            at = slice(owner * size, (owner + 1) * size)
+            out[:, at] = grad * gain
+            total = total + jnp.sum(
+                weight[:, at].astype(jnp.float32) * grad, axis=1, keepdims=True
+            )
+            first += size
+        size = grad_o.shape[1] // group
+        grad_o[:, owner * size : (owner + 1) * size] = mine[:, first:] * RESIDUAL
+    sums[...] = total
+
+
+def finish(me, pieces, query_w, key_w, value_w, gain, out_cols):
+    deep = query_w.shape[0]
+    vmem = pl.BlockSpec(memory_space=pltpu.VMEM)
+    shapes = [w.shape[1] for w in (query_w, key_w, value_w)] + [out_cols, 1]
+    return pl.pallas_call(
+        functools.partial(finish_kernel, len(pieces)),
+        out_shape=[jax.ShapeDtypeStruct((deep, cols), jnp.float32) for cols in shapes],
+        in_specs=[pl.BlockSpec(memory_space=pltpu.SMEM)] + [vmem] * (len(pieces) + 4),
+        out_specs=[vmem] * len(shapes),
+        compiler_params=pltpu.CompilerParams(vmem_limit_bytes=VMEM_LIMIT),
+        name="finish",
+    )(me, *pieces, query_w, key_w, value_w, gain)
+
+
 def after_kernel(*refs):
     del refs
 
@@ -842,7 +881,7 @@
                 + near_last.astype(jnp.float32),
             ]
         )
-        return total, to_ctx
+        return total, (ctx_first, near_last)
 
     def scatter_direct(mine):
         total = mine[:rows].astype(jnp.float32)
@@ -881,7 +920,7 @@
         starts[axis] = index * jnp.uint32(piece.shape[axis])
         return lax.dynamic_update_slice(whole, piece, starts)
 
-    def to_columns(*weights, parts=1):
+    def to_columns(*weights, parts=1, later=()):
         whole = None
         for m in range(group):
             there = me ^ jnp.uint32(m)
@@ -891,7 +930,8 @@
                 [w[:, n * size : (n + 1) * size] for n in range(parts) for w, size in zip(own, sizes)],
                 axis=1,
             )
-            piece = swap(piece, m) if m else piece
+            if m:
+                piece = swap(after(piece, *later) if later else piece, m)
             if whole is None:
                 whole = jnp.zeros((group * piece.shape[0], piece.shape[1]), piece.dtype)
             whole = put(whole, piece, there, 0)
@@ -949,14 +989,8 @@
     pair_cols = to_columns(
         scaled(gate_weight, gain_later), scaled(up_weight, gain_later), parts=units // block
     )
-    seg_others = [swap(segments, n * (group // near)) for n in range(1, near)]
-    own_in = after(own_half(hidden_in.reshape(rows_here, width)), pair_cols, *seg_others)
-    inputs = gather(own_in)
-    pair_w = far_gather(pair_cols)
-    own_cot = own_half(cotangent.reshape(rows_here, width))
-
     seg_all = jnp.concatenate(
-        [segments] + seg_others,
+        [segments] + [swap(segments, n * (group // near)) for n in range(1, near)],
         axis=0,
     )
     start = jnp.sum((seg_all[:, None, :] < seg_all[:, :, None]).astype(jnp.int32), axis=2)
@@ -976,26 +1010,31 @@
         + ((in_seq // cores) ^ here_ctx)
     ).astype(jnp.int32)
 
+    own_in = after(own_half(hidden_in.reshape(rows_here, width)), pair_cols)
+    inputs = gather(own_in, (cosine, sine))
+    pair_w = far_gather(pair_cols)
+    own_cot = own_half(cotangent.reshape(rows_here, width))
+
     qkv, inv_a = project(inputs, in_w, True, None, jnp.float32)
-    down_cols = to_columns(after(down_weight, inv_a))
+    down_cols = to_columns(down_weight, later=(inv_a,))
     down_w = far_gather(down_cols)
     query, kv, mixed, lse = attend(
         place, qkv, cosine, sine, start, near, blocks, rows, heads, ()
     )
-    product = narrow(after(mixed, down_cols), out_w)
+    product = narrow(mixed, out_w)
     branch_a, _ = scatter(own_side(product, swap_core(other_side(product))))
     own_f = own_in.astype(jnp.float32)
     middle = own_f + RESIDUAL * branch_a
 
-    mids = gather(middle.astype(bfloat))
+    mids = gather(after(middle.astype(bfloat), down_cols))
     gate_pre, upward, hidden, inv_f = gated(mids, pair_w, block, 512)
     cots = gather(after(own_cot, *mids[1 : len(mids) // 2]), (inv_f,))
-    down_part = outer([(cots, [hidden])], 256)
+    down_part = outer([(cots, [hidden])], 512)
     down_far = far_scatter(down_part)
     d_both = gated_back(cots, down_w, gate_pre, upward, inv_f, block, 512, (down_part,))
     product = plain(d_both, pair_w)
     other = other_side(product)
-    pair_part = outer([(mids, [d_both])], 256, (other,))
+    pair_part = outer([(mids, [d_both])], 512, (other,))
     pair_far = far_scatter(pair_part)
     back_mine = own_side(product, after(swap_core(other), pair_part))
     product = plain(after(hidden, back_mine), down_w)
@@ -1019,7 +1058,7 @@
     attn_cols_all = d_qkv.shape[1] + head_cols
     attn_part = outer(
         [(inputs, [d_qkv]), (d_mids, [mixed])],
-        256,
+        512,
         (pair_far,),
         pl.CostEstimate(
             flops=4 * d_qkv.shape[0] * width * attn_cols_all,
@@ -1031,10 +1070,9 @@
     pair_rows = to_rows(pair_far)
     product = narrow(after(d_qkv, attn_part, middle_out, *down_rows, *pair_rows), in_w)
     back_mine = own_side(product, swap_core(other_side(product)))
-    back_a, _ = scatter(back_mine)
+    back_a, passed = scatter(back_mine)
     layer_out = both_halves(after(middle_out, back_mine))
     input_grad = d_middle + through_norm(back_a, own_f * inverse_rms(own_f))
-    input_grad = both_halves(input_grad)
 
     one = jnp.ones_like(col_gain_a)
     (grad_down,) = unpack(
@@ -1043,33 +1081,34 @@
     grad_gate, grad_up = unpack(
         [after(piece, back_mine) for piece in pair_rows], [units, units], [one, one], parts=units // block
     )
-    grad_query, grad_key, grad_value, grad_out = unpack(
-        to_rows(after(attn_far, back_a)),
-        [head_cols, HD, HD, head_cols],
-        [one, one, one, RESIDUAL],
+    attn_rows = to_rows(after(attn_far, *passed))
+    grad_query, grad_key, grad_value, grad_out, gain_a = finish(
+        me.astype(jnp.int32)[None],
+        attn_rows,
+        query_weight,
+        key_weight,
+        value_weight,
+        col_gain_a,
+        out_weight.shape[1],
     )
 
     def row_sum(*pairs):
         return sum(jnp.sum(weight.astype(jnp.float32) * grad, axis=1) for weight, grad in pairs)
 
-    gain_grads = jnp.stack(
-        [
-            row_sum(
-                (query_weight, grad_query), (key_weight, grad_key), (value_weight, grad_value)
-            ),
-            row_sum((gate_weight, grad_gate), (up_weight, grad_up)),
-        ]
-    )
-    gain_grads = gain_grads + swap_core(gain_grads)
+    input_grad = both_halves(after(input_grad, gain_a))
+    gain_f = row_sum((gate_weight, grad_gate), (up_weight, grad_up))
+    gain_f = gain_f + swap_core(gain_f)
+    gain_a = gain_a[:, 0]
+    gain_a = gain_a + swap_core(gain_a)
     return (
         layer_out.reshape(hidden_in.shape),
         input_grad.reshape(hidden_in.shape),
-        gain_grads[0],
-        grad_query * col_gain_a,
-        grad_key * col_gain_a,
-        grad_value * col_gain_a,
+        gain_a,
+        grad_query,
+        grad_key,
+        grad_value,
         grad_out,
-        gain_grads[1],
+        gain_f,
         grad_gate * col_gain_f,
         grad_up * col_gain_f,
         grad_down,

time: 687 us -> 673 us (0.980)
  local copies, waits for them, and re-layouts: 87.1 us -> 76.9 us
  other arithmetic: 46.4 us -> 38.8 us
    ppermute x56, waiting for transfers between devices: 190 us -> 206 us  [swap(): lax.ppermute(value, ('near', 'ctx'), [(i, i ^ m) for i in range(group)])]
    ppermute x27 -> x28, waiting for transfers between devices: 19.3 us -> 10.5 us  [swap_core(): return lax.ppermute(value, 'tp', [(0, 1), (1, 0)])]
    dynamic_update_slice x19 -> x13, other arithmetic: 11.1 us -> 3.35 us  [put(): return lax.dynamic_update_slice(whole, piece, starts)]
    dynamic_update_slice x21 -> x14, local copies, waits for them, and re-layouts: 19.5 us -> 11.8 us  [put(): return lax.dynamic_update_slice(whole, piece, starts)]
    unnamed x183 -> x159, local copies, waits for them, and re-layouts: 30.9 us -> 24.6 us
  transfers between devices with their start and end apart: 89 -> 90, of which waited for: 39 -> 40; matrix products, arithmetic and copies ran while one was open for 17% -> 15% of each run, Pallas kernels for 34% -> 35%
where the time goes in v4:
time: 673 us; the launch traced here: 667 us
  Pallas kernels  232 us (34%)
  waiting for transfers between devices  216 us (32%)
  local copies, waits for them, and re-layouts  76.9 us (11%)
  starting transfers between devices  65.8 us (10%)
  other arithmetic  38.8 us (6%)
  matrix products  21.6 us (3%)
  between operations  15.7 us (2%)
    ppermute x56, waiting for transfers between devices, swap(): lax.ppermute(value, ('near', 'ctx'), [(i, i ^ m) for i in range(group)])  206 us
    ppermute x56, starting transfers between devices, swap(): lax.ppermute(value, ('near', 'ctx'), [(i, i ^ m) for i in range(group)])  62.3 us
    pallas_call x3, Pallas kernels, outer(): pl.pallas_call(functools.partial(outer_kernel, counts, len(tokens), block...  59.5 us
    pallas_call x4, Pallas kernels, rows_product(): pl.pallas_call(functools.partial(rows_kernel, len(extra)), out_shape=jax....  46.5 us
    pallas_call x1, Pallas kernels, attend_back(): pl.pallas_call(functools.partial(attend_back_kernel, rows, window, heads,...  28.7 us
    pallas_call x1, Pallas kernels, gated(): pl.pallas_call(functools.partial(gated_kernel, len(pieces), chunk), out_s...  25.7 us
    unnamed x159, local copies, waits for them, and re-layouts  24.6 us
    dot_general x4, matrix products, matmul_trans(): lax.dot_general(left, right, (((1,), (1,)), ((), ())), preferred_element_...  21.6 us
  transfers between devices with their start and end apart: 90, of which 40 were waited for; matrix products, arithmetic and copies ran while one was open for 15% of the time, Pallas kernels for 35%

profile of v4, /device:TPU:0, one launch (start us, length us, event | category | flops | bytes accessed | tf_op | source)
XLA Modules:
  0.0 667.2 jit_solution(1409431752722023398)
XLA Ops:
  11.3 3.0 collective-permute-start
  19.0 4.7 collective-permute-done.1
  37.5 9.0 %collective-permute-done.3 = bf16[128,2048]{1,0:T(8,128)(2,1)S(1)} collective-permute-done((bf16[128,2048]{1,0:T(8,128)(2,1)S(1)}, bf16[128,2048]{1,0:T(8,128)(2,1)S(1)}, u32[]{:S(2)}, u32[]{:S(2)}) %collective-permute-start.3) | collective-permute-done | bytes 524320 | tf_op jit(solution)/shard_map/ppermute | solution.py:847
  47.3 7.2 %collective-permute-done.4 = bf16[128,2048]{1,0:T(8,128)(2,1)S(1)} collective-permute-done((bf16[128,2048]{1,0:T(8,128)(2,1)S(1)}, bf16[128,2048]{1,0:T(8,128)(2,1)S(1)}, u32[]{:S(2)}, u32[]{:S(2)}) %collective-permute-start.4) | collective-permute-done | bytes 524320 | tf_op jit(solution)/shard_map/ppermute | solution.py:847
  65.6 3.7 fusion.14
  69.3 3.0 pad_maximum_fusion.2
  72.3 11.1 %collective-permute-done.8.refs_0_ = bf16[256,2048]{1,0:T(8,128)(2,1)S(1)} collective-permute-done((bf16[256,2048]{1,0:T(8,128)(2,1)}, bf16[256,2048]{1,0:T(8,128)(2,1)S(1)}, u32[]{:S(2)}, u32[]{:S(2)}) %collective-permute-start.8) | collective-permute-done | bytes 1048608 | tf_op jit(solution)/shard_map/ppermute | solution.py:847
  89.0 11.0 %collective-permute-done.10.refs_4_ = bf16[128,2048]{1,0:T(8,128)(2,1)} collective-permute-done((bf16[128,2048]{1,0:T(8,128)(2,1)S(1)}, bf16[128,2048]{1,0:T(8,128)(2,1)}, u32[]{:S(2)}, u32[]{:S(2)}) %collective-permute-start.10) | collective-permute-done | bytes 524320 | tf_op jit(solution)/shard_map/ppermute | solution.py:847
  106.2 11.3 %project.2 = (f32[2048,384]{1,0:T(8,128)}, f32[2048,1]{1,0:T(8,128)}) custom-call(bf16[256,2048]{1,0:T(8,128)(2,1)} %after.29.refs_0_, bf16[256,2048]{1,0:T(8,128)(2,1)} %after.30.refs_1_, bf16[256,2048]{1,0:T(8,128)(2,1)} %after.31.refs_2_, bf16[128,2048]{1,0:T(8,128)(2,1)} %collective-permute-done.9.refs_3_, ...), custom_call_target="tpu_custom_call" | custom-call | flops 6442450944 | bytes 8388608 | tf_op jit(solution)/shard_map/project/pallas_call | solution.py:564
  117.5 17.2 %attend.1 = (bf16[2048,256]{1,0:T(8,128)(2,1)S(1)}, bf16[2048,128]{1,0:T(8,128)(2,1)S(1)}, bf16[2048,256]{1,0:T(8,128)(2,1)S(1)}, f32[2048,4]{1,0:T(8,128)S(1)}) custom-call(s32[8]{0:T(128)S(1)} %fusion.18.place_ref, f32[2048,384]{1,0:T(8,128)} %get-tuple-element.32.qkv_ref, f32[2048,128]{1,0:T(8,128)S(1)} %copy-done.2, f32[2048,128]{1,0:T(8,128)S(1)} %copy-done.3, ...), custom_call_target="tpu_custom_call" | custom-call | tf_op jit(solution)/shard_map/attend/pallas_call | solution.py:453
  134.8 5.5 convolution_convert_fusion.1
  145.3 5.9 collective-permute-done.23
  151.2 6.2 collective-permute-done.24
  159.6 3.8 add_convert_fusion.1.mine
  169.5 10.8 %collective-permute-done.17.from_near = bf16[128,2048]{1,0:T(8,128)(2,1)S(1)} collective-permute-done((bf16[128,2048]{1,0:T(8,128)(2,1)S(1)}, bf16[128,2048]{1,0:T(8,128)(2,1)S(1)}, u32[]{:S(2)}, u32[]{:S(2)}) %collective-permute-start.17) | collective-permute-done | bytes 524320 | tf_op jit(solution)/shard_map/ppermute | solution.py:847
  181.9 3.6 fold.3
  187.1 4.3 collective-permute-done.20
  191.9 7.8 %collective-permute-done.19 = bf16[128,2048]{1,0:T(8,128)(2,1)S(1)} collective-permute-done((bf16[128,2048]{1,0:T(8,128)(2,1)}, bf16[128,2048]{1,0:T(8,128)(2,1)S(1)}, u32[]{:S(2)}, u32[]{:S(2)}) %collective-permute-start.19) | collective-permute-done | bytes 524320 | tf_op jit(solution)/shard_map/ppermute | solution.py:847
  205.7 21.4 %collective-permute-done.26.refs_1_ = bf16[256,2048]{1,0:T(8,128)(2,1)} collective-permute-done((bf16[256,2048]{1,0:T(8,128)(2,1)}, bf16[256,2048]{1,0:T(8,128)(2,1)}, u32[]{:S(2)}, u32[]{:S(2)}) %collective-permute-start.26) | collective-permute-done | bytes 1048608 | tf_op jit(solution)/shard_map/ppermute | solution.py:847
  233.9 5.9 collective-permute-done.28.refs_3_
  239.8 4.2 collective-permute-done.29.refs_4_
  250.6 25.7 %gated.1 = (bf16[2048,1024]{1,0:T(8,128)(2,1)}, bf16[2048,1024]{1,0:T(8,128)(2,1)}, bf16[2048,1024]{1,0:T(8,128)(2,1)}, f32[2048,1]{1,0:T(8,128)}) custom-call(bf16[256,2048]{1,0:T(8,128)(2,1)} %after.35.refs_0_, bf16[256,2048]{1,0:T(8,128)(2,1)} %collective-permute-done.26.refs_1_, bf16[256,2048]{1,0:T(8,128)(2,1)} %collective-permute-done.27.refs_2_, ...), custom_call_target="tpu_custom_call" | custom-call | tf_op jit(solution)/shard_map/gated/pallas_call | solution.py:609
  280.0 12.9 %collective-permute-done.38.refs_4_ = bf16[128,2048]{1,0:T(8,128)(2,1)} collective-permute-done((bf16[128,2048]{1,0:T(8,128)(2,1)}, bf16[128,2048]{1,0:T(8,128)(2,1)}, u32[]{:S(2)}, u32[]{:S(2)}) %collective-permute-start.38) | collective-permute-done | bytes 524320 | tf_op jit(solution)/shard_map/ppermute | solution.py:847
  296.8 16.2 %outer.3.refs_10_ = bf16[2048,1024]{1,0:T(8,128)(2,1)} custom-call(bf16[256,2048]{1,0:T(8,128)(2,1)} %after.36.refs_0_, bf16[256,2048]{1,0:T(8,128)(2,1)} %after.37.refs_1_, bf16[256,2048]{1,0:T(8,128)(2,1)} %after.38.refs_2_, bf16[128,2048]{1,0:T(8,128)(2,1)} %copy-done.56, bf16[128,2048]{1,0:T(8,128)(2,1)} %collective-permute-done.38.refs_4_, ...), custom_call_target="tpu_custom_call" | custom-call | tf_op jit(solution)/shard_map/outer/pallas_call | solution.py:713
  313.2 20.0 %gated_back.1.left_ref.refs_10_ = bf16[2048,2048]{1,0:T(8,128)(2,1)} custom-call(bf16[256,2048]{1,0:T(8,128)(2,1)} %after.36.refs_0_, bf16[256,2048]{1,0:T(8,128)(2,1)} %after.37.refs_1_, bf16[256,2048]{1,0:T(8,128)(2,1)} %after.38.refs_2_, bf16[128,2048]{1,0:T(8,128)(2,1)} %copy-done.56, bf16[128,2048]{1,0:T(8,128)(2,1)} %collective-permute-done.38.refs_4_, ...), custom_call_target="tpu_custom_call" | custom-call | tf_op jit(solution)/shard_map/gated_back/pallas_call | solution.py:652
  333.2 13.4 %rows_product.4.refs_11_ = bf16[1024,2048]{1,0:T(8,128)(2,1)} custom-call(bf16[2048,2048]{1,0:T(8,128)(2,1)} %gated_back.1.left_ref.refs_10_, bf16[2048,2048]{1,0:T(8,128)(2,1)} %all-gather.6.cloned.1.call-done.refs_10_.weight_ref), custom_call_target="tpu_custom_call" | custom-call | tf_op jit(solution)/shard_map/rows_product/pallas_call | solution.py:737
  346.7 26.5 %outer.4.refs_1_ = bf16[2048,2048]{1,0:T(8,128)(2,1)} custom-call(bf16[256,2048]{1,0:T(8,128)(2,1)} %after.35.refs_0_, bf16[256,2048]{1,0:T(8,128)(2,1)} %collective-permute-done.26.refs_1_, bf16[256,2048]{1,0:T(8,128)(2,1)} %collective-permute-done.27.refs_2_, bf16[128,2048]{1,0:T(8,128)(2,1)} %collective-permute-done.28.refs_3_, ...), custom_call_target="tpu_custom_call" | custom-call | tf_op jit(solution)/shard_map/outer/pallas_call | solution.py:713
  373.3 14.8 %rows_product.5.refs_1_.mine = bf16[1024,2048]{1,0:T(8,128)(2,1)} custom-call(bf16[2048,2048]{1,0:T(8,128)(2,1)} %gated_back.1.left_ref.refs_10_, bf16[2048,2048]{1,0:T(8,128)(2,1)} %all-gather.6.cloned.1.call-done.refs_10_.weight_ref, bf16[1024,2048]{1,0:T(8,128)(2,1)} %after.39.rest_0_), custom_call_target="tpu_custom_call" | custom-call | tf_op jit(solution)/shard_map/rows_product/pallas_call | solution.py:737
  388.2 8.7 %rows_product.6.rest_0_ = bf16[1024,2048]{1,0:T(8,128)(2,1)} custom-call(bf16[2048,1024]{1,0:T(8,128)(2,1)} %after.40.left_ref, bf16[2048,1024]{1,0:T(8,128)(2,1)} %all-gather.8.cloned.1.call-done.refs_11_.weight_ref), custom_call_target="tpu_custom_call" | custom-call | tf_op jit(solution)/shard_map/rows_product/pallas_call | solution.py:737
  402.5 10.8 %collective-permute-done.46.from_near = bf16[128,2048]{1,0:T(8,128)(2,1)} collective-permute-done((bf16[128,2048]{1,0:T(8,128)(2,1)S(1)}, bf16[128,2048]{1,0:T(8,128)(2,1)}, u32[]{:S(2)}, u32[]{:S(2)}) %collective-permute-start.46) | collective-permute-done | bytes 524320 | tf_op jit(solution)/shard_map/ppermute | solution.py:847
  414.7 3.5 fold.4
  420.8 9.6 %rows_product.7.refs_1_.refs_0_ = bf16[1024,2048]{1,0:T(8,128)(2,1)} custom-call(bf16[2048,1024]{1,0:T(8,128)(2,1)} %after.40.left_ref, bf16[2048,1024]{1,0:T(8,128)(2,1)} %all-gather.8.cloned.1.call-done.refs_11_.weight_ref, bf16[1024,2048]{1,0:T(8,128)(2,1)} %collective-permute-done.45.rest_0_), custom_call_target="tpu_custom_call" | custom-call | tf_op jit(solution)/shard_map/rows_product/pallas_call | solution.py:737
  430.4 5.4 collective-permute-done.48
  444.4 21.7 %collective-permute-done.52.refs_1_.refs_12_ = bf16[256,2048]{1,0:T(8,128)(2,1)S(1)} collective-permute-done((bf16[256,2048]{1,0:T(8,128)(2,1)}, bf16[256,2048]{1,0:T(8,128)(2,1)S(1)}, u32[]{:S(2)}, u32[]{:S(2)}) %collective-permute-start.52) | collective-permute-done | bytes 1048608 | tf_op jit(solution)/shard_map/ppermute | solution.py:847
  472.7 5.9 collective-permute-done.54.refs_3_.refs_14_
  480.2 3.7 fusion.27
  487.3 9.4 %project.3.grad_ref.refs_1_ = bf16[2048,256]{1,0:T(8,128)(2,1)} custom-call(bf16[256,2048]{1,0:T(8,128)(2,1)} %after.41.refs_0_.refs_11_, bf16[256,2048]{1,0:T(8,128)(2,1)} %copy-done.55, bf16[256,2048]{1,0:T(8,128)(2,1)} %collective-permute-done.53.refs_2_.refs_13_, bf16[128,2048]{1,0:T(8,128)(2,1)} %collective-permute-done.54.refs_3_.refs_14_, ...), custom_call_target="tpu_custom_call" | custom-call | flops 4294967296 | bytes 8388608 | tf_op jit(solution)/shard_map/project/pallas_call | solution.py:564
  502.7 28.7 %attend_back.1.refs_10_.refs_0_ = bf16[2048,384]{1,0:T(8,128)(2,1)} custom-call(s32[8]{0:T(128)S(1)} %fusion.18.place_ref, bf16[2048,256]{1,0:T(8,128)(2,1)S(1)} %copy-done.8, bf16[2048,128]{1,0:T(8,128)(2,1)S(1)} %copy-done.12, f32[2048,4]{1,0:T(8,128)S(1)} %copy-done.10, bf16[2048,256]{1,0:T(8,128)(2,1)S(1)} %copy-done.6, f32[2048,1]{1,0:T(8,128)S(1)} %copy-done.4, ...), custom_call_target="tpu_custom_call" | custom-call | flops 38654705664 | bytes 7340032 | tf_op jit(solution)/shard_map/attend_back/pallas_call | solution.py:487
  534.2 4.4 add_convert_fusion.2.refs_2_.refs_0_
  544.7 16.7 %outer.5.refs_1_ = bf16[2048,640]{1,0:T(8,128)(2,1)} custom-call(bf16[256,2048]{1,0:T(8,128)(2,1)} %after.29.refs_0_, bf16[256,2048]{1,0:T(8,128)(2,1)} %after.30.refs_1_, bf16[256,2048]{1,0:T(8,128)(2,1)} %after.31.refs_2_, bf16[128,2048]{1,0:T(8,128)(2,1)} %collective-permute-done.9.refs_3_, bf16[128,2048]{1,0:T(8,128)(2,1)} %collective-permute-done.10.refs_4_, ...), custom_call_target="tpu_custom_call" | custom-call | flops 10737418240 | bytes 33554432 | tf_op jit(solution)/shard_map/outer/pallas_call | solution.py:713
  561.5 5.5 collective-permute-done.68.refs_9_.refs_0_
  569.8 5.5 convolution_convert_fusion
  576.7 6.1 collective-permute-done.70
  582.8 6.8 %add_convert_fusion.refs_1_.mine = bf16[1024,2048]{1,0:T(8,128)(2,1)} fusion(bf16[1024,2048]{1,0:T(8,128)(2,1)} %collective-permute-done.70, bf16[2048,384]{1,0:T(8,128)(2,1)} %after.44, bf16[2048,640]{1,0:T(8,128)(2,1)S(1)} %copy-done.33), kind=kOutput, calls=%fused_computation | convolution fusion | flops 1616904192 | bytes 10747904 | tf_op jit(solution)/shard_map/dot_general | solution.py:33
  599.4 7.9 %collective-permute-done.72.from_near = bf16[128,2048]{1,0:T(8,128)(2,1)S(1)} collective-permute-done((bf16[128,2048]{1,0:T(8,128)(2,1)}, bf16[128,2048]{1,0:T(8,128)(2,1)S(1)}, u32[]{:S(2)}, u32[]{:S(2)}) %collective-permute-start.72) | collective-permute-done | bytes 524320 | tf_op jit(solution)/shard_map/ppermute | solution.py:847
  608.9 3.6 fold.5
  618.1 11.5 %collective-permute-done.74.refs_1_ = bf16[128,2048]{1,0:T(8,128)(2,1)} collective-permute-done((bf16[128,2048]{1,0:T(8,128)(2,1)}, bf16[128,2048]{1,0:T(8,128)(2,1)}, u32[]{:S(2)}, u32[]{:S(2)}) %collective-permute-start.74) | collective-permute-done | bytes 524320 | tf_op jit(solution)/shard_map/ppermute | solution.py:847
  642.8 3.2 finish.1
  (443 shorter events, 182.8 us)
Async XLA Ops:
  7.2 96.3 %all-gather.4.cloned.1.call-start = ((), (), s32[]{:S(2)}) async-start(), calls=%async_computation.3 | async-start | bytes 3276800 | tf_op jit(solution)/shard_map/all_gather | solution.py:965
  26.5 224.1 %all-gather.6.cloned.1.call-start = ((), (), s32[]{:S(2)}) async-start(), calls=%async_computation.4 | async-start | bytes 10485760 | tf_op jit(solution)/shard_map/all_gather | solution.py:965
  31.7 22.7 %collective-permute-start.4 = (bf16[128,2048]{1,0:T(8,128)(2,1)S(1)}, bf16[128,2048]{1,0:T(8,128)(2,1)S(1)}, u32[]{:S(2)}, u32[]{:S(2)}) collective-permute-start(bf16[128,2048]{1,0:T(8,128)(2,1)S(1)} %get-tuple-element.117), channel_id=1, source_target_pairs={{0,4},{2,6},{4,0},{6,2},{1,5},{3,7},{5,1},{7,3},{8,12},{10,14},{12... | collective-permute-start | bytes 1572872 | tf_op jit(solution)/shard_map/ppermute | solution.py:847
  33.7 22.6 %collective-permute-start.5 = (bf16[128,2048]{1,0:T(8,128)(2,1)S(1)}, bf16[128,2048]{1,0:T(8,128)(2,1)S(1)}, u32[]{:S(2)}, u32[]{:S(2)}) collective-permute-start(bf16[128,2048]{1,0:T(8,128)(2,1)S(1)} %get-tuple-element.93), channel_id=1, source_target_pairs={{0,6},{2,4},{4,2},{6,0},{1,7},{3,5},{5,3},{7,1},{8,14},{10,12},{12... | collective-permute-start | bytes 1572872 | tf_op jit(solution)/shard_map/ppermute | solution.py:847
  57.2 256.0 %all-gather.8.cloned.1.call-start = ((), (), s32[]{:S(2)}) async-start(), calls=%async_computation.5 | async-start | bytes 5242880 | tf_op jit(solution)/shard_map/all_gather | solution.py:965
  60.9 22.4 %collective-permute-start.8 = (bf16[256,2048]{1,0:T(8,128)(2,1)}, bf16[256,2048]{1,0:T(8,128)(2,1)S(1)}, u32[]{:S(2)}, u32[]{:S(2)}) collective-permute-start(bf16[256,2048]{1,0:T(8,128)(2,1)} %after.29.refs_0_), channel_id=1, source_target_pairs={{0,4},{2,6},{4,0},{6,2},{1,5},{3,7},{5,1},{7,3},{8,12},{10,14},{12... | collective-permute-start | bytes 3145736 | tf_op jit(solution)/shard_map/ppermute | solution.py:847
  62.5 23.2 %collective-permute-start.6 = (bf16[256,2048]{1,0:T(8,128)(2,1)}, bf16[256,2048]{1,0:T(8,128)(2,1)S(1)}, u32[]{:S(2)}, u32[]{:S(2)}) collective-permute-start(bf16[256,2048]{1,0:T(8,128)(2,1)} %after.29.refs_0_), channel_id=1, source_target_pairs={{0,2},{2,0},{4,6},{6,4},{1,3},{3,1},{5,7},{7,5},{8,10},{10,8},{12,... | collective-permute-start | bytes 3145736 | tf_op jit(solution)/shard_map/ppermute | solution.py:847
  72.3 33.9 %collective-permute-start.11 = (bf16[256,2048]{1,0:T(8,128)(2,1)S(1)}, bf16[256,2048]{1,0:T(8,128)(2,1)}, u32[]{:S(2)}, u32[]{:S(2)}) collective-permute-start(bf16[256,2048]{1,0:T(8,128)(2,1)S(1)} %copy-done.13), channel_id=1, source_target_pairs={{0,1},{1,0},{2,3},{3,2},{4,5},{5,4},{6,7},{7,6},{8,9},{9,8},{10,11... | collective-permute-start | bytes 3145736 | tf_op jit(solution)/shard_map/ppermute | solution.py:850
  85.4 20.8 %collective-permute-start.13 = (bf16[256,2048]{1,0:T(8,128)(2,1)}, bf16[256,2048]{1,0:T(8,128)(2,1)}, u32[]{:S(2)}, u32[]{:S(2)}) collective-permute-start(bf16[256,2048]{1,0:T(8,128)(2,1)} %after.31.refs_2_), channel_id=1, source_target_pairs={{0,1},{1,0},{2,3},{3,2},{4,5},{5,4},{6,7},{7,6},{8,9},{9,8},{10,11... | collective-permute-start | bytes 3145736 | tf_op jit(solution)/shard_map/ppermute | solution.py:850
  89.0 17.2 %collective-permute-start.12 = (bf16[256,2048]{1,0:T(8,128)(2,1)}, bf16[256,2048]{1,0:T(8,128)(2,1)}, u32[]{:S(2)}, u32[]{:S(2)}) collective-permute-start(bf16[256,2048]{1,0:T(8,128)(2,1)} %after.30.refs_1_), channel_id=1, source_target_pairs={{0,1},{1,0},{2,3},{3,2},{4,5},{5,4},{6,7},{7,6},{8,9},{9,8},{10,11... | collective-permute-start | bytes 3145736 | tf_op jit(solution)/shard_map/ppermute | solution.py:850
  140.2 19.3 %collective-permute-start.16 = (bf16[1024,2048]{1,0:T(8,128)(2,1)}, bf16[1024,2048]{1,0:T(8,128)(2,1)}, u32[]{:S(2)}, u32[]{:S(2)}) collective-permute-start(bf16[1024,2048]{1,0:T(8,128)(2,1)} %convolution_convert_fusion.1), channel_id=1, source_target_pairs={{0,1},{1,0},{2,3},{3,2},{4,5},{5,4},{6,7},{7,6},{8,9},{9,8},{10,11... | collective-permute-start | bytes 12582920 | tf_op jit(solution)/shard_map/ppermute | solution.py:850
  159.5 255.2 %reduce-scatter.4.cloned.1.call-start = ((), (), s32[]{:S(2)}) async-start(), calls=%async_computation.6 | async-start | bytes 5242880 | tf_op jit(solution)/shard_map/reduce_scatter | solution.py:968
  166.1 25.2 %collective-permute-start.20 = (bf16[128,2048]{1,0:T(8,128)(2,1)S(1)}, bf16[128,2048]{1,0:T(8,128)(2,1)S(1)}, u32[]{:S(2)}, u32[]{:S(2)}) collective-permute-start(bf16[128,2048]{1,0:T(8,128)(2,1)S(1)} %get-tuple-element.72), channel_id=1, source_target_pairs={{0,4},{2,6},{4,0},{6,2},{1,5},{3,7},{5,1},{7,3},{8,12},{10,14},{12... | collective-permute-start | bytes 1572872 | tf_op jit(solution)/shard_map/ppermute | solution.py:847
  167.8 24.1 %collective-permute-start.21 = (bf16[128,2048]{1,0:T(8,128)(2,1)S(1)}, bf16[128,2048]{1,0:T(8,128)(2,1)S(1)}, u32[]{:S(2)}, u32[]{:S(2)}) collective-permute-start(bf16[128,2048]{1,0:T(8,128)(2,1)S(1)} %get-tuple-element.73), channel_id=1, source_target_pairs={{0,2},{2,0},{4,6},{6,4},{1,3},{3,1},{5,7},{7,5},{8,10},{10,8},{12,... | collective-permute-start | bytes 1572872 | tf_op jit(solution)/shard_map/ppermute | solution.py:847
  203.6 23.5 %collective-permute-start.26 = (bf16[256,2048]{1,0:T(8,128)(2,1)}, bf16[256,2048]{1,0:T(8,128)(2,1)}, u32[]{:S(2)}, u32[]{:S(2)}) collective-permute-start(bf16[256,2048]{1,0:T(8,128)(2,1)} %after.35.refs_0_), channel_id=1, source_target_pairs={{0,2},{2,0},{4,6},{6,4},{1,3},{3,1},{5,7},{7,5},{8,10},{10,8},{12,... | collective-permute-start | bytes 3145736 | tf_op jit(solution)/shard_map/ppermute | solution.py:847
  205.3 23.6 %collective-permute-start.27 = (bf16[256,2048]{1,0:T(8,128)(2,1)}, bf16[256,2048]{1,0:T(8,128)(2,1)}, u32[]{:S(2)}, u32[]{:S(2)}) collective-permute-start(bf16[256,2048]{1,0:T(8,128)(2,1)} %after.35.refs_0_), channel_id=1, source_target_pairs={{0,4},{2,6},{4,0},{6,2},{1,5},{3,7},{5,1},{7,3},{8,12},{10,14},{12... | collective-permute-start | bytes 3145736 | tf_op jit(solution)/shard_map/ppermute | solution.py:847
  205.7 41.9 %collective-permute-start.30 = (bf16[256,2048]{1,0:T(8,128)(2,1)}, bf16[256,2048]{1,0:T(8,128)(2,1)}, u32[]{:S(2)}, u32[]{:S(2)}) collective-permute-start(bf16[256,2048]{1,0:T(8,128)(2,1)} %after.35.refs_0_), channel_id=1, source_target_pairs={{0,1},{1,0},{2,3},{3,2},{4,5},{5,4},{6,7},{7,6},{8,9},{9,8},{10,11... | collective-permute-start | bytes 3145736 | tf_op jit(solution)/shard_map/ppermute | solution.py:850
  228.4 19.2 %collective-permute-start.31 = (bf16[256,2048]{1,0:T(8,128)(2,1)}, bf16[256,2048]{1,0:T(8,128)(2,1)}, u32[]{:S(2)}, u32[]{:S(2)}) collective-permute-start(bf16[256,2048]{1,0:T(8,128)(2,1)} %collective-permute-done.26.refs_1_), channel_id=1, source_target_pairs={{0,1},{1,0},{2,3},{3,2},{4,5},{5,4},{6,7},{7,6},{8,9},{9,8},{10,11... | collective-permute-start | bytes 3145736 | tf_op jit(solution)/shard_map/ppermute | solution.py:850
  231.3 16.8 %collective-permute-start.32 = (bf16[256,2048]{1,0:T(8,128)(2,1)}, bf16[256,2048]{1,0:T(8,128)(2,1)}, u32[]{:S(2)}, u32[]{:S(2)}) collective-permute-start(bf16[256,2048]{1,0:T(8,128)(2,1)} %collective-permute-done.27.refs_2_), channel_id=1, source_target_pairs={{0,1},{1,0},{2,3},{3,2},{4,5},{5,4},{6,7},{7,6},{8,9},{9,8},{10,11... | collective-permute-start | bytes 3145736 | tf_op jit(solution)/shard_map/ppermute | solution.py:850
  244.0 32.3 %collective-permute-start.36 = (bf16[256,2048]{1,0:T(8,128)(2,1)}, bf16[256,2048]{1,0:T(8,128)(2,1)}, u32[]{:S(2)}, u32[]{:S(2)}) collective-permute-start(bf16[256,2048]{1,0:T(8,128)(2,1)} %after.36.refs_0_), channel_id=1, source_target_pairs={{0,4},{2,6},{4,0},{6,2},{1,5},{3,7},{5,1},{7,3},{8,12},{10,14},{12... | collective-permute-start | bytes 3145736 | tf_op jit(solution)/shard_map/ppermute | solution.py:847
  245.9 32.8 %collective-permute-start.35 = (bf16[256,2048]{1,0:T(8,128)(2,1)}, bf16[256,2048]{1,0:T(8,128)(2,1)}, u32[]{:S(2)}, u32[]{:S(2)}) collective-permute-start(bf16[256,2048]{1,0:T(8,128)(2,1)} %after.36.refs_0_), channel_id=1, source_target_pairs={{0,2},{2,0},{4,6},{6,4},{1,3},{3,1},{5,7},{7,5},{8,10},{10,8},{12,... | collective-permute-start | bytes 3145736 | tf_op jit(solution)/shard_map/ppermute | solution.py:847
  248.1 45.6 %collective-permute-start.39 = (bf16[256,2048]{1,0:T(8,128)(2,1)}, bf16[256,2048]{1,0:T(8,128)(2,1)}, u32[]{:S(2)}, u32[]{:S(2)}) collective-permute-start(bf16[256,2048]{1,0:T(8,128)(2,1)} %after.36.refs_0_), channel_id=1, source_target_pairs={{0,1},{1,0},{2,3},{3,2},{4,5},{5,4},{6,7},{7,6},{8,9},{9,8},{10,11... | collective-permute-start | bytes 3145736 | tf_op jit(solution)/shard_map/ppermute | solution.py:850
  278.3 16.8 %collective-permute-start.41 = (bf16[256,2048]{1,0:T(8,128)(2,1)}, bf16[256,2048]{1,0:T(8,128)(2,1)}, u32[]{:S(2)}, u32[]{:S(2)}) collective-permute-start(bf16[256,2048]{1,0:T(8,128)(2,1)} %after.38.refs_2_), channel_id=1, source_target_pairs={{0,1},{1,0},{2,3},{3,2},{4,5},{5,4},{6,7},{7,6},{8,9},{9,8},{10,11... | collective-permute-start | bytes 3145736 | tf_op jit(solution)/shard_map/ppermute | solution.py:850
  313.1 225.5 %reduce-scatter.6.cloned.1.call-start = ((), (), s32[]{:S(2)}) async-start(), calls=%async_computation.7 | async-start | bytes 10485760 | tf_op jit(solution)/shard_map/reduce_scatter | solution.py:968
  346.6 26.7 %collective-permute-start.44 = (bf16[1024,2048]{1,0:T(8,128)(2,1)}, bf16[1024,2048]{1,0:T(8,128)(2,1)}, u32[]{:S(2)}, u32[]{:S(2)}) collective-permute-start(bf16[1024,2048]{1,0:T(8,128)(2,1)} %rows_product.4.refs_11_), channel_id=1, source_target_pairs={{0,1},{1,0},{2,3},{3,2},{4,5},{5,4},{6,7},{7,6},{8,9},{9,8},{10,11... | collective-permute-start | bytes 12582920 | tf_op jit(solution)/shard_map/ppermute | solution.py:850
  373.3 256.3 %reduce-scatter.8.cloned.1.call-start = ((), (), s32[]{:S(2)}) async-start(), calls=%async_computation.8 | async-start | bytes 3276800 | tf_op jit(solution)/shard_map/reduce_scatter | solution.py:968
  396.8 23.9 %collective-permute-start.45 = (bf16[1024,2048]{1,0:T(8,128)(2,1)}, bf16[1024,2048]{1,0:T(8,128)(2,1)}, u32[]{:S(2)}, u32[]{:S(2)}) collective-permute-start(bf16[1024,2048]{1,0:T(8,128)(2,1)} %rows_product.6.rest_0_), channel_id=1, source_target_pairs={{0,1},{1,0},{2,3},{3,2},{4,5},{5,4},{6,7},{7,6},{8,9},{9,8},{10,11... | collective-permute-start | bytes 12582920 | tf_op jit(solution)/shard_map/ppermute | solution.py:850
  401.2 29.1 %collective-permute-start.49 = (bf16[128,2048]{1,0:T(8,128)(2,1)}, bf16[128,2048]{1,0:T(8,128)(2,1)}, u32[]{:S(2)}, u32[]{:S(2)}) collective-permute-start(bf16[128,2048]{1,0:T(8,128)(2,1)} %get-tuple-element.66), channel_id=1, source_target_pairs={{0,4},{2,6},{4,0},{6,2},{1,5},{3,7},{5,1},{7,3},{8,12},{10,14},{12... | collective-permute-start | bytes 1572872 | tf_op jit(solution)/shard_map/ppermute | solution.py:847
  402.3 28.1 %collective-permute-start.50 = (bf16[128,2048]{1,0:T(8,128)(2,1)}, bf16[128,2048]{1,0:T(8,128)(2,1)}, u32[]{:S(2)}, u32[]{:S(2)}) collective-permute-start(bf16[128,2048]{1,0:T(8,128)(2,1)} %get-tuple-element.67), channel_id=1, source_target_pairs={{0,2},{2,0},{4,6},{6,4},{1,3},{3,1},{5,7},{7,5},{8,10},{10,8},{12,... | collective-permute-start | bytes 1572872 | tf_op jit(solution)/shard_map/ppermute | solution.py:847
  418.2 17.5 %collective-permute-start.48 = (bf16[128,2048]{1,0:T(8,128)(2,1)}, bf16[128,2048]{1,0:T(8,128)(2,1)S(1)}, u32[]{:S(2)}, u32[]{:S(2)}) collective-permute-start(bf16[128,2048]{1,0:T(8,128)(2,1)} %get-tuple-element.41), channel_id=1, source_target_pairs={{0,2},{2,0},{4,6},{6,4},{1,3},{3,1},{5,7},{7,5},{8,10},{10,8},{12,... | collective-permute-start | bytes 1572872 | tf_op jit(solution)/shard_map/ppermute | solution.py:847
  441.9 24.2 %collective-permute-start.52 = (bf16[256,2048]{1,0:T(8,128)(2,1)}, bf16[256,2048]{1,0:T(8,128)(2,1)S(1)}, u32[]{:S(2)}, u32[]{:S(2)}) collective-permute-start(bf16[256,2048]{1,0:T(8,128)(2,1)} %after.41.refs_0_.refs_11_), channel_id=1, source_target_pairs={{0,2},{2,0},{4,6},{6,4},{1,3},{3,1},{5,7},{7,5},{8,10},{10,8},{12,... | collective-permute-start | bytes 3145736 | tf_op jit(solution)/shard_map/ppermute | solution.py:847
  443.3 24.4 %collective-permute-start.53 = (bf16[256,2048]{1,0:T(8,128)(2,1)}, bf16[256,2048]{1,0:T(8,128)(2,1)}, u32[]{:S(2)}, u32[]{:S(2)}) collective-permute-start(bf16[256,2048]{1,0:T(8,128)(2,1)} %after.41.refs_0_.refs_11_), channel_id=1, source_target_pairs={{0,4},{2,6},{4,0},{6,2},{1,5},{3,7},{5,1},{7,3},{8,12},{10,14},{12... | collective-permute-start | bytes 3145736 | tf_op jit(solution)/shard_map/ppermute | solution.py:847
  469.9 17.4 %collective-permute-start.60 = (bf16[256,2048]{1,0:T(8,128)(2,1)S(1)}, bf16[256,2048]{1,0:T(8,128)(2,1)}, u32[]{:S(2)}, u32[]{:S(2)}) collective-permute-start(bf16[256,2048]{1,0:T(8,128)(2,1)S(1)} %collective-permute-done.52.refs_1_.refs_12_), channel_id=1, source_target_pairs={{0,1},{1,0},{2,3},{3,2},{4,5},{5,4},{6,7},{7,6},{8,9},{9,8},{10,11... | collective-permute-start | bytes 3145736 | tf_op jit(solution)/shard_map/ppermute | solution.py:850
  470.4 16.9 %collective-permute-start.61 = (bf16[256,2048]{1,0:T(8,128)(2,1)}, bf16[256,2048]{1,0:T(8,128)(2,1)}, u32[]{:S(2)}, u32[]{:S(2)}) collective-permute-start(bf16[256,2048]{1,0:T(8,128)(2,1)} %collective-permute-done.53.refs_2_.refs_13_), channel_id=1, source_target_pairs={{0,1},{1,0},{2,3},{3,2},{4,5},{5,4},{6,7},{7,6},{8,9},{9,8},{10,11... | collective-permute-start | bytes 3145736 | tf_op jit(solution)/shard_map/ppermute | solution.py:850
  483.8 47.5 %collective-permute-start.56 = (bf16[256,2048]{1,0:T(8,128)(2,1)}, bf16[256,2048]{1,0:T(8,128)(2,1)}, u32[]{:S(2)}, u32[]{:S(2)}) collective-permute-start(bf16[256,2048]{1,0:T(8,128)(2,1)} %get-tuple-element.61), channel_id=1, source_target_pairs={{0,2},{2,0},{4,6},{6,4},{1,3},{3,1},{5,7},{7,5},{8,10},{10,8},{12,... | collective-permute-start | bytes 3145736 | tf_op jit(solution)/shard_map/ppermute | solution.py:847
  485.4 48.8 %collective-permute-start.57 = (bf16[256,2048]{1,0:T(8,128)(2,1)}, bf16[256,2048]{1,0:T(8,128)(2,1)}, u32[]{:S(2)}, u32[]{:S(2)}) collective-permute-start(bf16[256,2048]{1,0:T(8,128)(2,1)} %get-tuple-element.63), channel_id=1, source_target_pairs={{0,4},{2,6},{4,0},{6,2},{1,5},{3,7},{5,1},{7,3},{8,12},{10,14},{12... | collective-permute-start | bytes 3145736 | tf_op jit(solution)/shard_map/ppermute | solution.py:847
  486.2 47.9 %collective-permute-start.58 = (bf16[256,2048]{1,0:T(8,128)(2,1)}, bf16[256,2048]{1,0:T(8,128)(2,1)}, u32[]{:S(2)}, u32[]{:S(2)}) collective-permute-start(bf16[256,2048]{1,0:T(8,128)(2,1)} %get-tuple-element.62), channel_id=1, source_target_pairs={{0,6},{2,4},{4,2},{6,0},{1,7},{3,5},{5,3},{7,1},{8,14},{10,12},{12... | collective-permute-start | bytes 3145736 | tf_op jit(solution)/shard_map/ppermute | solution.py:847
  499.2 44.2 %collective-permute-start.64 = (bf16[128,1024]{1,0:T(8,128)(2,1)}, bf16[128,1024]{1,0:T(8,128)(2,1)}, u32[]{:S(2)}, u32[]{:S(2)}) collective-permute-start(bf16[128,1024]{1,0:T(8,128)(2,1)} %get-tuple-element.87), channel_id=1, source_target_pairs={{0,2},{2,0},{4,6},{6,4},{1,3},{3,1},{5,7},{7,5},{8,10},{10,8},{12,... | collective-permute-start | bytes 786440 | tf_op jit(solution)/shard_map/ppermute | solution.py:847
  500.7 60.8 %collective-permute-start.65 = (bf16[128,1024]{1,0:T(8,128)(2,1)}, bf16[128,1024]{1,0:T(8,128)(2,1)S(1)}, u32[]{:S(2)}, u32[]{:S(2)}) collective-permute-start(bf16[128,1024]{1,0:T(8,128)(2,1)} %get-tuple-element.86), channel_id=1, source_target_pairs={{0,4},{2,6},{4,0},{6,2},{1,5},{3,7},{5,1},{7,3},{8,12},{10,14},{12... | collective-permute-start | bytes 786440 | tf_op jit(solution)/shard_map/ppermute | solution.py:847
  531.4 30.1 %collective-permute-start.66 = (bf16[128,1024]{1,0:T(8,128)(2,1)}, bf16[128,1024]{1,0:T(8,128)(2,1)S(1)}, u32[]{:S(2)}, u32[]{:S(2)}) collective-permute-start(bf16[128,1024]{1,0:T(8,128)(2,1)} %get-tuple-element.85), channel_id=1, source_target_pairs={{0,6},{2,4},{4,2},{6,0},{1,7},{3,5},{5,3},{7,1},{8,14},{10,12},{12... | collective-permute-start | bytes 786440 | tf_op jit(solution)/shard_map/ppermute | solution.py:847
  541.2 20.3 %collective-permute-start.67 = (bf16[128,2048]{1,0:T(8,128)(2,1)}, bf16[128,2048]{1,0:T(8,128)(2,1)S(1)}, u32[]{:S(2)}, u32[]{:S(2)}) collective-permute-start(bf16[128,2048]{1,0:T(8,128)(2,1)} %get-tuple-element.83), channel_id=1, source_target_pairs={{0,2},{2,0},{4,6},{6,4},{1,3},{3,1},{5,7},{7,5},{8,10},{10,8},{12,... | collective-permute-start | bytes 1572872 | tf_op jit(solution)/shard_map/ppermute | solution.py:847
  541.9 25.2 %collective-permute-start.68 = (bf16[128,2048]{1,0:T(8,128)(2,1)S(1)}, bf16[128,2048]{1,0:T(8,128)(2,1)S(1)}, u32[]{:S(2)}, u32[]{:S(2)}) collective-permute-start(bf16[128,2048]{1,0:T(8,128)(2,1)S(1)} %get-tuple-element.82), channel_id=1, source_target_pairs={{0,4},{2,6},{4,0},{6,2},{1,5},{3,7},{5,1},{7,3},{8,12},{10,14},{12... | collective-permute-start | bytes 1572872 | tf_op jit(solution)/shard_map/ppermute | solution.py:847
  543.4 23.7 %collective-permute-start.69 = (bf16[128,2048]{1,0:T(8,128)(2,1)S(1)}, bf16[128,2048]{1,0:T(8,128)(2,1)S(1)}, u32[]{:S(2)}, u32[]{:S(2)}) collective-permute-start(bf16[128,2048]{1,0:T(8,128)(2,1)S(1)} %get-tuple-element.81), channel_id=1, source_target_pairs={{0,6},{2,4},{4,2},{6,0},{1,7},{3,5},{5,3},{7,1},{8,14},{10,12},{12... | collective-permute-start | bytes 1572872 | tf_op jit(solution)/shard_map/ppermute | solution.py:847
  594.1 38.2 %collective-permute-start.75 = (bf16[128,2048]{1,0:T(8,128)(2,1)}, bf16[128,2048]{1,0:T(8,128)(2,1)}, u32[]{:S(2)}, u32[]{:S(2)}) collective-permute-start(bf16[128,2048]{1,0:T(8,128)(2,1)} %get-tuple-element.57), channel_id=1, source_target_pairs={{0,4},{2,6},{4,0},{6,2},{1,5},{3,7},{5,1},{7,3},{8,12},{10,14},{12... | collective-permute-start | bytes 1572872 | tf_op jit(solution)/shard_map/ppermute | solution.py:847
  594.9 38.2 %collective-permute-start.76 = (bf16[128,2048]{1,0:T(8,128)(2,1)}, bf16[128,2048]{1,0:T(8,128)(2,1)}, u32[]{:S(2)}, u32[]{:S(2)}) collective-permute-start(bf16[128,2048]{1,0:T(8,128)(2,1)} %get-tuple-element.58), channel_id=1, source_target_pairs={{0,2},{2,0},{4,6},{6,4},{1,3},{3,1},{5,7},{7,5},{8,10},{10,8},{12,... | collective-permute-start | bytes 1572872 | tf_op jit(solution)/shard_map/ppermute | solution.py:847
  612.5 17.1 %collective-permute-start.74 = (bf16[128,2048]{1,0:T(8,128)(2,1)}, bf16[128,2048]{1,0:T(8,128)(2,1)}, u32[]{:S(2)}, u32[]{:S(2)}) collective-permute-start(bf16[128,2048]{1,0:T(8,128)(2,1)} %get-tuple-element.46), channel_id=1, source_target_pairs={{0,2},{2,0},{4,6},{6,4},{1,3},{3,1},{5,7},{7,5},{8,10},{10,8},{12,... | collective-permute-start | bytes 1572872 | tf_op jit(solution)/shard_map/ppermute | solution.py:847
  617.1 33.7 %collective-permute-start.83 = (f32[128]{0:T(128)S(1)}, f32[128]{0:T(128)S(1)}, u32[]{:S(2)}, u32[]{:S(2)}) collective-permute-start(f32[128]{0:T(128)S(1)} %add.146), channel_id=1, source_target_pairs={{0,1},{1,0},{2,3},{3,2},{4,5},{5,4},{6,7},{7,6},{8,9},{9,8},{10,11... | collective-permute-start | bytes 1544 | tf_op jit(solution)/shard_map/ppermute | solution.py:850
  629.6 21.7 %collective-permute-start.71 = (bf16[256,2048]{1,0:T(8,128)(2,1)S(1)}, bf16[256,2048]{1,0:T(8,128)(2,1)}, u32[]{:S(2)}, u32[]{:S(2)}) collective-permute-start(bf16[256,2048]{1,0:T(8,128)(2,1)S(1)} %copy-done.31), channel_id=1, source_target_pairs={{0,1},{1,0},{2,3},{3,2},{4,5},{5,4},{6,7},{7,6},{8,9},{9,8},{10,11... | collective-permute-start | bytes 3145736 | tf_op jit(solution)/shard_map/ppermute | solution.py:850
  (116 other events, 1161.7 us)
Sparse Core Ops, SparseCore 0:
  26.6 55.1 all-gather.3
  83.9 148.3 all-gather.5
  233.9 78.9 all-gather.7
  315.1 75.2 reduce-scatter.3
  392.8 144.9 reduce-scatter.5
  575.4 52.0 reduce-scatter.7

commit v5 on v4

--- a/solution.py
+++ b/solution.py
@@ -881,7 +881,7 @@
                 + near_last.astype(jnp.float32),
             ]
         )
-        return total, (ctx_first, near_last)
+        return total, (to_ctx, to_near)
 
     def scatter_direct(mine):
         total = mine[:rows].astype(jnp.float32)
@@ -1068,9 +1068,9 @@
     )
     attn_far = far_scatter(attn_part)
     pair_rows = to_rows(pair_far)
-    product = narrow(after(d_qkv, attn_part, middle_out, *down_rows, *pair_rows), in_w)
+    product = narrow(after(d_qkv, attn_part, middle_out, *down_rows), in_w)
     back_mine = own_side(product, swap_core(other_side(product)))
-    back_a, passed = scatter(back_mine)
+    back_a, passed = scatter(back_mine, *pair_rows)
     layer_out = both_halves(after(middle_out, back_mine))
     input_grad = d_middle + through_norm(back_a, own_f * inverse_rms(own_f))
 

time: 673 us -> 670 us (level)
  waiting for transfers between devices: 216 us -> 202 us
    ppermute x56, waiting for transfers between devices: 206 us -> 198 us  [swap(): lax.ppermute(value, ('near', 'ctx'), [(i, i ^ m) for i in range(group)])]
    unnamed x159 -> x151, local copies, waits for them, and re-layouts: 24.6 us -> 25.3 us
  transfers between devices with their start and end apart: 90 -> 90, of which waited for: 40 -> 38; matrix products, arithmetic and copies ran while one was open for 15% -> 17% of each run, Pallas kernels for 35% -> 35%
where the time goes in v5:
time: 670 us; the launch traced here: 664 us
  Pallas kernels  232 us (35%)
  waiting for transfers between devices  202 us (30%)
  local copies, waits for them, and re-layouts  82.7 us (12%)
  starting transfers between devices  66.4 us (10%)
  other arithmetic  44 us (7%)
  matrix products  21.4 us (3%)
  between operations  15.6 us (2%)
    ppermute x56, waiting for transfers between devices, swap(): lax.ppermute(value, ('near', 'ctx'), [(i, i ^ m) for i in range(group)])  198 us
    ppermute x56, starting transfers between devices, swap(): lax.ppermute(value, ('near', 'ctx'), [(i, i ^ m) for i in range(group)])  62.8 us
    pallas_call x3, Pallas kernels, outer(): pl.pallas_call(functools.partial(outer_kernel, counts, len(tokens), block...  59.4 us
    pallas_call x4, Pallas kernels, rows_product(): pl.pallas_call(functools.partial(rows_kernel, len(extra)), out_shape=jax....  46.5 us
    pallas_call x1, Pallas kernels, attend_back(): pl.pallas_call(functools.partial(attend_back_kernel, rows, window, heads,...  28.7 us
    pallas_call x1, Pallas kernels, gated(): pl.pallas_call(functools.partial(gated_kernel, len(pieces), chunk), out_s...  25.7 us
    unnamed x151, local copies, waits for them, and re-layouts  25.3 us
    dot_general x4, matrix products, matmul_trans(): lax.dot_general(left, right, (((1,), (1,)), ((), ())), preferred_element_...  21.4 us
  transfers between devices with their start and end apart: 90, of which 38 were waited for; matrix products, arithmetic and copies ran while one was open for 17% of the time, Pallas kernels for 35%

profile of v5, /device:TPU:0, one launch (start us, length us, event | category | flops | bytes accessed | tf_op | source)
XLA Modules:
  0.0 664.5 jit_solution(16729742470579112113)
XLA Ops:
  11.3 3.0 collective-permute-start
  19.0 4.7 collective-permute-done.1
  37.5 9.0 %collective-permute-done.3 = bf16[128,2048]{1,0:T(8,128)(2,1)S(1)} collective-permute-done((bf16[128,2048]{1,0:T(8,128)(2,1)S(1)}, bf16[128,2048]{1,0:T(8,128)(2,1)S(1)}, u32[]{:S(2)}, u32[]{:S(2)}) %collective-permute-start.3) | collective-permute-done | bytes 524320 | tf_op jit(solution)/shard_map/ppermute | solution.py:847
  47.3 7.2 %collective-permute-done.4 = bf16[128,2048]{1,0:T(8,128)(2,1)S(1)} collective-permute-done((bf16[128,2048]{1,0:T(8,128)(2,1)S(1)}, bf16[128,2048]{1,0:T(8,128)(2,1)S(1)}, u32[]{:S(2)}, u32[]{:S(2)}) %collective-permute-start.4) | collective-permute-done | bytes 524320 | tf_op jit(solution)/shard_map/ppermute | solution.py:847
  65.6 3.7 fusion.14
  69.3 3.0 pad_maximum_fusion.2
  72.3 11.1 %collective-permute-done.8.refs_0_ = bf16[256,2048]{1,0:T(8,128)(2,1)S(1)} collective-permute-done((bf16[256,2048]{1,0:T(8,128)(2,1)}, bf16[256,2048]{1,0:T(8,128)(2,1)S(1)}, u32[]{:S(2)}, u32[]{:S(2)}) %collective-permute-start.8) | collective-permute-done | bytes 1048608 | tf_op jit(solution)/shard_map/ppermute | solution.py:847
  89.0 11.0 %collective-permute-done.10.refs_4_ = bf16[128,2048]{1,0:T(8,128)(2,1)} collective-permute-done((bf16[128,2048]{1,0:T(8,128)(2,1)S(1)}, bf16[128,2048]{1,0:T(8,128)(2,1)}, u32[]{:S(2)}, u32[]{:S(2)}) %collective-permute-start.10) | collective-permute-done | bytes 524320 | tf_op jit(solution)/shard_map/ppermute | solution.py:847
  106.2 11.3 %project.2 = (f32[2048,384]{1,0:T(8,128)}, f32[2048,1]{1,0:T(8,128)}) custom-call(bf16[256,2048]{1,0:T(8,128)(2,1)} %after.29.refs_0_, bf16[256,2048]{1,0:T(8,128)(2,1)} %after.30.refs_1_, bf16[256,2048]{1,0:T(8,128)(2,1)} %after.31.refs_2_, bf16[128,2048]{1,0:T(8,128)(2,1)} %collective-permute-done.9.refs_3_, ...), custom_call_target="tpu_custom_call" | custom-call | flops 6442450944 | bytes 8388608 | tf_op jit(solution)/shard_map/project/pallas_call | solution.py:564
  117.6 17.2 %attend.1 = (bf16[2048,256]{1,0:T(8,128)(2,1)S(1)}, bf16[2048,128]{1,0:T(8,128)(2,1)S(1)}, bf16[2048,256]{1,0:T(8,128)(2,1)S(1)}, f32[2048,4]{1,0:T(8,128)S(1)}) custom-call(s32[8]{0:T(128)S(1)} %fusion.18.place_ref, f32[2048,384]{1,0:T(8,128)} %get-tuple-element.32.qkv_ref, f32[2048,128]{1,0:T(8,128)S(1)} %copy-done.2, f32[2048,128]{1,0:T(8,128)S(1)} %copy-done.3, ...), custom_call_target="tpu_custom_call" | custom-call | tf_op jit(solution)/shard_map/attend/pallas_call | solution.py:453
  134.8 5.5 convolution_convert_fusion.1
  145.3 5.9 collective-permute-done.23
  151.3 6.2 collective-permute-done.24
  159.6 3.8 add_convert_fusion.1.mine
  169.5 10.8 %collective-permute-done.17.from_near = bf16[128,2048]{1,0:T(8,128)(2,1)S(1)} collective-permute-done((bf16[128,2048]{1,0:T(8,128)(2,1)S(1)}, bf16[128,2048]{1,0:T(8,128)(2,1)S(1)}, u32[]{:S(2)}, u32[]{:S(2)}) %collective-permute-start.17) | collective-permute-done | bytes 524320 | tf_op jit(solution)/shard_map/ppermute | solution.py:847
  181.9 3.6 fold.3
  187.1 4.3 collective-permute-done.20
  191.9 7.8 %collective-permute-done.19 = bf16[128,2048]{1,0:T(8,128)(2,1)S(1)} collective-permute-done((bf16[128,2048]{1,0:T(8,128)(2,1)}, bf16[128,2048]{1,0:T(8,128)(2,1)S(1)}, u32[]{:S(2)}, u32[]{:S(2)}) %collective-permute-start.19) | collective-permute-done | bytes 524320 | tf_op jit(solution)/shard_map/ppermute | solution.py:847
  205.1 21.4 %collective-permute-done.26.refs_1_ = bf16[256,2048]{1,0:T(8,128)(2,1)} collective-permute-done((bf16[256,2048]{1,0:T(8,128)(2,1)}, bf16[256,2048]{1,0:T(8,128)(2,1)}, u32[]{:S(2)}, u32[]{:S(2)}) %collective-permute-start.26) | collective-permute-done | bytes 1048608 | tf_op jit(solution)/shard_map/ppermute | solution.py:847
  233.4 5.9 collective-permute-done.28.refs_3_
  239.3 4.2 collective-permute-done.29.refs_4_
  250.1 25.7 %gated.1 = (bf16[2048,1024]{1,0:T(8,128)(2,1)}, bf16[2048,1024]{1,0:T(8,128)(2,1)}, bf16[2048,1024]{1,0:T(8,128)(2,1)}, f32[2048,1]{1,0:T(8,128)}) custom-call(bf16[256,2048]{1,0:T(8,128)(2,1)} %after.35.refs_0_, bf16[256,2048]{1,0:T(8,128)(2,1)} %collective-permute-done.26.refs_1_, bf16[256,2048]{1,0:T(8,128)(2,1)} %collective-permute-done.27.refs_2_, ...), custom_call_target="tpu_custom_call" | custom-call | tf_op jit(solution)/shard_map/gated/pallas_call | solution.py:609
  279.5 12.9 %collective-permute-done.38.refs_4_ = bf16[128,2048]{1,0:T(8,128)(2,1)} collective-permute-done((bf16[128,2048]{1,0:T(8,128)(2,1)}, bf16[128,2048]{1,0:T(8,128)(2,1)}, u32[]{:S(2)}, u32[]{:S(2)}) %collective-permute-start.38) | collective-permute-done | bytes 524320 | tf_op jit(solution)/shard_map/ppermute | solution.py:847
  296.3 16.2 %outer.3.refs_10_ = bf16[2048,1024]{1,0:T(8,128)(2,1)} custom-call(bf16[256,2048]{1,0:T(8,128)(2,1)} %after.36.refs_0_, bf16[256,2048]{1,0:T(8,128)(2,1)} %after.37.refs_1_, bf16[256,2048]{1,0:T(8,128)(2,1)} %after.38.refs_2_, bf16[128,2048]{1,0:T(8,128)(2,1)} %copy-done.53, bf16[128,2048]{1,0:T(8,128)(2,1)} %collective-permute-done.38.refs_4_, ...), custom_call_target="tpu_custom_call" | custom-call | tf_op jit(solution)/shard_map/outer/pallas_call | solution.py:713
  313.0 20.0 %gated_back.1.left_ref.refs_10_ = bf16[2048,2048]{1,0:T(8,128)(2,1)} custom-call(bf16[256,2048]{1,0:T(8,128)(2,1)} %after.36.refs_0_, bf16[256,2048]{1,0:T(8,128)(2,1)} %after.37.refs_1_, bf16[256,2048]{1,0:T(8,128)(2,1)} %after.38.refs_2_, bf16[128,2048]{1,0:T(8,128)(2,1)} %copy-done.53, bf16[128,2048]{1,0:T(8,128)(2,1)} %collective-permute-done.38.refs_4_, ...), custom_call_target="tpu_custom_call" | custom-call | tf_op jit(solution)/shard_map/gated_back/pallas_call | solution.py:652
  333.0 13.4 %rows_product.4.refs_11_ = bf16[1024,2048]{1,0:T(8,128)(2,1)} custom-call(bf16[2048,2048]{1,0:T(8,128)(2,1)} %gated_back.1.left_ref.refs_10_, bf16[2048,2048]{1,0:T(8,128)(2,1)} %all-gather.6.cloned.1.call-done.refs_10_.weight_ref), custom_call_target="tpu_custom_call" | custom-call | tf_op jit(solution)/shard_map/rows_product/pallas_call | solution.py:737
  346.4 26.5 %outer.4.refs_1_ = bf16[2048,2048]{1,0:T(8,128)(2,1)} custom-call(bf16[256,2048]{1,0:T(8,128)(2,1)} %after.35.refs_0_, bf16[256,2048]{1,0:T(8,128)(2,1)} %collective-permute-done.26.refs_1_, bf16[256,2048]{1,0:T(8,128)(2,1)} %collective-permute-done.27.refs_2_, bf16[128,2048]{1,0:T(8,128)(2,1)} %collective-permute-done.28.refs_3_, ...), custom_call_target="tpu_custom_call" | custom-call | tf_op jit(solution)/shard_map/outer/pallas_call | solution.py:713
  373.0 14.8 %rows_product.5.refs_1_.mine = bf16[1024,2048]{1,0:T(8,128)(2,1)} custom-call(bf16[2048,2048]{1,0:T(8,128)(2,1)} %gated_back.1.left_ref.refs_10_, bf16[2048,2048]{1,0:T(8,128)(2,1)} %all-gather.6.cloned.1.call-done.refs_10_.weight_ref, bf16[1024,2048]{1,0:T(8,128)(2,1)} %after.39.rest_0_), custom_call_target="tpu_custom_call" | custom-call | tf_op jit(solution)/shard_map/rows_product/pallas_call | solution.py:737
  387.8 8.7 %rows_product.6.rest_0_ = bf16[1024,2048]{1,0:T(8,128)(2,1)} custom-call(bf16[2048,1024]{1,0:T(8,128)(2,1)} %after.40.left_ref, bf16[2048,1024]{1,0:T(8,128)(2,1)} %all-gather.8.cloned.1.call-done.refs_11_.weight_ref), custom_call_target="tpu_custom_call" | custom-call | tf_op jit(solution)/shard_map/rows_product/pallas_call | solution.py:737
  402.2 10.8 %collective-permute-done.46.from_near = bf16[128,2048]{1,0:T(8,128)(2,1)} collective-permute-done((bf16[128,2048]{1,0:T(8,128)(2,1)S(1)}, bf16[128,2048]{1,0:T(8,128)(2,1)}, u32[]{:S(2)}, u32[]{:S(2)}) %collective-permute-start.46) | collective-permute-done | bytes 524320 | tf_op jit(solution)/shard_map/ppermute | solution.py:847
  414.6 3.5 fold.4
  420.3 9.6 %rows_product.7.refs_1_.refs_0_ = bf16[1024,2048]{1,0:T(8,128)(2,1)} custom-call(bf16[2048,1024]{1,0:T(8,128)(2,1)} %after.40.left_ref, bf16[2048,1024]{1,0:T(8,128)(2,1)} %all-gather.8.cloned.1.call-done.refs_11_.weight_ref, bf16[1024,2048]{1,0:T(8,128)(2,1)} %collective-permute-done.45.rest_0_), custom_call_target="tpu_custom_call" | custom-call | tf_op jit(solution)/shard_map/rows_product/pallas_call | solution.py:737
  429.9 5.8 collective-permute-done.48
  443.8 22.2 %collective-permute-done.52.refs_1_.refs_12_ = bf16[256,2048]{1,0:T(8,128)(2,1)S(1)} collective-permute-done((bf16[256,2048]{1,0:T(8,128)(2,1)}, bf16[256,2048]{1,0:T(8,128)(2,1)S(1)}, u32[]{:S(2)}, u32[]{:S(2)}) %collective-permute-start.52) | collective-permute-done | bytes 1048608 | tf_op jit(solution)/shard_map/ppermute | solution.py:847
  472.3 6.3 collective-permute-done.54.refs_3_.refs_14_
  480.1 3.7 fusion.27
  487.3 9.4 %project.3.grad_ref.refs_1_ = bf16[2048,256]{1,0:T(8,128)(2,1)} custom-call(bf16[256,2048]{1,0:T(8,128)(2,1)} %after.41.refs_0_.refs_11_, bf16[256,2048]{1,0:T(8,128)(2,1)} %copy-done.52, bf16[256,2048]{1,0:T(8,128)(2,1)} %collective-permute-done.53.refs_2_.refs_13_, bf16[128,2048]{1,0:T(8,128)(2,1)} %collective-permute-done.54.refs_3_.refs_14_, ...), custom_call_target="tpu_custom_call" | custom-call | flops 4294967296 | bytes 8388608 | tf_op jit(solution)/shard_map/project/pallas_call | solution.py:564
  502.6 28.7 %attend_back.1.refs_10_.refs_0_ = bf16[2048,384]{1,0:T(8,128)(2,1)} custom-call(s32[8]{0:T(128)S(1)} %fusion.18.place_ref, bf16[2048,256]{1,0:T(8,128)(2,1)S(1)} %copy-done.8, bf16[2048,128]{1,0:T(8,128)(2,1)S(1)} %copy-done.12, f32[2048,4]{1,0:T(8,128)S(1)} %copy-done.10, bf16[2048,256]{1,0:T(8,128)(2,1)S(1)} %copy-done.6, f32[2048,1]{1,0:T(8,128)S(1)} %copy-done.4, ...), custom_call_target="tpu_custom_call" | custom-call | flops 38654705664 | bytes 7340032 | tf_op jit(solution)/shard_map/attend_back/pallas_call | solution.py:487
  533.7 4.4 add_convert_fusion.2.refs_2_.refs_0_
  538.1 16.7 %outer.5.refs_1_ = bf16[2048,640]{1,0:T(8,128)(2,1)} custom-call(bf16[256,2048]{1,0:T(8,128)(2,1)} %after.29.refs_0_, bf16[256,2048]{1,0:T(8,128)(2,1)} %after.30.refs_1_, bf16[256,2048]{1,0:T(8,128)(2,1)} %after.31.refs_2_, bf16[128,2048]{1,0:T(8,128)(2,1)} %collective-permute-done.9.refs_3_, bf16[128,2048]{1,0:T(8,128)(2,1)} %collective-permute-done.10.refs_4_, ...), custom_call_target="tpu_custom_call" | custom-call | flops 10737418240 | bytes 33554432 | tf_op jit(solution)/shard_map/outer/pallas_call | solution.py:713
  557.3 5.5 convolution_convert_fusion
  564.2 3.1 constant_dynamic-slice_fusion.4
  570.8 6.6 add_convert_fusion.refs_1_.mine
  595.8 9.1 %collective-permute-done.69.from_near = bf16[128,2048]{1,0:T(8,128)(2,1)S(1)} collective-permute-done((bf16[128,2048]{1,0:T(8,128)(2,1)}, bf16[128,2048]{1,0:T(8,128)(2,1)S(1)}, u32[]{:S(2)}, u32[]{:S(2)}) %collective-permute-start.69) | collective-permute-done | bytes 524320 | tf_op jit(solution)/shard_map/ppermute | solution.py:847
  605.9 3.6 fold.5
  622.9 4.5 collective-permute-done.74
  637.1 3.1 finish.1
  642.5 4.4 broadcast_multiply_fusion
  (435 shorter events, 189.1 us)
Async XLA Ops:
  7.2 96.3 %all-gather.4.cloned.1.call-start = ((), (), s32[]{:S(2)}) async-start(), calls=%async_computation.3 | async-start | bytes 3276800 | tf_op jit(solution)/shard_map/all_gather | solution.py:965
  26.5 223.6 %all-gather.6.cloned.1.call-start = ((), (), s32[]{:S(2)}) async-start(), calls=%async_computation.4 | async-start | bytes 10485760 | tf_op jit(solution)/shard_map/all_gather | solution.py:965
  31.7 22.7 %collective-permute-start.4 = (bf16[128,2048]{1,0:T(8,128)(2,1)S(1)}, bf16[128,2048]{1,0:T(8,128)(2,1)S(1)}, u32[]{:S(2)}, u32[]{:S(2)}) collective-permute-start(bf16[128,2048]{1,0:T(8,128)(2,1)S(1)} %get-tuple-element.117), channel_id=1, source_target_pairs={{0,4},{2,6},{4,0},{6,2},{1,5},{3,7},{5,1},{7,3},{8,12},{10,14},{12... | collective-permute-start | bytes 1572872 | tf_op jit(solution)/shard_map/ppermute | solution.py:847
  33.7 22.6 %collective-permute-start.5 = (bf16[128,2048]{1,0:T(8,128)(2,1)S(1)}, bf16[128,2048]{1,0:T(8,128)(2,1)S(1)}, u32[]{:S(2)}, u32[]{:S(2)}) collective-permute-start(bf16[128,2048]{1,0:T(8,128)(2,1)S(1)} %get-tuple-element.93), channel_id=1, source_target_pairs={{0,6},{2,4},{4,2},{6,0},{1,7},{3,5},{5,3},{7,1},{8,14},{10,12},{12... | collective-permute-start | bytes 1572872 | tf_op jit(solution)/shard_map/ppermute | solution.py:847
  57.2 255.8 %all-gather.8.cloned.1.call-start = ((), (), s32[]{:S(2)}) async-start(), calls=%async_computation.5 | async-start | bytes 5242880 | tf_op jit(solution)/shard_map/all_gather | solution.py:965
  60.9 22.4 %collective-permute-start.8 = (bf16[256,2048]{1,0:T(8,128)(2,1)}, bf16[256,2048]{1,0:T(8,128)(2,1)S(1)}, u32[]{:S(2)}, u32[]{:S(2)}) collective-permute-start(bf16[256,2048]{1,0:T(8,128)(2,1)} %after.29.refs_0_), channel_id=1, source_target_pairs={{0,4},{2,6},{4,0},{6,2},{1,5},{3,7},{5,1},{7,3},{8,12},{10,14},{12... | collective-permute-start | bytes 3145736 | tf_op jit(solution)/shard_map/ppermute | solution.py:847
  62.5 23.2 %collective-permute-start.6 = (bf16[256,2048]{1,0:T(8,128)(2,1)}, bf16[256,2048]{1,0:T(8,128)(2,1)S(1)}, u32[]{:S(2)}, u32[]{:S(2)}) collective-permute-start(bf16[256,2048]{1,0:T(8,128)(2,1)} %after.29.refs_0_), channel_id=1, source_target_pairs={{0,2},{2,0},{4,6},{6,4},{1,3},{3,1},{5,7},{7,5},{8,10},{10,8},{12,... | collective-permute-start | bytes 3145736 | tf_op jit(solution)/shard_map/ppermute | solution.py:847
  72.3 33.9 %collective-permute-start.11 = (bf16[256,2048]{1,0:T(8,128)(2,1)S(1)}, bf16[256,2048]{1,0:T(8,128)(2,1)}, u32[]{:S(2)}, u32[]{:S(2)}) collective-permute-start(bf16[256,2048]{1,0:T(8,128)(2,1)S(1)} %copy-done.13), channel_id=1, source_target_pairs={{0,1},{1,0},{2,3},{3,2},{4,5},{5,4},{6,7},{7,6},{8,9},{9,8},{10,11... | collective-permute-start | bytes 3145736 | tf_op jit(solution)/shard_map/ppermute | solution.py:850
  85.4 20.8 %collective-permute-start.13 = (bf16[256,2048]{1,0:T(8,128)(2,1)}, bf16[256,2048]{1,0:T(8,128)(2,1)}, u32[]{:S(2)}, u32[]{:S(2)}) collective-permute-start(bf16[256,2048]{1,0:T(8,128)(2,1)} %after.31.refs_2_), channel_id=1, source_target_pairs={{0,1},{1,0},{2,3},{3,2},{4,5},{5,4},{6,7},{7,6},{8,9},{9,8},{10,11... | collective-permute-start | bytes 3145736 | tf_op jit(solution)/shard_map/ppermute | solution.py:850
  89.0 17.2 %collective-permute-start.12 = (bf16[256,2048]{1,0:T(8,128)(2,1)}, bf16[256,2048]{1,0:T(8,128)(2,1)}, u32[]{:S(2)}, u32[]{:S(2)}) collective-permute-start(bf16[256,2048]{1,0:T(8,128)(2,1)} %after.30.refs_1_), channel_id=1, source_target_pairs={{0,1},{1,0},{2,3},{3,2},{4,5},{5,4},{6,7},{7,6},{8,9},{9,8},{10,11... | collective-permute-start | bytes 3145736 | tf_op jit(solution)/shard_map/ppermute | solution.py:850
  140.3 19.3 %collective-permute-start.16 = (bf16[1024,2048]{1,0:T(8,128)(2,1)}, bf16[1024,2048]{1,0:T(8,128)(2,1)}, u32[]{:S(2)}, u32[]{:S(2)}) collective-permute-start(bf16[1024,2048]{1,0:T(8,128)(2,1)} %convolution_convert_fusion.1), channel_id=1, source_target_pairs={{0,1},{1,0},{2,3},{3,2},{4,5},{5,4},{6,7},{7,6},{8,9},{9,8},{10,11... | collective-permute-start | bytes 12582920 | tf_op jit(solution)/shard_map/ppermute | solution.py:850
  159.5 255.1 %reduce-scatter.4.cloned.1.call-start = ((), (), s32[]{:S(2)}) async-start(), calls=%async_computation.6 | async-start | bytes 5242880 | tf_op jit(solution)/shard_map/reduce_scatter | solution.py:968
  166.1 25.3 %collective-permute-start.20 = (bf16[128,2048]{1,0:T(8,128)(2,1)S(1)}, bf16[128,2048]{1,0:T(8,128)(2,1)S(1)}, u32[]{:S(2)}, u32[]{:S(2)}) collective-permute-start(bf16[128,2048]{1,0:T(8,128)(2,1)S(1)} %get-tuple-element.72), channel_id=1, source_target_pairs={{0,4},{2,6},{4,0},{6,2},{1,5},{3,7},{5,1},{7,3},{8,12},{10,14},{12... | collective-permute-start | bytes 1572872 | tf_op jit(solution)/shard_map/ppermute | solution.py:847
  167.8 24.1 %collective-permute-start.21 = (bf16[128,2048]{1,0:T(8,128)(2,1)S(1)}, bf16[128,2048]{1,0:T(8,128)(2,1)S(1)}, u32[]{:S(2)}, u32[]{:S(2)}) collective-permute-start(bf16[128,2048]{1,0:T(8,128)(2,1)S(1)} %get-tuple-element.73), channel_id=1, source_target_pairs={{0,2},{2,0},{4,6},{6,4},{1,3},{3,1},{5,7},{7,5},{8,10},{10,8},{12,... | collective-permute-start | bytes 1572872 | tf_op jit(solution)/shard_map/ppermute | solution.py:847
  203.1 23.5 %collective-permute-start.26 = (bf16[256,2048]{1,0:T(8,128)(2,1)}, bf16[256,2048]{1,0:T(8,128)(2,1)}, u32[]{:S(2)}, u32[]{:S(2)}) collective-permute-start(bf16[256,2048]{1,0:T(8,128)(2,1)} %after.35.refs_0_), channel_id=1, source_target_pairs={{0,2},{2,0},{4,6},{6,4},{1,3},{3,1},{5,7},{7,5},{8,10},{10,8},{12,... | collective-permute-start | bytes 3145736 | tf_op jit(solution)/shard_map/ppermute | solution.py:847
  204.8 23.6 %collective-permute-start.27 = (bf16[256,2048]{1,0:T(8,128)(2,1)}, bf16[256,2048]{1,0:T(8,128)(2,1)}, u32[]{:S(2)}, u32[]{:S(2)}) collective-permute-start(bf16[256,2048]{1,0:T(8,128)(2,1)} %after.35.refs_0_), channel_id=1, source_target_pairs={{0,4},{2,6},{4,0},{6,2},{1,5},{3,7},{5,1},{7,3},{8,12},{10,14},{12... | collective-permute-start | bytes 3145736 | tf_op jit(solution)/shard_map/ppermute | solution.py:847
  205.1 41.9 %collective-permute-start.30 = (bf16[256,2048]{1,0:T(8,128)(2,1)}, bf16[256,2048]{1,0:T(8,128)(2,1)}, u32[]{:S(2)}, u32[]{:S(2)}) collective-permute-start(bf16[256,2048]{1,0:T(8,128)(2,1)} %after.35.refs_0_), channel_id=1, source_target_pairs={{0,1},{1,0},{2,3},{3,2},{4,5},{5,4},{6,7},{7,6},{8,9},{9,8},{10,11... | collective-permute-start | bytes 3145736 | tf_op jit(solution)/shard_map/ppermute | solution.py:850
  227.9 19.2 %collective-permute-start.31 = (bf16[256,2048]{1,0:T(8,128)(2,1)}, bf16[256,2048]{1,0:T(8,128)(2,1)}, u32[]{:S(2)}, u32[]{:S(2)}) collective-permute-start(bf16[256,2048]{1,0:T(8,128)(2,1)} %collective-permute-done.26.refs_1_), channel_id=1, source_target_pairs={{0,1},{1,0},{2,3},{3,2},{4,5},{5,4},{6,7},{7,6},{8,9},{9,8},{10,11... | collective-permute-start | bytes 3145736 | tf_op jit(solution)/shard_map/ppermute | solution.py:850
  243.5 32.3 %collective-permute-start.36 = (bf16[256,2048]{1,0:T(8,128)(2,1)}, bf16[256,2048]{1,0:T(8,128)(2,1)}, u32[]{:S(2)}, u32[]{:S(2)}) collective-permute-start(bf16[256,2048]{1,0:T(8,128)(2,1)} %after.36.refs_0_), channel_id=1, source_target_pairs={{0,4},{2,6},{4,0},{6,2},{1,5},{3,7},{5,1},{7,3},{8,12},{10,14},{12... | collective-permute-start | bytes 3145736 | tf_op jit(solution)/shard_map/ppermute | solution.py:847
  245.3 32.8 %collective-permute-start.35 = (bf16[256,2048]{1,0:T(8,128)(2,1)}, bf16[256,2048]{1,0:T(8,128)(2,1)}, u32[]{:S(2)}, u32[]{:S(2)}) collective-permute-start(bf16[256,2048]{1,0:T(8,128)(2,1)} %after.36.refs_0_), channel_id=1, source_target_pairs={{0,2},{2,0},{4,6},{6,4},{1,3},{3,1},{5,7},{7,5},{8,10},{10,8},{12,... | collective-permute-start | bytes 3145736 | tf_op jit(solution)/shard_map/ppermute | solution.py:847
  247.6 45.6 %collective-permute-start.39 = (bf16[256,2048]{1,0:T(8,128)(2,1)}, bf16[256,2048]{1,0:T(8,128)(2,1)}, u32[]{:S(2)}, u32[]{:S(2)}) collective-permute-start(bf16[256,2048]{1,0:T(8,128)(2,1)} %after.36.refs_0_), channel_id=1, source_target_pairs={{0,1},{1,0},{2,3},{3,2},{4,5},{5,4},{6,7},{7,6},{8,9},{9,8},{10,11... | collective-permute-start | bytes 3145736 | tf_op jit(solution)/shard_map/ppermute | solution.py:850
  312.5 225.5 %reduce-scatter.6.cloned.1.call-start = ((), (), s32[]{:S(2)}) async-start(), calls=%async_computation.7 | async-start | bytes 10485760 | tf_op jit(solution)/shard_map/reduce_scatter | solution.py:968
  346.4 26.6 %collective-permute-start.44 = (bf16[1024,2048]{1,0:T(8,128)(2,1)}, bf16[1024,2048]{1,0:T(8,128)(2,1)}, u32[]{:S(2)}, u32[]{:S(2)}) collective-permute-start(bf16[1024,2048]{1,0:T(8,128)(2,1)} %rows_product.4.refs_11_), channel_id=1, source_target_pairs={{0,1},{1,0},{2,3},{3,2},{4,5},{5,4},{6,7},{7,6},{8,9},{9,8},{10,11... | collective-permute-start | bytes 12582920 | tf_op jit(solution)/shard_map/ppermute | solution.py:850
  372.9 246.4 %reduce-scatter.8.cloned.1.call-start = ((), (), s32[]{:S(2)}) async-start(), calls=%async_computation.8 | async-start | bytes 3276800 | tf_op jit(solution)/shard_map/reduce_scatter | solution.py:968
  396.5 23.8 %collective-permute-start.45 = (bf16[1024,2048]{1,0:T(8,128)(2,1)}, bf16[1024,2048]{1,0:T(8,128)(2,1)}, u32[]{:S(2)}, u32[]{:S(2)}) collective-permute-start(bf16[1024,2048]{1,0:T(8,128)(2,1)} %rows_product.6.rest_0_), channel_id=1, source_target_pairs={{0,1},{1,0},{2,3},{3,2},{4,5},{5,4},{6,7},{7,6},{8,9},{9,8},{10,11... | collective-permute-start | bytes 12582920 | tf_op jit(solution)/shard_map/ppermute | solution.py:850
  401.2 28.7 %collective-permute-start.49 = (bf16[128,2048]{1,0:T(8,128)(2,1)}, bf16[128,2048]{1,0:T(8,128)(2,1)}, u32[]{:S(2)}, u32[]{:S(2)}) collective-permute-start(bf16[128,2048]{1,0:T(8,128)(2,1)} %get-tuple-element.66), channel_id=1, source_target_pairs={{0,4},{2,6},{4,0},{6,2},{1,5},{3,7},{5,1},{7,3},{8,12},{10,14},{12... | collective-permute-start | bytes 1572872 | tf_op jit(solution)/shard_map/ppermute | solution.py:847
  401.7 28.1 %collective-permute-start.50 = (bf16[128,2048]{1,0:T(8,128)(2,1)}, bf16[128,2048]{1,0:T(8,128)(2,1)}, u32[]{:S(2)}, u32[]{:S(2)}) collective-permute-start(bf16[128,2048]{1,0:T(8,128)(2,1)} %get-tuple-element.67), channel_id=1, source_target_pairs={{0,2},{2,0},{4,6},{6,4},{1,3},{3,1},{5,7},{7,5},{8,10},{10,8},{12,... | collective-permute-start | bytes 1572872 | tf_op jit(solution)/shard_map/ppermute | solution.py:847
  418.2 17.5 %collective-permute-start.48 = (bf16[128,2048]{1,0:T(8,128)(2,1)}, bf16[128,2048]{1,0:T(8,128)(2,1)S(1)}, u32[]{:S(2)}, u32[]{:S(2)}) collective-permute-start(bf16[128,2048]{1,0:T(8,128)(2,1)} %get-tuple-element.41), channel_id=1, source_target_pairs={{0,2},{2,0},{4,6},{6,4},{1,3},{3,1},{5,7},{7,5},{8,10},{10,8},{12,... | collective-permute-start | bytes 1572872 | tf_op jit(solution)/shard_map/ppermute | solution.py:847
  441.8 24.2 %collective-permute-start.52 = (bf16[256,2048]{1,0:T(8,128)(2,1)}, bf16[256,2048]{1,0:T(8,128)(2,1)S(1)}, u32[]{:S(2)}, u32[]{:S(2)}) collective-permute-start(bf16[256,2048]{1,0:T(8,128)(2,1)} %after.41.refs_0_.refs_11_), channel_id=1, source_target_pairs={{0,2},{2,0},{4,6},{6,4},{1,3},{3,1},{5,7},{7,5},{8,10},{10,8},{12,... | collective-permute-start | bytes 3145736 | tf_op jit(solution)/shard_map/ppermute | solution.py:847
  443.3 24.4 %collective-permute-start.53 = (bf16[256,2048]{1,0:T(8,128)(2,1)}, bf16[256,2048]{1,0:T(8,128)(2,1)}, u32[]{:S(2)}, u32[]{:S(2)}) collective-permute-start(bf16[256,2048]{1,0:T(8,128)(2,1)} %after.41.refs_0_.refs_11_), channel_id=1, source_target_pairs={{0,4},{2,6},{4,0},{6,2},{1,5},{3,7},{5,1},{7,3},{8,12},{10,14},{12... | collective-permute-start | bytes 3145736 | tf_op jit(solution)/shard_map/ppermute | solution.py:847
  469.4 17.9 %collective-permute-start.60 = (bf16[256,2048]{1,0:T(8,128)(2,1)S(1)}, bf16[256,2048]{1,0:T(8,128)(2,1)}, u32[]{:S(2)}, u32[]{:S(2)}) collective-permute-start(bf16[256,2048]{1,0:T(8,128)(2,1)S(1)} %collective-permute-done.52.refs_1_.refs_12_), channel_id=1, source_target_pairs={{0,1},{1,0},{2,3},{3,2},{4,5},{5,4},{6,7},{7,6},{8,9},{9,8},{10,11... | collective-permute-start | bytes 3145736 | tf_op jit(solution)/shard_map/ppermute | solution.py:850
  469.9 17.4 %collective-permute-start.61 = (bf16[256,2048]{1,0:T(8,128)(2,1)}, bf16[256,2048]{1,0:T(8,128)(2,1)}, u32[]{:S(2)}, u32[]{:S(2)}) collective-permute-start(bf16[256,2048]{1,0:T(8,128)(2,1)} %collective-permute-done.53.refs_2_.refs_13_), channel_id=1, source_target_pairs={{0,1},{1,0},{2,3},{3,2},{4,5},{5,4},{6,7},{7,6},{8,9},{9,8},{10,11... | collective-permute-start | bytes 3145736 | tf_op jit(solution)/shard_map/ppermute | solution.py:850
  483.8 47.5 %collective-permute-start.56 = (bf16[256,2048]{1,0:T(8,128)(2,1)}, bf16[256,2048]{1,0:T(8,128)(2,1)}, u32[]{:S(2)}, u32[]{:S(2)}) collective-permute-start(bf16[256,2048]{1,0:T(8,128)(2,1)} %get-tuple-element.61), channel_id=1, source_target_pairs={{0,2},{2,0},{4,6},{6,4},{1,3},{3,1},{5,7},{7,5},{8,10},{10,8},{12,... | collective-permute-start | bytes 3145736 | tf_op jit(solution)/shard_map/ppermute | solution.py:847
  484.9 48.8 %collective-permute-start.57 = (bf16[256,2048]{1,0:T(8,128)(2,1)}, bf16[256,2048]{1,0:T(8,128)(2,1)}, u32[]{:S(2)}, u32[]{:S(2)}) collective-permute-start(bf16[256,2048]{1,0:T(8,128)(2,1)} %get-tuple-element.63), channel_id=1, source_target_pairs={{0,4},{2,6},{4,0},{6,2},{1,5},{3,7},{5,1},{7,3},{8,12},{10,14},{12... | collective-permute-start | bytes 3145736 | tf_op jit(solution)/shard_map/ppermute | solution.py:847
  486.2 47.5 %collective-permute-start.58 = (bf16[256,2048]{1,0:T(8,128)(2,1)}, bf16[256,2048]{1,0:T(8,128)(2,1)}, u32[]{:S(2)}, u32[]{:S(2)}) collective-permute-start(bf16[256,2048]{1,0:T(8,128)(2,1)} %get-tuple-element.62), channel_id=1, source_target_pairs={{0,6},{2,4},{4,2},{6,0},{1,7},{3,5},{5,3},{7,1},{8,14},{10,12},{12... | collective-permute-start | bytes 3145736 | tf_op jit(solution)/shard_map/ppermute | solution.py:847
  499.1 55.7 %collective-permute-start.64 = (bf16[128,1024]{1,0:T(8,128)(2,1)}, bf16[128,1024]{1,0:T(8,128)(2,1)S(1)}, u32[]{:S(2)}, u32[]{:S(2)}) collective-permute-start(bf16[128,1024]{1,0:T(8,128)(2,1)} %get-tuple-element.87), channel_id=1, source_target_pairs={{0,2},{2,0},{4,6},{6,4},{1,3},{3,1},{5,7},{7,5},{8,10},{10,8},{12,... | collective-permute-start | bytes 786440 | tf_op jit(solution)/shard_map/ppermute | solution.py:847
  500.2 54.6 %collective-permute-start.65 = (bf16[128,1024]{1,0:T(8,128)(2,1)}, bf16[128,1024]{1,0:T(8,128)(2,1)}, u32[]{:S(2)}, u32[]{:S(2)}) collective-permute-start(bf16[128,1024]{1,0:T(8,128)(2,1)} %get-tuple-element.86), channel_id=1, source_target_pairs={{0,4},{2,6},{4,0},{6,2},{1,5},{3,7},{5,1},{7,3},{8,12},{10,14},{12... | collective-permute-start | bytes 786440 | tf_op jit(solution)/shard_map/ppermute | solution.py:847
  531.3 23.5 %collective-permute-start.66 = (bf16[128,1024]{1,0:T(8,128)(2,1)}, bf16[128,1024]{1,0:T(8,128)(2,1)S(1)}, u32[]{:S(2)}, u32[]{:S(2)}) collective-permute-start(bf16[128,1024]{1,0:T(8,128)(2,1)} %get-tuple-element.85), channel_id=1, source_target_pairs={{0,6},{2,4},{4,2},{6,0},{1,7},{3,5},{5,3},{7,1},{8,14},{10,12},{12... | collective-permute-start | bytes 786440 | tf_op jit(solution)/shard_map/ppermute | solution.py:847
  567.3 23.1 %collective-permute-start.71 = (bf16[128,2048]{1,0:T(8,128)(2,1)}, bf16[128,2048]{1,0:T(8,128)(2,1)S(1)}, u32[]{:S(2)}, u32[]{:S(2)}) collective-permute-start(bf16[128,2048]{1,0:T(8,128)(2,1)} %get-tuple-element.83), channel_id=1, source_target_pairs={{0,2},{2,0},{4,6},{6,4},{1,3},{3,1},{5,7},{7,5},{8,10},{10,8},{12,... | collective-permute-start | bytes 1572872 | tf_op jit(solution)/shard_map/ppermute | solution.py:847
  568.5 24.7 %collective-permute-start.72 = (bf16[128,2048]{1,0:T(8,128)(2,1)}, bf16[128,2048]{1,0:T(8,128)(2,1)}, u32[]{:S(2)}, u32[]{:S(2)}) collective-permute-start(bf16[128,2048]{1,0:T(8,128)(2,1)} %get-tuple-element.82), channel_id=1, source_target_pairs={{0,4},{2,6},{4,0},{6,2},{1,5},{3,7},{5,1},{7,3},{8,12},{10,14},{12... | collective-permute-start | bytes 1572872 | tf_op jit(solution)/shard_map/ppermute | solution.py:847
  569.9 25.7 %collective-permute-start.73 = (bf16[128,2048]{1,0:T(8,128)(2,1)}, bf16[128,2048]{1,0:T(8,128)(2,1)}, u32[]{:S(2)}, u32[]{:S(2)}) collective-permute-start(bf16[128,2048]{1,0:T(8,128)(2,1)} %get-tuple-element.81), channel_id=1, source_target_pairs={{0,6},{2,4},{4,2},{6,0},{1,7},{3,5},{5,3},{7,1},{8,14},{10,12},{12... | collective-permute-start | bytes 1572872 | tf_op jit(solution)/shard_map/ppermute | solution.py:847
  580.1 24.8 %collective-permute-start.69 = (bf16[128,2048]{1,0:T(8,128)(2,1)}, bf16[128,2048]{1,0:T(8,128)(2,1)S(1)}, u32[]{:S(2)}, u32[]{:S(2)}) collective-permute-start(bf16[128,2048]{1,0:T(8,128)(2,1)} %get-tuple-element.60), channel_id=1, source_target_pairs={{0,4},{2,6},{4,0},{6,2},{1,5},{3,7},{5,1},{7,3},{8,12},{10,14},{12... | collective-permute-start | bytes 1572872 | tf_op jit(solution)/shard_map/ppermute | solution.py:847
  581.4 23.5 %collective-permute-start.70 = (bf16[128,2048]{1,0:T(8,128)(2,1)S(1)}, bf16[128,2048]{1,0:T(8,128)(2,1)S(1)}, u32[]{:S(2)}, u32[]{:S(2)}) collective-permute-start(bf16[128,2048]{1,0:T(8,128)(2,1)S(1)} %get-tuple-element.59), channel_id=1, source_target_pairs={{0,2},{2,0},{4,6},{6,4},{1,3},{3,1},{5,7},{7,5},{8,10},{10,8},{12,... | collective-permute-start | bytes 1572872 | tf_op jit(solution)/shard_map/ppermute | solution.py:847
  590.4 58.3 %collective-permute-start.68 = (bf16[256,2048]{1,0:T(8,128)(2,1)S(1)}, bf16[256,2048]{1,0:T(8,128)(2,1)}, u32[]{:S(2)}, u32[]{:S(2)}) collective-permute-start(bf16[256,2048]{1,0:T(8,128)(2,1)S(1)} %copy-done.31), channel_id=1, source_target_pairs={{0,1},{1,0},{2,3},{3,2},{4,5},{5,4},{6,7},{7,6},{8,9},{9,8},{10,11... | collective-permute-start | bytes 3145736 | tf_op jit(solution)/shard_map/ppermute | solution.py:850
  593.1 28.0 %collective-permute-start.75 = (bf16[128,2048]{1,0:T(8,128)(2,1)}, bf16[128,2048]{1,0:T(8,128)(2,1)}, u32[]{:S(2)}, u32[]{:S(2)}) collective-permute-start(bf16[128,2048]{1,0:T(8,128)(2,1)} %get-tuple-element.57), channel_id=1, source_target_pairs={{0,4},{2,6},{4,0},{6,2},{1,5},{3,7},{5,1},{7,3},{8,12},{10,14},{12... | collective-permute-start | bytes 1572872 | tf_op jit(solution)/shard_map/ppermute | solution.py:847
  595.7 27.0 %collective-permute-start.76 = (bf16[128,2048]{1,0:T(8,128)(2,1)}, bf16[128,2048]{1,0:T(8,128)(2,1)}, u32[]{:S(2)}, u32[]{:S(2)}) collective-permute-start(bf16[128,2048]{1,0:T(8,128)(2,1)} %get-tuple-element.58), channel_id=1, source_target_pairs={{0,2},{2,0},{4,6},{6,4},{1,3},{3,1},{5,7},{7,5},{8,10},{10,8},{12,... | collective-permute-start | bytes 1572872 | tf_op jit(solution)/shard_map/ppermute | solution.py:847
  609.4 18.0 %collective-permute-start.74 = (bf16[128,2048]{1,0:T(8,128)(2,1)}, bf16[128,2048]{1,0:T(8,128)(2,1)}, u32[]{:S(2)}, u32[]{:S(2)}) collective-permute-start(bf16[128,2048]{1,0:T(8,128)(2,1)} %get-tuple-element.46.refs_1_), channel_id=1, source_target_pairs={{0,2},{2,0},{4,6},{6,4},{1,3},{3,1},{5,7},{7,5},{8,10},{10,8},{12,... | collective-permute-start | bytes 1572872 | tf_op jit(solution)/shard_map/ppermute | solution.py:847
  610.4 19.1 %collective-permute-start.77 = (bf16[128,2048]{1,0:T(8,128)(2,1)}, bf16[128,2048]{1,0:T(8,128)(2,1)}, u32[]{:S(2)}, u32[]{:S(2)}) collective-permute-start(bf16[128,2048]{1,0:T(8,128)(2,1)} %get-tuple-element.47.refs_2_), channel_id=1, source_target_pairs={{0,4},{2,6},{4,0},{6,2},{1,5},{3,7},{5,1},{7,3},{8,12},{10,14},{12... | collective-permute-start | bytes 1572872 | tf_op jit(solution)/shard_map/ppermute | solution.py:847
  (112 other events, 1110.5 us)
Sparse Core Ops, SparseCore 0:
  26.6 55.1 all-gather.3
  83.9 148.3 all-gather.5
  233.9 78.9 all-gather.7
  315.1 75.2 reduce-scatter.3
  392.8 144.9 reduce-scatter.5
  563.0 52.7 reduce-scatter.7
